TPU v7x, 32 devices: a whole 2x2x4 slice. The times are simulated.
32 devices in a mesh: depth: 8 (over y, x, core), plane: 4 (over z).
Axes of the slice: x: 2, y: 2, z: 4, core: 2. Of those that a mesh axis runs over, the one named last changes fastest.
Arguments:
- spectrum: bfloat16 [2, 1024, 16, 1024], P(None, 'depth', 'plane'), may hold values from -6 to 6
- transfer_coeffs: float32 [8, 4, 4], replicated, may hold values from -3 to 3
- transfer_index: int32 [8], replicated, may hold values from 0 to 7, each once
Outputs:
- scalar_field: float32 [1024, 16, 1024], P('depth', 'plane')
- rendered: float32 [8, 4, 16, 1024], P(None, None, 'plane', 'depth')
Inputs may be any that keep to these rules, and one draw needn't show every extreme that they name: `transfer_index`: each transfer function is used by exactly one image.
All inputs are finite; a program needn't handle non-finite values.
Results may differ from a plain program's by a relative error of at most 0.0003.
Values may be sent and summed in bfloat16 or wider, within the bound.
No kernel may reach another device: no remote copies, remote signals or barrier semaphores. Data moves between devices by JAX's collectives and lax.ppermute only.
A program may use at most 64 MiB of HBM per device.

v0:
```python
import functools

import jax
import jax.numpy as jnp
import numpy as np
from jax import lax
from jax.experimental import pallas as pl
from jax.experimental.pallas import tpu as pltpu
from jax.sharding import PartitionSpec as P

density = 2.0
shade_gain = 0.4
highest = lax.Precision.HIGHEST
LANES = 128
SEGS = 8
RADIX = 4
LOG2E = 1.4426950408889634
LN2 = 0.6931471805599453


def split_table(table):
    hi = table.astype(jnp.bfloat16)
    lo = (table - hi.astype(np.float64)).astype(jnp.bfloat16)
    return jnp.asarray(hi), jnp.asarray(lo)


def x_tables(nx, blocks):
    k = np.arange(nx, dtype=np.int64)
    angle = 2.0 * np.pi * ((k[:, None] * k[None, :]) % nx) / nx
    cols = nx // blocks
    cos = (np.cos(angle) / np.sqrt(nx)).reshape(nx, blocks, cols)
    sin = (np.sin(angle) / np.sqrt(nx)).reshape(nx, blocks, cols)
    return split_table(np.concatenate([cos, sin], axis=2).transpose(1, 0, 2))


def z_tables(nz):
    quarter = nz // RADIX
    q = np.arange(quarter, dtype=np.int64)
    steps = quarter // SEGS
    row = np.arange(quarter)
    m = (row % SEGS) * steps + row // SEGS
    angle = 2.0 * np.pi * ((m[:, None] * q[None, :]) % quarter) / quarter
    table = np.concatenate([np.cos(angle), -np.sin(angle)], axis=1) / np.sqrt(nz)
    turn = 2.0 * np.pi * np.arange(1, RADIX)[:, None] * q[None, :] / nz
    twiddle = np.stack([np.cos(turn), np.sin(turn)], axis=1)
    wide = np.broadcast_to(twiddle[..., None], twiddle.shape + (LANES,))
    return split_table(table) + (jnp.asarray(wide, jnp.float32),)


def x_kernel(spec_ref, hi_ref, lo_ref, out_ref):
    planes, _, rows, cols = out_ref.shape[1:]
    hi = hi_ref[0]
    lo = lo_ref[0]

    def product(part, plane):
        modes = spec_ref[part, plane]
        return jnp.dot(modes, hi, preferred_element_type=jnp.float32) + jnp.dot(
            modes, lo, preferred_element_type=jnp.float32
        )

    for plane in range(planes):
        a = product(0, plane)
        b = product(1, plane)
        out_ref[0, plane, 0] = a[:, :cols] - b[:, cols:]
        out_ref[0, plane, 1] = a[:, cols:] + b[:, :cols]


def x_transform(spec, hi, lo):
    parts, planes, rows, nx = spec.shape
    blocks, _, wide = hi.shape
    cols = wide // 2
    return pl.pallas_call(
        x_kernel,
        grid=(blocks,),
        in_specs=[
            pl.BlockSpec((parts, planes, rows, nx), lambda d: (0, 0, 0, 0)),
            pl.BlockSpec((1, nx, wide), lambda d: (d, 0, 0)),
            pl.BlockSpec((1, nx, wide), lambda d: (d, 0, 0)),
        ],
        out_specs=pl.BlockSpec((1, planes, 2, rows, cols), lambda d: (d, 0, 0, 0, 0)),
        out_shape=jax.ShapeDtypeStruct((blocks, planes, 2, rows, cols), jnp.float32),
        cost_estimate=pl.CostEstimate(
            flops=2 * parts * planes * rows * nx * nx * 4,
            bytes_accessed=12 * 2**20,
            transcendentals=0,
        ),
        name="x_transform",
    )(spec, hi, lo)


def z_kernel(in_ref, hi_ref, lo_ref, twiddle_ref, out_ref, yhi_ref, ylo_ref):
    blocks, _, _, rows, cols = in_ref.shape
    quarter = hi_ref.shape[0]
    per = quarter // rows

    def split(value, row, rank):
        high = value.astype(jnp.bfloat16)
        yhi_ref[pl.ds(row, rows), rank * cols : (rank + 1) * cols] = high
        ylo_ref[pl.ds(row, rows), rank * cols : (rank + 1) * cols] = (
            value - high.astype(jnp.float32)
        ).astype(jnp.bfloat16)

    for block in range(per):
        re = [in_ref[t * per + block, 0, 0] for t in range(RADIX)]
        im = [in_ref[t * per + block, 0, 1] for t in range(RADIX)]
        row = block * rows
        even_re, even_im = re[0] + re[2], im[0] + im[2]
        diff_re, diff_im = re[0] - re[2], im[0] - im[2]
        odd_re, odd_im = re[1] + re[3], im[1] + im[3]
        side_re, side_im = re[1] - re[3], im[1] - im[3]
        sums = (
            (even_re + odd_re, even_im + odd_im),
            (diff_re - side_im, diff_im + side_re),
            (even_re - odd_re, even_im - odd_im),
            (diff_re + side_im, diff_im - side_re),
        )
        for rank in range(RADIX):
            a, b = sums[rank]
            if rank > 0:
                c = twiddle_ref[rank - 1, 0, pl.ds(row, rows)]
                s = twiddle_ref[rank - 1, 1, pl.ds(row, rows)]
                a, b = a * c - b * s, a * s + b * c
            split(a, row, rank)
            split(b, quarter + row, rank)
    hi = hi_ref[...]
    lo = lo_ref[...]
    yhi = yhi_ref[...]
    ylo = ylo_ref[...]
    total = (
        jnp.dot(hi, yhi, preferred_element_type=jnp.float32)
        + jnp.dot(hi, ylo, preferred_element_type=jnp.float32)
        + jnp.dot(lo, yhi, preferred_element_type=jnp.float32)
    )
    for rank in range(RADIX):
        out_ref[0, rank] = total[:, rank * cols : (rank + 1) * cols]


def z_transform(arrived, hi, lo, twiddle):
    blocks, planes, _, rows, cols = arrived.shape
    quarter = hi.shape[0]
    return pl.pallas_call(
        z_kernel,
        grid=(planes,),
        in_specs=[
            pl.BlockSpec((blocks, 1, 2, rows, cols), lambda p: (0, p, 0, 0, 0)),
            pl.BlockSpec(hi.shape, lambda p: (0, 0)),
            pl.BlockSpec(lo.shape, lambda p: (0, 0)),
            pl.BlockSpec(twiddle.shape, lambda p: (0, 0, 0, 0)),
        ],
        out_specs=pl.BlockSpec((1, RADIX, quarter, cols), lambda p: (p, 0, 0, 0)),
        out_shape=jax.ShapeDtypeStruct((planes, RADIX, quarter, cols), jnp.float32),
        scratch_shapes=[
            pltpu.VMEM((2 * quarter, RADIX * cols), jnp.bfloat16),
            pltpu.VMEM((2 * quarter, RADIX * cols), jnp.bfloat16),
        ],
        cost_estimate=pl.CostEstimate(
            flops=2 * planes * quarter * 2 * quarter * RADIX * cols * 3,
            bytes_accessed=6 * 2**20,
            transcendentals=0,
        ),
        name="z_transform",
    )(arrived, hi, lo, twiddle)


def soft2(coeffs, value):
    power = ((coeffs[3] * value + coeffs[2]) * value + coeffs[1]) * value + coeffs[0]
    grown = jnp.exp2(jnp.minimum(power, 126.0))
    large = jnp.log2(1.0 + grown)
    soft = jnp.where(grown < 2.0**-12, grown * LOG2E, large)
    return jnp.maximum(soft, power)


def render_kernel(cells, coeffs_ref, index_ref, *refs):
    planes = len(refs) - 4
    field_refs = refs[:planes]
    before_ref, after_ref, out_ref, light_ref = refs[planes:]
    steps = field_refs[0].shape[1] // SEGS
    images = index_ref.shape[0]
    chain = [before_ref, *field_refs, after_ref]
    shape = (SEGS, LANES)
    for plane in range(planes):
        below, here, above = chain[plane], chain[plane + 1], chain[plane + 2]

        def light(i, carry):
            rows = pl.ds(pl.multiple_of(i * SEGS, SEGS), SEGS)
            for rank in range(RADIX):
                slope = 0.5 * (above[rank, rows] - below[rank, rows])
                light_ref[rank, rows] = 1.0 + shade_gain * jnp.tanh(slope)
            return carry

        lax.fori_loop(0, steps, light, 0, unroll=2)

        def image(m, carry):
            which = index_ref[m]
            table = [
                [jnp.full(shape, coeffs_ref[which, j, n] * LOG2E, jnp.float32) for n in range(4)]
                for j in range(4)
            ]

            def step(i, state):
                clear, sums = state
                rows = pl.ds(pl.multiple_of(i * SEGS, SEGS), SEGS)
                for rank in range(RADIX):
                    value = here[rank, rows]
                    depth = soft2(table[3], value) * (density / cells * LN2)
                    passed = jnp.exp2(depth * -LOG2E)
                    taken = jnp.where(depth < 2.0**-9, depth * (1.0 - 0.5 * depth), 1.0 - passed)
                    weight = clear * taken * light_ref[rank, rows]
                    clear = clear * passed
                    sums = [acc + weight * soft2(table[j], value) for j, acc in enumerate(sums)]
                return clear, sums

            zero = jnp.zeros(shape, jnp.float32)
            clear, sums = lax.fori_loop(
                0, steps, step, (jnp.ones(shape, jnp.float32), [zero, zero, zero]), unroll=2
            )
            reach = clear[0:1]
            totals = [acc[0:1] for acc in sums]
            for seg in range(1, SEGS):
                totals = [t + reach * acc[seg : seg + 1] for t, acc in zip(totals, sums)]
                reach = reach * clear[seg : seg + 1]
            for j in range(3):
                out_ref[m, j, plane : plane + 1] = totals[j] * LN2
            out_ref[m, 3, plane : plane + 1] = reach
            return carry

        lax.fori_loop(0, images, image, 0)


def render(cells, fields, before, after, coeffs, index):
    planes = len(fields)
    images = index.shape[0]
    vmem = pl.BlockSpec(memory_space=pltpu.VMEM)
    smem = pl.BlockSpec(memory_space=pltpu.SMEM)
    return pl.pallas_call(
        functools.partial(render_kernel, cells),
        in_specs=[smem, smem] + [vmem] * (planes + 2),
        out_specs=vmem,
        out_shape=jax.ShapeDtypeStruct((images, 4, planes, LANES), jnp.float32),
        scratch_shapes=[pltpu.VMEM(fields[0].shape, jnp.float32)],
        cost_estimate=pl.CostEstimate(
            flops=64 * images * planes * cells * LANES,
            bytes_accessed=4 * (planes + 2) * cells * LANES,
            transcendentals=9 * images * planes * cells * LANES,
        ),
        name="render",
    )(coeffs, index, *fields, before, after)


def shifts(axis):
    devices = lax.axis_size(axis)
    up = [(i, (i + 1) % devices) for i in range(devices)]
    return up, [(j, i) for i, j in up]


def fast_body(spectrum, transfer_coeffs, transfer_index):
    _, rows, planes, nx = spectrum.shape
    blocks = lax.axis_size("depth")
    nz = rows * blocks
    xhi, xlo = x_tables(nx, blocks)
    zhi, zlo, twiddle = z_tables(nz)
    groups = [[0, planes - 1], list(range(1, planes - 1))]
    fields = [None] * planes
    sent = []
    for group in groups:
        picked = jnp.stack([spectrum[:, :, p] for p in group], axis=1)
        mixed = x_transform(picked, xhi, xlo)
        sent.append(lax.all_to_all(mixed, "depth", split_axis=0, concat_axis=0, tiled=True))
    halos = None
    up, down = shifts("plane")
    for group, arrived in zip(groups, sent):
        done = z_transform(arrived, zhi, zlo, twiddle)
        for at, p in enumerate(group):
            fields[p] = done[at]
        if halos is None:
            halos = (lax.ppermute(fields[-1], "plane", up), lax.ppermute(fields[0], "plane", down))
    steps = nz // RADIX // SEGS
    stacked = jnp.stack(fields).reshape(planes, RADIX, steps, SEGS, LANES)
    slabs = stacked.transpose(3, 2, 1, 0, 4).reshape(nz, planes, LANES)
    scalar_field = lax.all_to_all(slabs, "depth", split_axis=0, concat_axis=2, tiled=True)
    rendered = render(nz, fields, *halos, transfer_coeffs, transfer_index)
    return scalar_field, rendered


def with_halo(array, sides, width):
    for axis, dim in sides:
        devices, length = (lax.axis_size(axis), array.shape[dim])
        up = [(i, (i + 1) % devices) for i in range(devices)]
        down = [(j, i) for i, j in up]
        last = lax.slice_in_dim(array, length - width, length, axis=dim)
        first = lax.slice_in_dim(array, 0, width, axis=dim)
        before = lax.ppermute(last, axis, up)
        after = lax.ppermute(first, axis, down)
        array = jnp.concatenate([before, array, after], axis=dim)
    return array


def dft_tables(length):
    indices = jnp.arange(length, dtype=jnp.int32)
    phase_index = indices[:, None] * indices[None, :] % length
    angles = phase_index.astype(jnp.float32) * (2.0 * jnp.pi / length)
    scaling = 1.0 / jnp.sqrt(jnp.float32(length))
    return (jnp.cos(angles) * scaling, jnp.sin(angles) * scaling)


def polynomial(coeffs, values):
    result = coeffs[-1] + jnp.zeros_like(values)
    for degree in range(coeffs.shape[0] - 2, -1, -1):
        result = result * values + coeffs[degree]
    return result


def plane_slope(field_cells):
    padded = with_halo(field_cells, (("plane", 1),), 1)
    return 0.5 * (padded[:, 2:] - padded[:, :-2])


def render_blocks(field_cells, slope_cells, selected, blocks):
    depth_cells, plane_count, column_count = field_cells.shape
    block_cells = depth_cells // blocks
    values = field_cells.reshape(blocks, block_cells, plane_count, column_count)
    lighting = 1.0 + shade_gain * jnp.tanh(
        slope_cells.reshape(blocks, block_cells, plane_count, column_count)
    )
    per_image = []
    for which_image in range(selected.shape[0]):
        coeffs = selected[which_image]
        optical = jax.nn.softplus(polynomial(coeffs[3], values)) * (density / depth_cells)
        before = jnp.cumsum(optical, axis=1) - optical
        weight = jnp.exp(-before) * -jnp.expm1(-optical) * lighting
        block_depth = jnp.sum(optical, axis=1)
        ahead = jnp.cumsum(block_depth, axis=0) - block_depth
        reach = jnp.exp(-ahead)
        channels = []
        for channel in range(3):
            glow_cells = jax.nn.softplus(polynomial(coeffs[channel], values))
            channels.append(jnp.sum(reach * jnp.sum(weight * glow_cells, axis=1), axis=0))
        channels.append(jnp.sum(block_depth, axis=0))
        per_image.append(jnp.stack(channels))
    return jnp.stack(per_image)


def body(spectrum, transfer_coeffs, transfer_index):
    _, rows, _, nx = spectrum.shape
    cos_z, sin_z = dft_tables(rows * lax.axis_size("depth"))
    cos_x, sin_x = dft_tables(nx)
    one_hot = (
        transfer_index[:, None] == jnp.arange(transfer_coeffs.shape[0], dtype=jnp.int32)[None, :]
    ).astype(jnp.float32)
    selected = jnp.sum(one_hot[:, :, None, None] * transfer_coeffs[None], axis=1)
    depth_count = lax.axis_size("depth")
    real_part = spectrum[0].astype(jnp.float32)
    imag_part = spectrum[1].astype(jnp.float32)
    h_re = jnp.einsum("zpk,kx->zpx", real_part, cos_x, precision=highest) - jnp.einsum(
        "zpk,kx->zpx", imag_part, sin_x, precision=highest
    )
    h_im = jnp.einsum("zpk,kx->zpx", real_part, sin_x, precision=highest) + jnp.einsum(
        "zpk,kx->zpx", imag_part, cos_x, precision=highest
    )
    mixed = jnp.stack([h_re, h_im])
    arrived = lax.all_to_all(mixed, "depth", split_axis=3, concat_axis=1, tiled=True)
    field_columns = jnp.einsum("zk,kpx->zpx", cos_z, arrived[0], precision=highest) - jnp.einsum(
        "zk,kpx->zpx", sin_z, arrived[1], precision=highest
    )
    slope_cells = plane_slope(field_columns)
    merged = render_blocks(field_columns, slope_cells, selected, depth_count)
    scalar_field = lax.all_to_all(field_columns, "depth", split_axis=0, concat_axis=2, tiled=True)
    rendered = jnp.concatenate([merged[:, :3], jnp.exp(-merged[:, 3:4])], axis=1)
    return (scalar_field, rendered)


def solution(mesh):
    def pick(spectrum, *rest):
        _, rows, planes, nx = spectrum.shape
        blocks = lax.axis_size("depth")
        if nx == LANES * blocks and blocks % RADIX == 0 and planes > 3 and rows % 16 == 0:
            return fast_body(spectrum, *rest)
        return body(spectrum, *rest)

    return jax.shard_map(
        pick,
        mesh=mesh,
        in_specs=(P(None, "depth", "plane", None), P(), P()),
        out_specs=(P("depth", "plane", None), P(None, None, "plane", "depth")),
        check_vma=False,
    )
```

profile of v0, /device:TPU:0, one launch (start us, length us, event | category | flops | bytes accessed | tf_op | source)
XLA Modules:
  0.0 182.6 jit_solution(12585998822866647100)
XLA Ops:
  0.6 8.8 %fusion = (bf16[2,128,1,1024]{3,2,1,0:T(2,128)(2,1)S(1)}, bf16[2,128,1,1024]{3,2,1,0:T(2,128)(2,1)S(1)}, bf16[2,128,1,1024]{3,2,1,0:T(2,128)(2,1)S(1)}, bf16[2,128,1,1024]{3,2,1,0:T(2,128)(2,1)}) fusion(bf16[2,128,4,1024]{3,2,1,0:T(4,128)(2,1)} %param.8), kind=kLoop, calls=%fused_computation.11 | loop fusion | bytes 4194304 | tf_op jit(solution)/shard_map/slice | solution.py:266
  9.4 0.4 copy_bitcast_fusion.2
  9.8 1.1 pad_maximum_fusion.spec_ref
  10.9 10.0 %x_transform.2 = f32[8,2,2,128,128]{4,3,2,1,0:T(8,128)} custom-call(bf16[2,2,128,1024]{3,2,1,0:T(8,128)(2,1)} %pad_maximum_fusion.spec_ref, bf16[8,1024,256]{2,1,0:T(8,128)(2,1)} %constant.10.clone.hi_ref, bf16[8,1024,256]{2,1,0:T(8,128)(2,1)} %constant.11.clone.lo_ref), custom_call_target="tpu_custom_call" | custom-call | flops 4294967296 | bytes 12582912 | tf_op jit(solution)/shard_map/x_transform/pallas_call | solution.py:72
  20.9 5.2 %all-to-all-start = ((f32[8,2,2,128,128]{4,3,2,1,0:T(8,128)}), f32[8,2,2,128,128]{4,3,2,1,0:T(8,128)S(1)}, u32[]{:S(2)}, u32[]{:S(2)}) async-start(f32[8,2,2,128,128]{4,3,2,1,0:T(8,128)} %x_transform.2), calls=%async_computation | async-start | bytes 4194304 | tf_op jit(solution)/shard_map/all_to_all | solution.py:268
  26.1 1.6 copy_bitcast_fusion
  27.7 1.1 pad_maximum_fusion.1.spec_ref
  28.8 10.0 %x_transform.3 = f32[8,2,2,128,128]{4,3,2,1,0:T(8,128)} custom-call(bf16[2,2,128,1024]{3,2,1,0:T(8,128)(2,1)} %pad_maximum_fusion.1.spec_ref, bf16[8,1024,256]{2,1,0:T(8,128)(2,1)} %constant.10.clone.hi_ref, bf16[8,1024,256]{2,1,0:T(8,128)(2,1)} %constant.11.clone.lo_ref), custom_call_target="tpu_custom_call" | custom-call | flops 4294967296 | bytes 12582912 | tf_op jit(solution)/shard_map/x_transform/pallas_call | solution.py:72
  38.8 13.9 %all-to-all-done.in_ref = f32[8,2,2,128,128]{4,3,2,1,0:T(8,128)S(1)} async-done(((f32[8,2,2,128,128]{4,3,2,1,0:T(8,128)}), f32[8,2,2,128,128]{4,3,2,1,0:T(8,128)S(1)}, u32[]{:S(2)}, u32[]{:S(2)}) %all-to-all-start) | async-done | bytes 2097184 | tf_op jit(solution)/shard_map/all_to_all | solution.py:268
  52.7 1.3 copy-done.1
  54.0 4.3 %all-to-all-start.1 = ((f32[8,2,2,128,128]{4,3,2,1,0:T(8,128)}), f32[8,2,2,128,128]{4,3,2,1,0:T(8,128)}, u32[]{:S(2)}, u32[]{:S(2)}) async-start(f32[8,2,2,128,128]{4,3,2,1,0:T(8,128)} %x_transform.3), calls=%async_computation.1 | async-start | bytes 4194304 | tf_op jit(solution)/shard_map/all_to_all | solution.py:268
  58.4 4.2 %z_transform.2 = f32[2,4,256,128]{3,2,1,0:T(8,128)} custom-call(f32[8,2,2,128,128]{4,3,2,1,0:T(8,128)} %copy-done.1, bf16[256,512]{1,0:T(8,128)(2,1)} %constant.12.clone.hi_ref, bf16[256,512]{1,0:T(8,128)(2,1)} %constant.13.clone.lo_ref, f32[3,2,256,128]{3,2,1,0:T(8,128)} %constant.14.clone.twiddle_ref), custom_call_target="tpu_custom_call" | custom-call | flops 805306368 | bytes 6291456 | tf_op jit(solution)/shard_map/z_transform/pallas_call | solution.py:141
  62.6 2.4 %slice_bitcast_fusion.2 = (f32[4,256,128]{2,1,0:T(8,128)}, f32[4,256,128]{2,1,0:T(8,128)}, f32[1,4,256,128]{3,2,1,0:T(8,128)S(1)}, f32[1,4,256,128]{3,2,1,0:T(8,128)S(1)}) fusion(f32[2,4,256,128]{3,2,1,0:T(8,128)} %z_transform.2), kind=kLoop, calls=%fused_computation.9 | loop fusion | bytes 3145728 | tf_op jit(solution)/shard_map/squeeze | solution.py:274
  65.0 20.0 %all-to-all-done.1.in_ref = f32[8,2,2,128,128]{4,3,2,1,0:T(8,128)} async-done(((f32[8,2,2,128,128]{4,3,2,1,0:T(8,128)}), f32[8,2,2,128,128]{4,3,2,1,0:T(8,128)}, u32[]{:S(2)}, u32[]{:S(2)}) %all-to-all-start.1) | async-done | bytes 2097184 | tf_op jit(solution)/shard_map/all_to_all | solution.py:268
  85.0 4.2 %z_transform.3 = f32[2,4,256,128]{3,2,1,0:T(8,128)} custom-call(f32[8,2,2,128,128]{4,3,2,1,0:T(8,128)} %all-to-all-done.1.in_ref, bf16[256,512]{1,0:T(8,128)(2,1)} %constant.12.clone.hi_ref, bf16[256,512]{1,0:T(8,128)(2,1)} %constant.13.clone.lo_ref, f32[3,2,256,128]{3,2,1,0:T(8,128)} %constant.14.clone.twiddle_ref), custom_call_target="tpu_custom_call" | custom-call | flops 805306368 | bytes 6291456 | tf_op jit(solution)/shard_map/z_transform/pallas_call | solution.py:141
  89.2 1.4 maximum_bitcast_fusion
  90.6 1.4 copy.33
  91.9 2.7 %copy.34 = f32[1024,4,128]{2,1,0:T(4,128)} copy(f32[1024,4,128]{2,0,1:T(8,128)S(1)} %bitcast.25) | data formatting | bytes 4194304 | tf_op jit(solution)/shard_map/reshape | solution.py:279
  94.6 3.7 %all-to-all-start.2 = ((f32[1024,4,128]{2,1,0:T(4,128)}), f32[1024,4,128]{2,1,0:T(4,128)S(1)}, u32[]{:S(2)}, u32[]{:S(2)}) async-start(f32[1024,4,128]{2,1,0:T(4,128)} %copy.34), calls=%async_computation.2 | async-start | bytes 4194304 | tf_op jit(solution)/shard_map/all_to_all | solution.py:280
  98.4 1.6 collective-permute-start
  100.0 2.3 %collective-permute-start.1 = (f32[4,256,128]{2,1,0:T(8,128)}, f32[4,256,128]{2,1,0:T(8,128)}, u32[]{:S(2)}, u32[]{:S(2)}) collective-permute-start(f32[4,256,128]{2,1,0:T(8,128)} %get-tuple-element.11.refs_0_), channel_id=1, source_target_pairs={{1,0},{2,1},{3,2},{0,3},{5,4},{6,5},{7,6},{4,7},{9,8},{10,9},{11,1... | collective-permute-start | bytes 1572872 | tf_op jit(solution)/shard_map/ppermute | solution.py:276
  102.2 0.0 copy-done.2
  102.2 0.7 copy.37.coeffs_ref
  102.9 0.0 copy-done
  102.9 1.1 slice_bitcast_fusion
  104.0 11.4 %collective-permute-done.refs_4_ = f32[4,256,128]{2,1,0:T(8,128)} collective-permute-done((f32[4,256,128]{2,1,0:T(8,128)}, f32[4,256,128]{2,1,0:T(8,128)}, u32[]{:S(2)}, u32[]{:S(2)}) %collective-permute-start) | collective-permute-done | bytes 524320 | tf_op jit(solution)/shard_map/ppermute | solution.py:276
  115.4 10.1 %collective-permute-done.1.refs_5_ = f32[4,256,128]{2,1,0:T(8,128)} collective-permute-done((f32[4,256,128]{2,1,0:T(8,128)}, f32[4,256,128]{2,1,0:T(8,128)}, u32[]{:S(2)}, u32[]{:S(2)}) %collective-permute-start.1) | collective-permute-done | bytes 524320 | tf_op jit(solution)/shard_map/ppermute | solution.py:276
  125.4 51.8 %render.1 = f32[8,4,4,128]{3,2,1,0:T(4,128)} custom-call(f32[8,4,4]{2,1,0:T(4,128)} %copy.37.coeffs_ref, s32[8]{0:T(128)} %index_ref.1, f32[4,256,128]{2,1,0:T(8,128)} %get-tuple-element.11.refs_0_, f32[4,256,128]{2,1,0:T(8,128)} %get-tuple-element.15.refs_1_, f32[4,256,128]{2,1,0:T(8,128)} %get-tuple-element.14.refs_2_, ...), custom_call_target="tpu_custom_call" | custom-call | flops 268435456 | bytes 3145728 | tf_op jit(solution)/shard_map/render/pallas_call | solution.py:235
  177.2 0.0 all-to-all-done.2
  177.2 1.5 copy.35
  178.7 1.9 %copy.36 = f32[128,4,8,128]{0,3,2,1:T(8,128)S(1)} copy(f32[128,4,8,128]{3,0,2,1:T(8,128)} %bitcast.26) | data formatting | bytes 4194304 | tf_op jit(solution)/shard_map/all_to_all | solution.py:280
  180.6 2.0 %copy.38 = f32[128,4,1024]{2,1,0:T(4,128)} copy(f32[128,4,1024]{0,2,1:T(8,128)S(1)} %bitcast.27) | data formatting | bytes 4194304
  (3 shorter events, 0.0 us)
Async XLA Ops:
  20.9 31.8 %all-to-all-start = ((f32[8,2,2,128,128]{4,3,2,1,0:T(8,128)}), f32[8,2,2,128,128]{4,3,2,1,0:T(8,128)S(1)}, u32[]{:S(2)}, u32[]{:S(2)}) async-start(f32[8,2,2,128,128]{4,3,2,1,0:T(8,128)} %x_transform.2), calls=%async_computation | async-start | bytes 4194304 | tf_op jit(solution)/shard_map/all_to_all | solution.py:268
  52.7 1.3 copy-start.1
  54.0 31.0 %all-to-all-start.1 = ((f32[8,2,2,128,128]{4,3,2,1,0:T(8,128)}), f32[8,2,2,128,128]{4,3,2,1,0:T(8,128)}, u32[]{:S(2)}, u32[]{:S(2)}) async-start(f32[8,2,2,128,128]{4,3,2,1,0:T(8,128)} %x_transform.3), calls=%async_computation.1 | async-start | bytes 4194304 | tf_op jit(solution)/shard_map/all_to_all | solution.py:268
  94.6 7.6 %copy-start.2 = (f32[8,4,4]{0,2,1:T(4,128)S(1)}, f32[8,4,4]{0,2,1:T(4,128)}, u32[]{:S(2)}) copy-start(f32[8,4,4]{0,2,1:T(4,128)} %param.9) | copy-start | bytes 1540
  94.6 8.3 %copy-start = (f32[2,4,256,128]{3,2,1,0:T(8,128)S(1)}, f32[2,4,256,128]{3,2,1,0:T(8,128)}, u32[]{:S(2)}) copy-start(f32[2,4,256,128]{3,2,1,0:T(8,128)} %z_transform.3) | copy-start | bytes 3145732
  94.6 82.6 %all-to-all-start.2 = ((f32[1024,4,128]{2,1,0:T(4,128)}), f32[1024,4,128]{2,1,0:T(4,128)S(1)}, u32[]{:S(2)}, u32[]{:S(2)}) async-start(f32[1024,4,128]{2,1,0:T(4,128)} %copy.34), calls=%async_computation.2 | async-start | bytes 4194304 | tf_op jit(solution)/shard_map/all_to_all | solution.py:280
  98.4 17.0 %collective-permute-start = (f32[4,256,128]{2,1,0:T(8,128)}, f32[4,256,128]{2,1,0:T(8,128)}, u32[]{:S(2)}, u32[]{:S(2)}) collective-permute-start(f32[4,256,128]{2,1,0:T(8,128)} %get-tuple-element.10.refs_3_), channel_id=1, source_target_pairs={{0,1},{1,2},{2,3},{3,0},{4,5},{5,6},{6,7},{7,4},{8,9},{9,10},{10,1... | collective-permute-start | bytes 1572872 | tf_op jit(solution)/shard_map/ppermute | solution.py:276
  100.0 25.5 %collective-permute-start.1 = (f32[4,256,128]{2,1,0:T(8,128)}, f32[4,256,128]{2,1,0:T(8,128)}, u32[]{:S(2)}, u32[]{:S(2)}) collective-permute-start(f32[4,256,128]{2,1,0:T(8,128)} %get-tuple-element.11.refs_0_), channel_id=1, source_target_pairs={{1,0},{2,1},{3,2},{0,3},{5,4},{6,5},{7,6},{4,7},{9,8},{10,9},{11,1... | collective-permute-start | bytes 1572872 | tf_op jit(solution)/shard_map/ppermute | solution.py:276
where the time goes:
time: 183 us
  Pallas kernels  80.2 us (44%)
  waiting for transfers between devices  55.3 us (30%)
  local copies, waits for them, and re-layouts  25.6 us (14%)
  starting transfers between devices  17.2 us (9%)
  other arithmetic  3.53 us (2%)
    pallas_call x1, Pallas kernels, render(): pl.pallas_call(functools.partial(render_kernel, cells), in_specs=[smem, s...  51.8 us
    all_to_all x2, waiting for transfers between devices, fast_body(): lax.all_to_all(mixed, 'depth', split_axis=0, concat_axis=0, tiled=True)  33.9 us
    pallas_call x2, Pallas kernels, x_transform(): pl.pallas_call(x_kernel, grid=(blocks,), in_specs=[pl.BlockSpec((parts, p...  20.1 us
    ppermute x1, waiting for transfers between devices, fast_body(): lax.ppermute(fields[-1], 'plane', up)  11.4 us
    ppermute x1, waiting for transfers between devices, fast_body(): lax.ppermute(fields[0], 'plane', down)  10.1 us
    all_to_all x2, starting transfers between devices, fast_body(): lax.all_to_all(mixed, 'depth', split_axis=0, concat_axis=0, tiled=True)  9.55 us
    slice x1, local copies, waits for them, and re-layouts, fast_body(): picked = jnp.stack([spectrum[:, :, p] for p in group], axis=1)  8.76 us
    pallas_call x2, Pallas kernels, z_transform(): pl.pallas_call(z_kernel, grid=(planes,), in_specs=[pl.BlockSpec((blocks,...  8.4 us
  transfers between devices with their start and end apart: 5, of which 4 were waited for; matrix products, arithmetic and copies ran while one was open for 4% of the time, Pallas kernels for 36%

commit v1 on v0

--- a/solution.py
+++ b/solution.py
@@ -14,6 +14,10 @@
 LANES = 128
 SEGS = 8
 RADIX = 4
+PACK = 16
+LEVELS = 16.0
+STEPS = 32766.0
+TINY = 2.0**-108
 LOG2E = 1.4426950408889634
 LN2 = 0.6931471805599453
 
@@ -47,49 +51,70 @@
     return split_table(table) + (jnp.asarray(wide, jnp.float32),)
 
 
-def x_kernel(spec_ref, hi_ref, lo_ref, out_ref):
-    planes, _, rows, cols = out_ref.shape[1:]
+def x_kernel(planes, spec_ref, hi_ref, lo_ref, out_ref, mixed_ref):
+    half = spec_ref.shape[0] // 2
+    rows = half // planes
+    cols = hi_ref.shape[2] // 2
     hi = hi_ref[0]
     lo = lo_ref[0]
 
-    def product(part, plane):
-        modes = spec_ref[part, plane]
+    def product(part):
+        modes = spec_ref[part * half : (part + 1) * half]
         return jnp.dot(modes, hi, preferred_element_type=jnp.float32) + jnp.dot(
             modes, lo, preferred_element_type=jnp.float32
         )
 
+    a = product(0)
+    b = product(1)
+    mixed_ref[0] = a[:, :cols] - b[:, cols:]
+    mixed_ref[1] = a[:, cols:] + b[:, :cols]
+    levels = jnp.zeros((PACK, cols), jnp.float32)
+    place = lax.broadcasted_iota(jnp.int32, (PACK, cols), 0)
     for plane in range(planes):
-        a = product(0, plane)
-        b = product(1, plane)
-        out_ref[0, plane, 0] = a[:, :cols] - b[:, cols:]
-        out_ref[0, plane, 1] = a[:, cols:] + b[:, :cols]
-
-
-def x_transform(spec, hi, lo):
-    parts, planes, rows, nx = spec.shape
+        parts = [mixed_ref[part, pl.ds(plane, rows, stride=planes)] for part in range(2)]
+        peak = jnp.maximum(jnp.abs(parts[0]), jnp.abs(parts[1]))
+        peak = jnp.max(peak, axis=0, keepdims=True)
+        level = jnp.ceil(LEVELS * jnp.log2(jnp.maximum(peak, TINY))) + 1.0
+        scale = STEPS * jnp.exp2(level * (-1.0 / LEVELS))
+        for part in range(2):
+            at = (plane * 2 + part) * rows
+            whole = jnp.round(parts[part] * scale).astype(jnp.int32)
+            out_ref[0, at : at + rows] = whole.astype(jnp.int16)
+        levels = jnp.where(place == plane, jnp.broadcast_to(level, levels.shape), levels)
+    at = planes * 2 * rows
+    out_ref[0, at : at + PACK] = levels.astype(jnp.int32).astype(jnp.int16)
+
+
+def x_transform(spec, planes, hi, lo):
+    modes, nx = spec.shape
     blocks, _, wide = hi.shape
     cols = wide // 2
     return pl.pallas_call(
-        x_kernel,
+        functools.partial(x_kernel, planes),
         grid=(blocks,),
         in_specs=[
-            pl.BlockSpec((parts, planes, rows, nx), lambda d: (0, 0, 0, 0)),
+            pl.BlockSpec((modes, nx), lambda d: (0, 0)),
             pl.BlockSpec((1, nx, wide), lambda d: (d, 0, 0)),
             pl.BlockSpec((1, nx, wide), lambda d: (d, 0, 0)),
         ],
-        out_specs=pl.BlockSpec((1, planes, 2, rows, cols), lambda d: (d, 0, 0, 0, 0)),
-        out_shape=jax.ShapeDtypeStruct((blocks, planes, 2, rows, cols), jnp.float32),
+        out_specs=pl.BlockSpec((1, modes + PACK, cols), lambda d: (d, 0, 0)),
+        out_shape=jax.ShapeDtypeStruct((blocks, modes + PACK, cols), jnp.int16),
+        scratch_shapes=[pltpu.VMEM((2, modes // 2, cols), jnp.float32)],
         cost_estimate=pl.CostEstimate(
-            flops=2 * parts * planes * rows * nx * nx * 4,
-            bytes_accessed=12 * 2**20,
-            transcendentals=0,
+            flops=2 * modes * nx * nx * 4, bytes_accessed=12 * 2**20, transcendentals=0
         ),
         name="x_transform",
     )(spec, hi, lo)
 
 
-def z_kernel(in_ref, hi_ref, lo_ref, twiddle_ref, out_ref, yhi_ref, ylo_ref):
-    blocks, _, _, rows, cols = in_ref.shape
+def z_kernel(
+    in_ref, level_ref, hi_ref, lo_ref, twiddle_ref, out_ref, low_ref, high_ref, slab_ref,
+    yhi_ref, ylo_ref,
+):
+    plane = pl.program_id(0)
+    planes = pl.num_programs(0)
+    blocks, double, cols = in_ref.shape
+    rows = double // 2
     quarter = hi_ref.shape[0]
     per = quarter // rows
 
@@ -100,9 +125,18 @@
             value - high.astype(jnp.float32)
         ).astype(jnp.bfloat16)
 
+    place = lax.broadcasted_iota(jnp.int32, (PACK, cols), 0)
+
+    def load(source, part):
+        level = level_ref[source].astype(jnp.int32).astype(jnp.float32)
+        level = jnp.sum(jnp.where(place == plane, level, 0.0), axis=0, keepdims=True)
+        scale = jnp.exp2(level * (1.0 / LEVELS)) * (1.0 / STEPS)
+        whole = in_ref[source, part * rows : (part + 1) * rows]
+        return whole.astype(jnp.int32).astype(jnp.float32) * scale
+
     for block in range(per):
-        re = [in_ref[t * per + block, 0, 0] for t in range(RADIX)]
-        im = [in_ref[t * per + block, 0, 1] for t in range(RADIX)]
+        re = [load(t * per + block, 0) for t in range(RADIX)]
+        im = [load(t * per + block, 1) for t in range(RADIX)]
         row = block * rows
         even_re, even_im = re[0] + re[2], im[0] + im[2]
         diff_re, diff_im = re[0] - re[2], im[0] - im[2]
@@ -134,21 +168,50 @@
     for rank in range(RADIX):
         out_ref[0, rank] = total[:, rank * cols : (rank + 1) * cols]
 
-
-def z_transform(arrived, hi, lo, twiddle):
-    blocks, planes, _, rows, cols = arrived.shape
+    @pl.when(plane == 0)
+    def _():
+        low_ref[...] = out_ref[0]
+
+    @pl.when(plane == planes - 1)
+    def _():
+        high_ref[...] = out_ref[0]
+
+    steps = quarter // SEGS
+    count = slab_ref.shape[1] // (RADIX * steps)
+    for seg in range(SEGS):
+        for rank in range(RADIX):
+            values = out_ref[0, rank, pl.ds(seg, steps, stride=SEGS)]
+            slab_ref[seg, pl.ds(rank * count + plane, steps, stride=RADIX * count)] = values
+
+
+def z_transform(arrived, planes, hi, lo, twiddle):
+    blocks, total, cols = arrived.shape
+    double = (total - PACK) // planes
     quarter = hi.shape[0]
+    field = (RADIX, quarter, cols)
+    last = planes * double // PACK
     return pl.pallas_call(
         z_kernel,
         grid=(planes,),
         in_specs=[
-            pl.BlockSpec((blocks, 1, 2, rows, cols), lambda p: (0, p, 0, 0, 0)),
+            pl.BlockSpec((blocks, double, cols), lambda p: (0, p, 0)),
+            pl.BlockSpec((blocks, PACK, cols), lambda p: (0, last, 0)),
             pl.BlockSpec(hi.shape, lambda p: (0, 0)),
             pl.BlockSpec(lo.shape, lambda p: (0, 0)),
             pl.BlockSpec(twiddle.shape, lambda p: (0, 0, 0, 0)),
         ],
-        out_specs=pl.BlockSpec((1, RADIX, quarter, cols), lambda p: (p, 0, 0, 0)),
-        out_shape=jax.ShapeDtypeStruct((planes, RADIX, quarter, cols), jnp.float32),
+        out_specs=[
+            pl.BlockSpec((1, *field), lambda p: (p, 0, 0, 0)),
+            pl.BlockSpec(field, lambda p: (0, 0, 0)),
+            pl.BlockSpec(field, lambda p: (0, 0, 0)),
+            pl.BlockSpec((SEGS, RADIX * quarter // SEGS * planes, cols), lambda p: (0, 0, 0)),
+        ],
+        out_shape=[
+            jax.ShapeDtypeStruct((planes, *field), jnp.float32),
+            jax.ShapeDtypeStruct(field, jnp.float32),
+            jax.ShapeDtypeStruct(field, jnp.float32),
+            jax.ShapeDtypeStruct((SEGS, RADIX * quarter // SEGS * planes, cols), jnp.float32),
+        ],
         scratch_shapes=[
             pltpu.VMEM((2 * quarter, RADIX * cols), jnp.bfloat16),
             pltpu.VMEM((2 * quarter, RADIX * cols), jnp.bfloat16),
@@ -159,7 +222,7 @@
             transcendentals=0,
         ),
         name="z_transform",
-    )(arrived, hi, lo, twiddle)
+    )(arrived, arrived, hi, lo, twiddle)
 
 
 def soft2(coeffs, value):
@@ -170,16 +233,19 @@
     return jnp.maximum(soft, power)
 
 
-def render_kernel(cells, coeffs_ref, index_ref, *refs):
-    planes = len(refs) - 4
-    field_refs = refs[:planes]
-    before_ref, after_ref, out_ref, light_ref = refs[planes:]
-    steps = field_refs[0].shape[1] // SEGS
+def render_kernel(cells, picked, coeffs_ref, index_ref, field_ref, *refs):
+    edges, (out_ref, light_ref) = refs[:-2], refs[-2:]
+    steps = field_ref.shape[2] // SEGS
     images = index_ref.shape[0]
-    chain = [before_ref, *field_refs, after_ref]
+    last = field_ref.shape[0] - 1
     shape = (SEGS, LANES)
-    for plane in range(planes):
-        below, here, above = chain[plane], chain[plane + 1], chain[plane + 2]
+    if edges:
+        done_ref, before_ref, after_ref = edges
+        out_ref[...] = done_ref[...]
+    for plane in picked:
+        here = field_ref.at[plane]
+        below = before_ref if plane == 0 else field_ref.at[plane - 1]
+        above = after_ref if plane == last else field_ref.at[plane + 1]
 
         def light(i, carry):
             rows = pl.ds(pl.multiple_of(i * SEGS, SEGS), SEGS)
@@ -227,24 +293,23 @@
         lax.fori_loop(0, images, image, 0)
 
 
-def render(cells, fields, before, after, coeffs, index):
-    planes = len(fields)
+def render(cells, picked, coeffs, index, fields, *edges):
     images = index.shape[0]
+    planes = fields.shape[0]
     vmem = pl.BlockSpec(memory_space=pltpu.VMEM)
     smem = pl.BlockSpec(memory_space=pltpu.SMEM)
+    points = images * len(picked) * cells * LANES
     return pl.pallas_call(
-        functools.partial(render_kernel, cells),
-        in_specs=[smem, smem] + [vmem] * (planes + 2),
+        functools.partial(render_kernel, cells, picked),
+        in_specs=[smem, smem, vmem] + [vmem] * len(edges),
         out_specs=vmem,
         out_shape=jax.ShapeDtypeStruct((images, 4, planes, LANES), jnp.float32),
-        scratch_shapes=[pltpu.VMEM(fields[0].shape, jnp.float32)],
+        scratch_shapes=[pltpu.VMEM(fields.shape[1:], jnp.float32)],
         cost_estimate=pl.CostEstimate(
-            flops=64 * images * planes * cells * LANES,
-            bytes_accessed=4 * (planes + 2) * cells * LANES,
-            transcendentals=9 * images * planes * cells * LANES,
+            flops=64 * points, bytes_accessed=4 * 2**20, transcendentals=9 * points
         ),
         name="render",
-    )(coeffs, index, *fields, before, after)
+    )(coeffs, index, fields, *edges)
 
 
 def shifts(axis):
@@ -259,26 +324,21 @@
     nz = rows * blocks
     xhi, xlo = x_tables(nx, blocks)
     zhi, zlo, twiddle = z_tables(nz)
-    groups = [[0, planes - 1], list(range(1, planes - 1))]
-    fields = [None] * planes
-    sent = []
-    for group in groups:
-        picked = jnp.stack([spectrum[:, :, p] for p in group], axis=1)
-        mixed = x_transform(picked, xhi, xlo)
-        sent.append(lax.all_to_all(mixed, "depth", split_axis=0, concat_axis=0, tiled=True))
-    halos = None
+    mixed = x_transform(spectrum.reshape(2 * rows * planes, nx), planes, xhi, xlo)
+    arrived = lax.all_to_all(mixed, "depth", split_axis=0, concat_axis=0, tiled=True)
+    fields, low, high, slabs = z_transform(arrived, planes, zhi, zlo, twiddle)
     up, down = shifts("plane")
-    for group, arrived in zip(groups, sent):
-        done = z_transform(arrived, zhi, zlo, twiddle)
-        for at, p in enumerate(group):
-            fields[p] = done[at]
-        if halos is None:
-            halos = (lax.ppermute(fields[-1], "plane", up), lax.ppermute(fields[0], "plane", down))
-    steps = nz // RADIX // SEGS
-    stacked = jnp.stack(fields).reshape(planes, RADIX, steps, SEGS, LANES)
-    slabs = stacked.transpose(3, 2, 1, 0, 4).reshape(nz, planes, LANES)
-    scalar_field = lax.all_to_all(slabs, "depth", split_axis=0, concat_axis=2, tiled=True)
-    rendered = render(nz, fields, *halos, transfer_coeffs, transfer_index)
+    before = lax.ppermute(high, "plane", up)
+    after = lax.ppermute(low, "plane", down)
+    slabs = lax.all_to_all(
+        slabs.reshape(blocks, rows, planes, LANES), "depth", split_axis=0, concat_axis=0, tiled=True
+    )
+    scalar_field = slabs.transpose(1, 2, 0, 3).reshape(rows, planes, nx)
+    inner = tuple(range(1, planes - 1))
+    picture = render(nz, inner, transfer_coeffs, transfer_index, fields)
+    rendered = render(
+        nz, (0, planes - 1), transfer_coeffs, transfer_index, fields, picture, before, after
+    )
     return scalar_field, rendered
 
 
@@ -373,7 +433,7 @@
     def pick(spectrum, *rest):
         _, rows, planes, nx = spectrum.shape
         blocks = lax.axis_size("depth")
-        if nx == LANES * blocks and blocks % RADIX == 0 and planes > 3 and rows % 16 == 0:
+        if nx == LANES * blocks and blocks == SEGS and planes > 2 and rows % PACK == 0:
             return fast_body(spectrum, *rest)
         return body(spectrum, *rest)
 

time: 183 us -> 124 us (0.68)
  waiting for transfers between devices: 55.3 us -> 0.01 us
  blocking collectives: 0 us -> 32.2 us
  local copies, waits for them, and re-layouts: 25.6 us -> 6.58 us
  starting transfers between devices: 17.2 us -> 7.98 us
  Pallas kernels: 80.2 us -> 76.4 us
  other arithmetic: 3.53 us -> 0 us
    all_to_all x3 -> x1, waiting for transfers between devices: 33.9 us -> 0.01 us  [fast_body(): lax.all_to_all(slabs.reshape(blocks, rows, planes, LANES), 'depth', split...]
    all_to_all x0 -> x1, blocking collectives: none -> 32.2 us  [fast_body(): lax.all_to_all(mixed, 'depth', split_axis=0, concat_axis=0, tiled=True)]
    ppermute x2, waiting for transfers between devices: 21.4 us -> 0.01 us  [the longest x1 0.01 us: fast_body(): before = lax.ppermute(high, 'plane', up)]
    all_to_all x3 -> x1, starting transfers between devices: 13.3 us -> 3.75 us  [fast_body(): lax.all_to_all(slabs.reshape(blocks, rows, planes, LANES), 'depth', split...]
    slice x1 -> x0, local copies, waits for them, and re-layouts: 8.76 us -> none  [fast_body(): picked = jnp.stack([spectrum[:, :, p] for p in group], axis=1)]
    pallas_call x3, Pallas kernels: 71.8 us -> 67.8 us  [the longest x2 54 us: render(): pl.pallas_call(functools.partial(render_kernel, cells, picked), in_specs=...]
    squeeze x2 -> x0, local copies, waits for them, and re-layouts: 3.48 us -> none  [fast_body(): fields[p] = done[at]]
    all_to_all x2 -> x0, local copies, waits for them, and re-layouts: 3.37 us -> none  [fast_body(): lax.all_to_all(slabs, 'depth', split_axis=0, concat_axis=2, tiled=True)]
  transfers between devices with their start and end apart: 5 -> 3, of which waited for: 4 -> 0; matrix products, arithmetic and copies ran while one was open for 4% -> 1% of each run, Pallas kernels for 36% -> 44%
where the time goes in v1:
time: 124 us
  Pallas kernels  76.4 us (62%)
  blocking collectives  32.2 us (26%)
  starting transfers between devices  7.98 us (6%)
  local copies, waits for them, and re-layouts  6.58 us (5%)
    pallas_call x2, Pallas kernels, render(): pl.pallas_call(functools.partial(render_kernel, cells, picked), in_specs=...  54 us
    all_to_all x1, blocking collectives, fast_body(): lax.all_to_all(mixed, 'depth', split_axis=0, concat_axis=0, tiled=True)  32.2 us
    pallas_call x1, Pallas kernels, x_transform(): pl.pallas_call(functools.partial(x_kernel, planes), grid=(blocks,), in_sp...  13.7 us
    pallas_call x1, Pallas kernels, z_transform(): pl.pallas_call(z_kernel, grid=(planes,), in_specs=[pl.BlockSpec((blocks,...  8.61 us
    reshape x1, local copies, waits for them, and re-layouts, fast_body(): spectrum.reshape(2 * rows * planes, nx)  3.95 us
    all_to_all x1, starting transfers between devices, fast_body(): lax.all_to_all(slabs.reshape(blocks, rows, planes, LANES), 'depth', split...  3.75 us
  transfers between devices with their start and end apart: 3, of which 0 were waited for; matrix products, arithmetic and copies ran while one was open for 1% of the time, Pallas kernels for 44%

profile of v1, /device:TPU:0, one launch (start us, length us, event | category | flops | bytes accessed | tf_op | source)
XLA Modules:
  0.0 123.8 jit_solution(15494345706946690600)
XLA Ops:
  0.6 4.0 %reshape.13.spec_ref = bf16[1024,1024]{1,0:T(8,128)(2,1)} reshape(bf16[2,128,4,1024]{3,2,1,0:T(4,128)(2,1)} %param.8) | data formatting | bytes 4194304 | tf_op jit(solution)/shard_map/reshape | solution.py:327
  4.6 13.7 %x_transform.1 = s16[8,1040,128]{2,1,0:T(8,128)(2,1)} custom-call(bf16[1024,1024]{1,0:T(8,128)(2,1)} %reshape.13.spec_ref, bf16[8,1024,256]{2,1,0:T(8,128)(2,1)} %constant.10.clone.hi_ref, bf16[8,1024,256]{2,1,0:T(8,128)(2,1)} %constant.11.clone.lo_ref), custom_call_target="tpu_custom_call" | custom-call | flops 8589934592 | bytes 12582912 | tf_op jit(solution)/shard_map/x_transform/pallas_call | solution.py:92
  18.3 32.2 %all_to_all.10.in_ref.level_ref = s16[8,1040,128]{2,1,0:T(8,128)(2,1)} all-to-all(s16[8,1040,128]{2,1,0:T(8,128)(2,1)} %x_transform.1), channel_id=1, replica_groups=mesh['depth'=8,'plane'=4] {'depth'}, dimensions={0} | all-to-all | bytes 4259840 | tf_op jit(solution)/shard_map/all_to_all | solution.py:328
  50.5 8.6 %z_transform.1 = (f32[4,4,256,128]{3,2,1,0:T(8,128)}, f32[4,256,128]{2,1,0:T(8,128)}, f32[4,256,128]{2,1,0:T(8,128)}, f32[8,512,128]{2,1,0:T(8,128)}) custom-call(s16[8,1040,128]{2,1,0:T(8,128)(2,1)} %all_to_all.10.in_ref.level_ref, s16[8,1040,128]{2,1,0:T(8,128)(2,1)} %all_to_all.10.in_ref.level_ref, bf16[256,512]{1,0:T(8,128)(2,1)} %constant.12.clone.hi_ref, ...), custom_call_target="tpu_custom_call" | custom-call | flops 1610612736 | bytes 6291456 | tf_op jit(solution)/shard_map/z_transform/pallas_call | solution.py:193
  59.1 0.0 copy-start.2
  59.1 0.0 copy-start.1
  59.1 0.0 copy-start
  59.1 3.7 %all-to-all-start.1 = ((f32[8,128,4,128]{3,2,1,0:T(4,128)}), f32[8,128,4,128]{3,2,1,0:T(4,128)S(1)}, u32[]{:S(2)}, u32[]{:S(2)}) async-start(f32[8,128,4,128]{3,2,1,0:T(4,128)} %bitcast.7), calls=%async_computation.1 | async-start | bytes 4194304 | tf_op jit(solution)/shard_map/all_to_all | solution.py:333
  62.9 0.0 copy-done.2
  62.9 2.1 %collective-permute-start = (f32[4,256,128]{2,1,0:T(8,128)S(1)}, f32[4,256,128]{2,1,0:T(8,128)}, u32[]{:S(2)}, u32[]{:S(2)}) collective-permute-start(f32[4,256,128]{2,1,0:T(8,128)S(1)} %copy-done.2), channel_id=1, source_target_pairs={{0,1},{1,2},{2,3},{3,0},{4,5},{5,6},{6,7},{7,4},{8,9},{9,10},{10,1... | collective-permute-start | bytes 1572872 | tf_op jit(solution)/shard_map/ppermute | solution.py:331
  65.0 0.0 copy-done.1
  65.0 2.1 %collective-permute-start.1 = (f32[4,256,128]{2,1,0:T(8,128)S(1)}, f32[4,256,128]{2,1,0:T(8,128)}, u32[]{:S(2)}, u32[]{:S(2)}) collective-permute-start(f32[4,256,128]{2,1,0:T(8,128)S(1)} %copy-done.1), channel_id=1, source_target_pairs={{1,0},{2,1},{3,2},{0,3},{5,4},{6,5},{7,6},{4,7},{9,8},{10,9},{11,1... | collective-permute-start | bytes 1572872 | tf_op jit(solution)/shard_map/ppermute | solution.py:332
  67.1 0.0 copy-done
  67.2 0.7 copy.12.coeffs_ref
  67.8 26.9 %render.2.refs_0_ = f32[8,4,4,128]{3,2,1,0:T(4,128)} custom-call(f32[8,4,4]{2,1,0:T(4,128)} %copy.12.coeffs_ref, s32[8]{0:T(128)} %index_ref.3, f32[4,4,256,128]{3,2,1,0:T(8,128)} %get-tuple-element.7.field_ref), custom_call_target="tpu_custom_call" | custom-call | flops 134217728 | bytes 4194304 | tf_op jit(solution)/shard_map/render/pallas_call | solution.py:302
  94.7 0.0 collective-permute-done.refs_1_
  94.7 0.0 collective-permute-done.1.refs_2_
  94.7 27.2 %render.3 = f32[8,4,4,128]{3,2,1,0:T(4,128)} custom-call(f32[8,4,4]{2,1,0:T(4,128)} %copy.12.coeffs_ref, s32[8]{0:T(128)} %index_ref.3, f32[4,4,256,128]{3,2,1,0:T(8,128)} %get-tuple-element.7.field_ref, f32[8,4,4,128]{3,2,1,0:T(4,128)} %render.2.refs_0_, f32[4,256,128]{2,1,0:T(8,128)} %collective-permute-done.refs_1_, ...), custom_call_target="tpu_custom_call" | custom-call | flops 134217728 | bytes 4194304 | tf_op jit(solution)/shard_map/render/pallas_call | solution.py:302
  121.9 0.0 all-to-all-done.1
  121.9 1.9 %copy_bitcast_fusion = f32[128,4,1024]{2,1,0:T(4,128)} fusion(f32[8,128,4,128]{3,2,1,0:T(4,128)S(1)} %all-to-all-done.1), kind=kLoop, calls=%fused_computation | loop fusion | bytes 4194304 | tf_op jit(solution)/shard_map/reshape | solution.py:336
Async XLA Ops:
  59.1 3.8 %copy-start.2 = (f32[4,256,128]{2,1,0:T(8,128)S(1)}, f32[4,256,128]{2,1,0:T(8,128)}, u32[]{:S(2)}) copy-start(f32[4,256,128]{2,1,0:T(8,128)} %get-tuple-element.8) | copy-start | bytes 1572868
  59.1 5.9 %copy-start.1 = (f32[4,256,128]{2,1,0:T(8,128)S(1)}, f32[4,256,128]{2,1,0:T(8,128)}, u32[]{:S(2)}) copy-start(f32[4,256,128]{2,1,0:T(8,128)} %get-tuple-element.9) | copy-start | bytes 1572868
  59.1 8.0 %copy-start = (f32[8,4,4]{0,2,1:T(4,128)S(1)}, f32[8,4,4]{0,2,1:T(4,128)}, u32[]{:S(2)}) copy-start(f32[8,4,4]{0,2,1:T(4,128)} %param.9) | copy-start | bytes 1540
  59.1 62.8 %all-to-all-start.1 = ((f32[8,128,4,128]{3,2,1,0:T(4,128)}), f32[8,128,4,128]{3,2,1,0:T(4,128)S(1)}, u32[]{:S(2)}, u32[]{:S(2)}) async-start(f32[8,128,4,128]{3,2,1,0:T(4,128)} %bitcast.7), calls=%async_computation.1 | async-start | bytes 4194304 | tf_op jit(solution)/shard_map/all_to_all | solution.py:333
  62.9 31.8 %collective-permute-start = (f32[4,256,128]{2,1,0:T(8,128)S(1)}, f32[4,256,128]{2,1,0:T(8,128)}, u32[]{:S(2)}, u32[]{:S(2)}) collective-permute-start(f32[4,256,128]{2,1,0:T(8,128)S(1)} %copy-done.2), channel_id=1, source_target_pairs={{0,1},{1,2},{2,3},{3,0},{4,5},{5,6},{6,7},{7,4},{8,9},{9,10},{10,1... | collective-permute-start | bytes 1572872 | tf_op jit(solution)/shard_map/ppermute | solution.py:331
  65.0 29.7 %collective-permute-start.1 = (f32[4,256,128]{2,1,0:T(8,128)S(1)}, f32[4,256,128]{2,1,0:T(8,128)}, u32[]{:S(2)}, u32[]{:S(2)}) collective-permute-start(f32[4,256,128]{2,1,0:T(8,128)S(1)} %copy-done.1), channel_id=1, source_target_pairs={{1,0},{2,1},{3,2},{0,3},{5,4},{6,5},{7,6},{4,7},{9,8},{10,9},{11,1... | collective-permute-start | bytes 1572872 | tf_op jit(solution)/shard_map/ppermute | solution.py:332

commit v2 on v1

--- a/solution.py
+++ b/solution.py
@@ -8,6 +8,7 @@
 from jax.experimental.pallas import tpu as pltpu
 from jax.sharding import PartitionSpec as P
 
+
 density = 2.0
 shade_gain = 0.4
 highest = lax.Precision.HIGHEST
@@ -15,9 +16,12 @@
 SEGS = 8
 RADIX = 4
 PACK = 16
+PAIRS = ((6, 7), (2, 4), (3, 5), (1, 0))
 LEVELS = 16.0
 STEPS = 32766.0
 TINY = 2.0**-108
+FAINT = 2.0**-9
+SPARSE = 0.02
 LOG2E = 1.4426950408889634
 LN2 = 0.6931471805599453
 
@@ -51,7 +55,8 @@
     return split_table(table) + (jnp.asarray(wide, jnp.float32),)
 
 
-def x_kernel(planes, spec_ref, hi_ref, lo_ref, out_ref, mixed_ref):
+def x_kernel(planes, target_ref, spec_ref, hi_ref, lo_ref, *refs):
+    outs, (mixed_ref,) = refs[:-1], refs[-1:]
     half = spec_ref.shape[0] // 2
     rows = half // planes
     cols = hi_ref.shape[2] // 2
@@ -68,105 +73,139 @@
     b = product(1)
     mixed_ref[0] = a[:, :cols] - b[:, cols:]
     mixed_ref[1] = a[:, cols:] + b[:, :cols]
-    levels = jnp.zeros((PACK, cols), jnp.float32)
     place = lax.broadcasted_iota(jnp.int32, (PACK, cols), 0)
-    for plane in range(planes):
-        parts = [mixed_ref[part, pl.ds(plane, rows, stride=planes)] for part in range(2)]
-        peak = jnp.maximum(jnp.abs(parts[0]), jnp.abs(parts[1]))
-        peak = jnp.max(peak, axis=0, keepdims=True)
-        level = jnp.ceil(LEVELS * jnp.log2(jnp.maximum(peak, TINY))) + 1.0
-        scale = STEPS * jnp.exp2(level * (-1.0 / LEVELS))
-        for part in range(2):
-            at = (plane * 2 + part) * rows
-            whole = jnp.round(parts[part] * scale).astype(jnp.int32)
-            out_ref[0, at : at + rows] = whole.astype(jnp.int16)
-        levels = jnp.where(place == plane, jnp.broadcast_to(level, levels.shape), levels)
-    at = planes * 2 * rows
-    out_ref[0, at : at + PACK] = levels.astype(jnp.int32).astype(jnp.int16)
-
-
-def x_transform(spec, planes, hi, lo):
+
+    def emit(out_ref):
+        levels = jnp.zeros((PACK, cols), jnp.float32)
+        for plane in range(planes):
+            parts = [mixed_ref[part, pl.ds(plane, rows, stride=planes)] for part in range(2)]
+            peak = jnp.maximum(jnp.abs(parts[0]), jnp.abs(parts[1]))
+            peak = jnp.max(peak, axis=0, keepdims=True)
+            level = jnp.ceil(LEVELS * jnp.log2(jnp.maximum(peak, TINY))) + 1.0
+            scale = STEPS * jnp.exp2(level * (-1.0 / LEVELS))
+            for part in range(2):
+                at = (plane * 2 + part) * rows
+                whole = jnp.round(parts[part] * scale).astype(jnp.int32)
+                out_ref[at : at + rows] = whole.astype(jnp.int16)
+            levels = jnp.where(place == plane, jnp.broadcast_to(level, levels.shape), levels)
+        at = planes * 2 * rows
+        out_ref[at : at + PACK] = levels.astype(jnp.int32).astype(jnp.int16)
+
+    for which, out_ref in enumerate(outs):
+        pl.when(pl.program_id(0) == which)(functools.partial(emit, out_ref))
+
+
+def x_transform(spec, me, pair, planes, hi, lo):
     modes, nx = spec.shape
-    blocks, _, wide = hi.shape
+    _, _, wide = hi.shape
     cols = wide // 2
+    count = len(pair)
+    sent = (modes + PACK, cols)
+
+    def table(d, t):
+        return (jnp.bitwise_xor(t[0], jnp.where(d == 0, pair[0], pair[1])), 0, 0)
+
     return pl.pallas_call(
         functools.partial(x_kernel, planes),
-        grid=(blocks,),
-        in_specs=[
-            pl.BlockSpec((modes, nx), lambda d: (0, 0)),
-            pl.BlockSpec((1, nx, wide), lambda d: (d, 0, 0)),
-            pl.BlockSpec((1, nx, wide), lambda d: (d, 0, 0)),
-        ],
-        out_specs=pl.BlockSpec((1, modes + PACK, cols), lambda d: (d, 0, 0)),
-        out_shape=jax.ShapeDtypeStruct((blocks, modes + PACK, cols), jnp.int16),
-        scratch_shapes=[pltpu.VMEM((2, modes // 2, cols), jnp.float32)],
+        grid_spec=pltpu.PrefetchScalarGridSpec(
+            num_scalar_prefetch=1,
+            grid=(count,),
+            in_specs=[
+                pl.BlockSpec((modes, nx), lambda d, t: (0, 0)),
+                pl.BlockSpec((1, nx, wide), table),
+                pl.BlockSpec((1, nx, wide), table),
+            ],
+            out_specs=[pl.BlockSpec(sent, lambda d, t: (0, 0))] * count,
+            scratch_shapes=[pltpu.VMEM((2, modes // 2, cols), jnp.float32)],
+        ),
+        out_shape=[jax.ShapeDtypeStruct(sent, jnp.int16)] * count,
         cost_estimate=pl.CostEstimate(
-            flops=2 * modes * nx * nx * 4, bytes_accessed=12 * 2**20, transcendentals=0
+            flops=2 * modes * nx * wide * 2 * count,
+            bytes_accessed=2 * modes * nx + 4 * nx * wide * count,
+            transcendentals=0,
         ),
         name="x_transform",
-    )(spec, hi, lo)
-
-
-def z_kernel(
-    in_ref, level_ref, hi_ref, lo_ref, twiddle_ref, out_ref, low_ref, high_ref, slab_ref,
-    yhi_ref, ylo_ref,
-):
+    )(me, spec, hi, lo)
+
+
+def z_kernel(me_ref, *refs):
+    blocks = SEGS
+    sent, refs = refs[:blocks], refs[blocks:]
+    hi_ref, lo_ref, twiddle_ref, out_ref, low_ref, high_ref, slab_ref = refs[:7]
+    in_ref, yhi_ref, ylo_ref, sem = refs[7:]
     plane = pl.program_id(0)
     planes = pl.num_programs(0)
-    blocks, double, cols = in_ref.shape
-    rows = double // 2
+    _, total, cols = in_ref.shape
     quarter = hi_ref.shape[0]
-    per = quarter // rows
+    rows = quarter * RADIX // blocks
+    per = blocks // RADIX
+
+    @pl.when(plane == 0)
+    def _():
+        copies = [
+            pltpu.make_async_copy(ref, in_ref.at[jnp.bitwise_xor(me_ref[0], step)], sem.at[step])
+            for step, ref in enumerate(sent)
+        ]
+        for copy in copies:
+            copy.start()
+        for copy in copies:
+            copy.wait()
 
     def split(value, row, rank):
         high = value.astype(jnp.bfloat16)
-        yhi_ref[pl.ds(row, rows), rank * cols : (rank + 1) * cols] = high
-        ylo_ref[pl.ds(row, rows), rank * cols : (rank + 1) * cols] = (
+        yhi_ref[pl.ds(row, PACK), rank * cols : (rank + 1) * cols] = high
+        ylo_ref[pl.ds(row, PACK), rank * cols : (rank + 1) * cols] = (
             value - high.astype(jnp.float32)
         ).astype(jnp.bfloat16)
 
     place = lax.broadcasted_iota(jnp.int32, (PACK, cols), 0)
 
-    def load(source, part):
-        level = level_ref[source].astype(jnp.int32).astype(jnp.float32)
+    def scale_of(source):
+        level = in_ref[source, total - PACK : total].astype(jnp.int32).astype(jnp.float32)
         level = jnp.sum(jnp.where(place == plane, level, 0.0), axis=0, keepdims=True)
-        scale = jnp.exp2(level * (1.0 / LEVELS)) * (1.0 / STEPS)
-        whole = in_ref[source, part * rows : (part + 1) * rows]
-        return whole.astype(jnp.int32).astype(jnp.float32) * scale
-
+        return jnp.exp2(level * (1.0 / LEVELS)) * (1.0 / STEPS)
+
+    base = pl.multiple_of(plane * (2 * rows), 2 * rows)
     for block in range(per):
-        re = [load(t * per + block, 0) for t in range(RADIX)]
-        im = [load(t * per + block, 1) for t in range(RADIX)]
-        row = block * rows
-        even_re, even_im = re[0] + re[2], im[0] + im[2]
-        diff_re, diff_im = re[0] - re[2], im[0] - im[2]
-        odd_re, odd_im = re[1] + re[3], im[1] + im[3]
-        side_re, side_im = re[1] - re[3], im[1] - im[3]
-        sums = (
-            (even_re + odd_re, even_im + odd_im),
-            (diff_re - side_im, diff_im + side_re),
-            (even_re - odd_re, even_im - odd_im),
-            (diff_re + side_im, diff_im - side_re),
+        sources = [t * per + block for t in range(RADIX)]
+        scales = [jnp.broadcast_to(scale_of(source), (PACK, cols)) for source in sources]
+
+        def load(t, part, chunk):
+            whole = in_ref[sources[t], pl.ds(base + part * rows + chunk, PACK)]
+            return whole.astype(jnp.int32).astype(jnp.float32) * scales[t]
+
+        for chunk in range(0, rows, PACK):
+            re = [load(t, 0, chunk) for t in range(RADIX)]
+            im = [load(t, 1, chunk) for t in range(RADIX)]
+            row = block * rows + chunk
+            even_re, even_im = re[0] + re[2], im[0] + im[2]
+            diff_re, diff_im = re[0] - re[2], im[0] - im[2]
+            odd_re, odd_im = re[1] + re[3], im[1] + im[3]
+            side_re, side_im = re[1] - re[3], im[1] - im[3]
+            sums = (
+                (even_re + odd_re, even_im + odd_im),
+                (diff_re - side_im, diff_im + side_re),
+                (even_re - odd_re, even_im - odd_im),
+                (diff_re + side_im, diff_im - side_re),
+            )
+            for rank in range(RADIX):
+                a, b = sums[rank]
+                if rank > 0:
+                    c = twiddle_ref[rank - 1, 0, pl.ds(row, PACK)]
+                    s = twiddle_ref[rank - 1, 1, pl.ds(row, PACK)]
+                    a, b = a * c - b * s, a * s + b * c
+                split(a, row, rank)
+                split(b, quarter + row, rank)
+    for pair in range(0, RADIX, 2):
+        at = slice(pair * cols, (pair + 2) * cols)
+        high = yhi_ref[:, at]
+        value = (
+            jnp.dot(hi_ref[...], high, preferred_element_type=jnp.float32)
+            + jnp.dot(hi_ref[...], ylo_ref[:, at], preferred_element_type=jnp.float32)
+            + jnp.dot(lo_ref[...], high, preferred_element_type=jnp.float32)
         )
-        for rank in range(RADIX):
-            a, b = sums[rank]
-            if rank > 0:
-                c = twiddle_ref[rank - 1, 0, pl.ds(row, rows)]
-                s = twiddle_ref[rank - 1, 1, pl.ds(row, rows)]
-                a, b = a * c - b * s, a * s + b * c
-            split(a, row, rank)
-            split(b, quarter + row, rank)
-    hi = hi_ref[...]
-    lo = lo_ref[...]
-    yhi = yhi_ref[...]
-    ylo = ylo_ref[...]
-    total = (
-        jnp.dot(hi, yhi, preferred_element_type=jnp.float32)
-        + jnp.dot(hi, ylo, preferred_element_type=jnp.float32)
-        + jnp.dot(lo, yhi, preferred_element_type=jnp.float32)
-    )
-    for rank in range(RADIX):
-        out_ref[0, rank] = total[:, rank * cols : (rank + 1) * cols]
+        out_ref[0, pair] = value[:, :cols]
+        out_ref[0, pair + 1] = value[:, cols:]
 
     @pl.when(plane == 0)
     def _():
@@ -184,18 +223,18 @@
             slab_ref[seg, pl.ds(rank * count + plane, steps, stride=RADIX * count)] = values
 
 
-def z_transform(arrived, planes, hi, lo, twiddle):
-    blocks, total, cols = arrived.shape
-    double = (total - PACK) // planes
+def z_transform(me, sent, planes, hi, lo, twiddle):
+    total, cols = sent[0].shape
+    blocks = len(sent)
     quarter = hi.shape[0]
     field = (RADIX, quarter, cols)
-    last = planes * double // PACK
+    slabs = (SEGS, RADIX * quarter // SEGS * planes, cols)
     return pl.pallas_call(
         z_kernel,
         grid=(planes,),
-        in_specs=[
-            pl.BlockSpec((blocks, double, cols), lambda p: (0, p, 0)),
-            pl.BlockSpec((blocks, PACK, cols), lambda p: (0, last, 0)),
+        in_specs=[pl.BlockSpec(memory_space=pltpu.SMEM)]
+        + [pl.BlockSpec(memory_space=pl.ANY)] * blocks
+        + [
             pl.BlockSpec(hi.shape, lambda p: (0, 0)),
             pl.BlockSpec(lo.shape, lambda p: (0, 0)),
             pl.BlockSpec(twiddle.shape, lambda p: (0, 0, 0, 0)),
@@ -204,17 +243,19 @@
             pl.BlockSpec((1, *field), lambda p: (p, 0, 0, 0)),
             pl.BlockSpec(field, lambda p: (0, 0, 0)),
             pl.BlockSpec(field, lambda p: (0, 0, 0)),
-            pl.BlockSpec((SEGS, RADIX * quarter // SEGS * planes, cols), lambda p: (0, 0, 0)),
+            pl.BlockSpec(slabs, lambda p: (0, 0, 0)),
         ],
         out_shape=[
             jax.ShapeDtypeStruct((planes, *field), jnp.float32),
             jax.ShapeDtypeStruct(field, jnp.float32),
             jax.ShapeDtypeStruct(field, jnp.float32),
-            jax.ShapeDtypeStruct((SEGS, RADIX * quarter // SEGS * planes, cols), jnp.float32),
+            jax.ShapeDtypeStruct(slabs, jnp.float32),
         ],
         scratch_shapes=[
+            pltpu.VMEM((blocks, total, cols), jnp.int16),
             pltpu.VMEM((2 * quarter, RADIX * cols), jnp.bfloat16),
             pltpu.VMEM((2 * quarter, RADIX * cols), jnp.bfloat16),
+            pltpu.SemaphoreType.DMA((blocks,)),
         ],
         cost_estimate=pl.CostEstimate(
             flops=2 * planes * quarter * 2 * quarter * RADIX * cols * 3,
@@ -222,14 +263,15 @@
             transcendentals=0,
         ),
         name="z_transform",
-    )(arrived, arrived, hi, lo, twiddle)
-
-
-def soft2(coeffs, value):
+    )(me, *sent, hi, lo, twiddle)
+
+
+def soft2(coeffs, value, careful):
     power = ((coeffs[3] * value + coeffs[2]) * value + coeffs[1]) * value + coeffs[0]
     grown = jnp.exp2(jnp.minimum(power, 126.0))
-    large = jnp.log2(1.0 + grown)
-    soft = jnp.where(grown < 2.0**-12, grown * LOG2E, large)
+    soft = jnp.log2(1.0 + grown)
+    if careful:
+        soft = jnp.where(grown < 2.0**-12, grown * LOG2E, soft)
     return jnp.maximum(soft, power)
 
 
@@ -263,31 +305,52 @@
                 for j in range(4)
             ]
 
-            def step(i, state):
+            def step(careful, i, state):
                 clear, sums = state
                 rows = pl.ds(pl.multiple_of(i * SEGS, SEGS), SEGS)
                 for rank in range(RADIX):
                     value = here[rank, rows]
-                    depth = soft2(table[3], value) * (density / cells * LN2)
-                    passed = jnp.exp2(depth * -LOG2E)
-                    taken = jnp.where(depth < 2.0**-9, depth * (1.0 - 0.5 * depth), 1.0 - passed)
-                    weight = clear * taken * light_ref[rank, rows]
-                    clear = clear * passed
-                    sums = [acc + weight * soft2(table[j], value) for j, acc in enumerate(sums)]
+                    depth = soft2(table[3], value, careful) * (-density / cells)
+                    left = clear * jnp.exp2(depth)
+                    weight = clear - left
+                    if careful:
+                        near = depth * (-LN2 - (0.5 * LN2 * LN2) * depth)
+                        weight = jnp.where(depth > -(2.0**-9), clear * near, weight)
+                    clear = left
+                    weight = weight * light_ref[rank, rows]
+                    sums = [
+                        acc + weight * soft2(table[j], value, careful)
+                        for j, acc in enumerate(sums)
+                    ]
                 return clear, sums
 
-            zero = jnp.zeros(shape, jnp.float32)
-            clear, sums = lax.fori_loop(
-                0, steps, step, (jnp.ones(shape, jnp.float32), [zero, zero, zero]), unroll=2
-            )
-            reach = clear[0:1]
-            totals = [acc[0:1] for acc in sums]
-            for seg in range(1, SEGS):
-                totals = [t + reach * acc[seg : seg + 1] for t, acc in zip(totals, sums)]
-                reach = reach * clear[seg : seg + 1]
-            for j in range(3):
-                out_ref[m, j, plane : plane + 1] = totals[j] * LN2
-            out_ref[m, 3, plane : plane + 1] = reach
+            def march(careful, unroll):
+                zero = jnp.zeros(shape, jnp.float32)
+                clear, sums = lax.fori_loop(
+                    0,
+                    steps,
+                    functools.partial(step, careful),
+                    (jnp.ones(shape, jnp.float32), [zero, zero, zero]),
+                    unroll=unroll,
+                )
+                reach = clear[0:1]
+                totals = [acc[0:1] for acc in sums]
+                for seg in range(1, SEGS):
+                    totals = [t + reach * acc[seg : seg + 1] for t, acc in zip(totals, sums)]
+                    reach = reach * clear[seg : seg + 1]
+                for j in range(3):
+                    out_ref[m, j, plane : plane + 1] = totals[j] * LN2
+                out_ref[m, 3, plane : plane + 1] = reach
+                least = jnp.minimum(jnp.minimum(totals[0], totals[1]), totals[2])
+                taken = 1.0 - reach
+                return jnp.min(jnp.minimum(least - FAINT * taken, taken - SPARSE))
+
+            margin = march(False, 2)
+
+            @pl.when(jnp.logical_not(margin > 0.0))
+            def _():
+                march(True, 1)
+
             return carry
 
         lax.fori_loop(0, images, image, 0)
@@ -324,9 +387,15 @@
     nz = rows * blocks
     xhi, xlo = x_tables(nx, blocks)
     zhi, zlo, twiddle = z_tables(nz)
-    mixed = x_transform(spectrum.reshape(2 * rows * planes, nx), planes, xhi, xlo)
-    arrived = lax.all_to_all(mixed, "depth", split_axis=0, concat_axis=0, tiled=True)
-    fields, low, high, slabs = z_transform(arrived, planes, zhi, zlo, twiddle)
+    me = lax.axis_index("depth")[None]
+    modes = spectrum.reshape(2 * rows * planes, nx)
+    sent = [None] * blocks
+    for pair in PAIRS:
+        made = x_transform(modes, me, pair, planes, xhi, xlo)
+        for step, block in zip(pair, made):
+            swap = [(i, i ^ step) for i in range(blocks)]
+            sent[step] = lax.ppermute(block, "depth", swap) if step else block
+    fields, low, high, slabs = z_transform(me, sent, planes, zhi, zlo, twiddle)
     up, down = shifts("plane")
     before = lax.ppermute(high, "plane", up)
     after = lax.ppermute(low, "plane", down)

time: 124 us -> 117 us (0.944)
  blocking collectives: 32.2 us -> 0 us
  waiting for transfers between devices: 0.01 us -> 15.1 us
  starting transfers between devices: 7.98 us -> 15.7 us
  Pallas kernels: 76.4 us -> 77.7 us
    all_to_all x1 -> x0, blocking collectives: 32.2 us -> none  [fast_body(): lax.all_to_all(mixed, 'depth', split_axis=0, concat_axis=0, tiled=True)]
    ppermute x0 -> x7, waiting for transfers between devices: none -> 15 us  [fast_body(): sent[step] = lax.ppermute(block, 'depth', swap) if step else block]
    pallas_call x2 -> x5, Pallas kernels: 22.3 us -> 32 us  [the longest x4 21.8 us: x_transform(): pl.pallas_call(functools.partial(x_kernel, planes), grid_spec=pltpu.Prefe...]
    pallas_call x2, Pallas kernels: 54 us -> 45.8 us  [render(): pl.pallas_call(functools.partial(render_kernel, cells, picked), in_specs=...]
    ppermute x0 -> x7, starting transfers between devices: none -> 7.68 us  [fast_body(): sent[step] = lax.ppermute(block, 'depth', swap) if step else block]
  transfers between devices with their start and end apart: 3 -> 10, of which waited for: 0 -> 1; matrix products, arithmetic and copies ran while one was open for 1% -> 1% of each run, Pallas kernels for 44% -> 53%
where the time goes in v2:
time: 117 us
  Pallas kernels  77.7 us (66%)
  starting transfers between devices  15.7 us (13%)
  waiting for transfers between devices  15.1 us (13%)
  local copies, waits for them, and re-layouts  7.47 us (6%)
    pallas_call x2, Pallas kernels, render(): pl.pallas_call(functools.partial(render_kernel, cells, picked), in_specs=...  45.8 us
    pallas_call x4, Pallas kernels, x_transform(): pl.pallas_call(functools.partial(x_kernel, planes), grid_spec=pltpu.Prefe...  21.8 us
    ppermute x7, waiting for transfers between devices, fast_body(): sent[step] = lax.ppermute(block, 'depth', swap) if step else block  15 us
    pallas_call x1, Pallas kernels, z_transform(): pl.pallas_call(z_kernel, grid=(planes,), in_specs=[pl.BlockSpec(memory_sp...  10.2 us
    ppermute x7, starting transfers between devices, fast_body(): sent[step] = lax.ppermute(block, 'depth', swap) if step else block  7.68 us
    all_to_all x1, starting transfers between devices, fast_body(): lax.all_to_all(slabs.reshape(blocks, rows, planes, LANES), 'depth', split...  4.14 us
    reshape x1, local copies, waits for them, and re-layouts, fast_body(): modes = spectrum.reshape(2 * rows * planes, nx)  3.95 us
  transfers between devices with their start and end apart: 10, of which 1 were waited for; matrix products, arithmetic and copies ran while one was open for 1% of the time, Pallas kernels for 53%

profile of v2, /device:TPU:0, one launch (start us, length us, event | category | flops | bytes accessed | tf_op | source)
XLA Modules:
  0.0 116.7 jit_solution(5111155841802313386)
XLA Ops:
  0.6 4.0 %reshape.13.spec_ref = bf16[1024,1024]{1,0:T(8,128)(2,1)} reshape(bf16[2,128,4,1024]{3,2,1,0:T(4,128)(2,1)} %param.8) | data formatting | bytes 4194304 | tf_op jit(solution)/shard_map/reshape | solution.py:391
  4.6 5.5 %x_transform.4 = (s16[1040,128]{1,0:T(8,128)(2,1)}, s16[1040,128]{1,0:T(8,128)(2,1)}) custom-call(s32[1]{0:T(128)} %bitcast.target_ref.me_ref, bf16[1024,1024]{1,0:T(8,128)(2,1)} %reshape.13.spec_ref, bf16[8,1024,256]{2,1,0:T(8,128)(2,1)} %constant.16.clone.hi_ref, bf16[8,1024,256]{2,1,0:T(8,128)(2,1)} %constant.17.clone.lo_ref), custom_call_target="tpu_custom_call" | custom-call | flops 2147483648 | bytes 4194304 | tf_op jit(solution)/shard_map/x_transform/pallas_call | solution.py:108
  10.0 0.5 collective-permute-start
  10.5 5.4 %x_transform.5 = (s16[1040,128]{1,0:T(8,128)(2,1)}, s16[1040,128]{1,0:T(8,128)(2,1)}) custom-call(s32[1]{0:T(128)} %bitcast.target_ref.me_ref, bf16[1024,1024]{1,0:T(8,128)(2,1)} %reshape.13.spec_ref, bf16[8,1024,256]{2,1,0:T(8,128)(2,1)} %constant.16.clone.hi_ref, bf16[8,1024,256]{2,1,0:T(8,128)(2,1)} %constant.17.clone.lo_ref), custom_call_target="tpu_custom_call" | custom-call | flops 2147483648 | bytes 4194304 | tf_op jit(solution)/shard_map/x_transform/pallas_call | solution.py:108
  16.0 2.5 %collective-permute-start.1 = (s16[1040,128]{1,0:T(8,128)(2,1)}, s16[1040,128]{1,0:T(8,128)(2,1)S(1)}, u32[]{:S(2)}, u32[]{:S(2)}) collective-permute-start(s16[1040,128]{1,0:T(8,128)(2,1)} %get-tuple-element.16), channel_id=1, source_target_pairs={{0,8},{4,12},{8,0},{12,4},{16,24},{20,28},{24,16},{28,20},{1,9},{5... | collective-permute-start | bytes 798728 | tf_op jit(solution)/shard_map/ppermute | solution.py:397
  18.5 5.4 %x_transform.6 = (s16[1040,128]{1,0:T(8,128)(2,1)}, s16[1040,128]{1,0:T(8,128)(2,1)}) custom-call(s32[1]{0:T(128)} %bitcast.target_ref.me_ref, bf16[1024,1024]{1,0:T(8,128)(2,1)} %reshape.13.spec_ref, bf16[8,1024,256]{2,1,0:T(8,128)(2,1)} %constant.16.clone.hi_ref, bf16[8,1024,256]{2,1,0:T(8,128)(2,1)} %constant.17.clone.lo_ref), custom_call_target="tpu_custom_call" | custom-call | flops 2147483648 | bytes 4194304 | tf_op jit(solution)/shard_map/x_transform/pallas_call | solution.py:108
  23.9 0.2 collective-permute-start.2
  24.1 1.7 %collective-permute-start.3 = (s16[1040,128]{1,0:T(8,128)(2,1)S(1)}, s16[1040,128]{1,0:T(8,128)(2,1)S(1)}, u32[]{:S(2)}, u32[]{:S(2)}) collective-permute-start(s16[1040,128]{1,0:T(8,128)(2,1)S(1)} %copy-done.8), channel_id=1, source_target_pairs={{0,16},{4,20},{8,24},{12,28},{16,0},{20,4},{24,8},{28,12},{1,17},{... | collective-permute-start | bytes 798728 | tf_op jit(solution)/shard_map/ppermute | solution.py:397
  25.8 0.0 collective-permute-start.4
  25.8 5.4 %x_transform.7 = (s16[1040,128]{1,0:T(8,128)(2,1)}, s16[1040,128]{1,0:T(8,128)(2,1)}) custom-call(s32[1]{0:T(128)} %bitcast.target_ref.me_ref, bf16[1024,1024]{1,0:T(8,128)(2,1)} %reshape.13.spec_ref, bf16[8,1024,256]{2,1,0:T(8,128)(2,1)} %constant.16.clone.hi_ref, bf16[8,1024,256]{2,1,0:T(8,128)(2,1)} %constant.17.clone.lo_ref), custom_call_target="tpu_custom_call" | custom-call | flops 2147483648 | bytes 4194304 | tf_op jit(solution)/shard_map/x_transform/pallas_call | solution.py:108
  31.2 0.0 collective-permute-done.refs_1_
  31.2 2.6 %collective-permute-start.5 = (s16[1040,128]{1,0:T(8,128)(2,1)}, s16[1040,128]{1,0:T(8,128)(2,1)S(1)}, u32[]{:S(2)}, u32[]{:S(2)}) collective-permute-start(s16[1040,128]{1,0:T(8,128)(2,1)} %get-tuple-element.20), channel_id=1, source_target_pairs={{0,24},{4,28},{8,16},{12,20},{16,8},{20,12},{24,0},{28,4},{1,25},{... | collective-permute-start | bytes 798728 | tf_op jit(solution)/shard_map/ppermute | solution.py:397
  33.9 0.0 collective-permute-done.1.refs_2_
  33.9 0.2 collective-permute-start.6
  34.1 0.0 collective-permute-done.2.refs_3_
  34.1 0.0 collective-permute-done.3.refs_4_
  34.1 15.0 %collective-permute-done.4.refs_5_ = s16[1040,128]{1,0:T(8,128)(2,1)S(1)} collective-permute-done((s16[1040,128]{1,0:T(8,128)(2,1)}, s16[1040,128]{1,0:T(8,128)(2,1)S(1)}, u32[]{:S(2)}, u32[]{:S(2)}) %collective-permute-start.4) | collective-permute-done | bytes 266272 | tf_op jit(solution)/shard_map/ppermute | solution.py:397
  49.1 0.0 collective-permute-done.5.refs_6_
  49.1 0.0 collective-permute-done.6.refs_7_
  49.2 0.7 copy-done.7
  49.8 0.1 copy-done.9
  49.9 0.1 copy-done.10
  50.0 10.2 %z_transform.1 = (f32[4,4,256,128]{3,2,1,0:T(8,128)}, f32[4,256,128]{2,1,0:T(8,128)}, f32[4,256,128]{2,1,0:T(8,128)}, f32[8,512,128]{2,1,0:T(8,128)}) custom-call(s32[1]{0:T(128)} %bitcast.target_ref.me_ref, s16[1040,128]{1,0:T(8,128)(2,1)} %get-tuple-element.14.refs_0_, s16[1040,128]{1,0:T(8,128)(2,1)} %copy-done.3, s16[1040,128]{1,0:T(8,128)(2,1)} %copy-done.4, ...), custom_call_target="tpu_custom_call" | custom-call | flops 1610612736 | bytes 6291456 | tf_op jit(solution)/shard_map/z_transform/pallas_call | solution.py:232
  60.2 0.0 copy-start
  60.3 4.1 %all-to-all-start = ((f32[8,128,4,128]{3,2,1,0:T(4,128)}), f32[8,128,4,128]{3,2,1,0:T(4,128)S(1)}, u32[]{:S(2)}, u32[]{:S(2)}) async-start(f32[8,128,4,128]{3,2,1,0:T(4,128)} %bitcast.8), calls=%async_computation | async-start | bytes 4194304 | tf_op jit(solution)/shard_map/all_to_all | solution.py:402
  64.4 1.6 %collective-permute-start.7 = (f32[4,256,128]{2,1,0:T(8,128)S(1)}, f32[4,256,128]{2,1,0:T(8,128)}, u32[]{:S(2)}, u32[]{:S(2)}) collective-permute-start(f32[4,256,128]{2,1,0:T(8,128)S(1)} %copy-done.2), channel_id=1, source_target_pairs={{0,1},{1,2},{2,3},{3,0},{4,5},{5,6},{6,7},{7,4},{8,9},{9,10},{10,1... | collective-permute-start | bytes 1572872 | tf_op jit(solution)/shard_map/ppermute | solution.py:400
  66.0 2.2 %collective-permute-start.8 = (f32[4,256,128]{2,1,0:T(8,128)S(1)}, f32[4,256,128]{2,1,0:T(8,128)}, u32[]{:S(2)}, u32[]{:S(2)}) collective-permute-start(f32[4,256,128]{2,1,0:T(8,128)S(1)} %copy-done.1), channel_id=1, source_target_pairs={{1,0},{2,1},{3,2},{0,3},{5,4},{6,5},{7,6},{4,7},{9,8},{10,9},{11,1... | collective-permute-start | bytes 1572872 | tf_op jit(solution)/shard_map/ppermute | solution.py:401
  68.3 0.7 copy.12.coeffs_ref
  69.0 22.7 %render.2.refs_0_ = f32[8,4,4,128]{3,2,1,0:T(4,128)} custom-call(f32[8,4,4]{2,1,0:T(4,128)} %copy.12.coeffs_ref, s32[8]{0:T(128)} %index_ref.3, f32[4,4,256,128]{3,2,1,0:T(8,128)} %get-tuple-element.23.field_ref), custom_call_target="tpu_custom_call" | custom-call | flops 134217728 | bytes 4194304 | tf_op jit(solution)/shard_map/render/pallas_call | solution.py:365
  91.7 23.0 %render.3 = f32[8,4,4,128]{3,2,1,0:T(4,128)} custom-call(f32[8,4,4]{2,1,0:T(4,128)} %copy.12.coeffs_ref, s32[8]{0:T(128)} %index_ref.3, f32[4,4,256,128]{3,2,1,0:T(8,128)} %get-tuple-element.23.field_ref, f32[8,4,4,128]{3,2,1,0:T(4,128)} %render.2.refs_0_, f32[4,256,128]{2,1,0:T(8,128)} %collective-permute-done.7.refs_1_, ...), custom_call_target="tpu_custom_call" | custom-call | flops 134217728 | bytes 4194304 | tf_op jit(solution)/shard_map/render/pallas_call | solution.py:365
  114.8 0.0 all-to-all-done
  114.8 1.9 %copy_bitcast_fusion = f32[128,4,1024]{2,1,0:T(4,128)} fusion(f32[8,128,4,128]{3,2,1,0:T(4,128)S(1)} %all-to-all-done), kind=kLoop, calls=%fused_computation | loop fusion | bytes 4194304 | tf_op jit(solution)/shard_map/reshape | solution.py:405
  (20 shorter events, 0.0 us)
Async XLA Ops:
  10.0 21.2 %collective-permute-start = (s16[1040,128]{1,0:T(8,128)(2,1)}, s16[1040,128]{1,0:T(8,128)(2,1)S(1)}, u32[]{:S(2)}, u32[]{:S(2)}) collective-permute-start(s16[1040,128]{1,0:T(8,128)(2,1)} %get-tuple-element.15), channel_id=1, source_target_pairs={{0,4},{4,0},{8,12},{12,8},{16,20},{20,16},{24,28},{28,24},{1,5},{5... | collective-permute-start | bytes 798728 | tf_op jit(solution)/shard_map/ppermute | solution.py:397
  16.0 8.1 %copy-start.8 = (s16[1040,128]{1,0:T(8,128)(2,1)S(1)}, s16[1040,128]{1,0:T(8,128)(2,1)}, u32[]{:S(2)}) copy-start(s16[1040,128]{1,0:T(8,128)(2,1)} %get-tuple-element.18) | copy-start | bytes 798724
  16.0 17.9 %collective-permute-start.1 = (s16[1040,128]{1,0:T(8,128)(2,1)}, s16[1040,128]{1,0:T(8,128)(2,1)S(1)}, u32[]{:S(2)}, u32[]{:S(2)}) collective-permute-start(s16[1040,128]{1,0:T(8,128)(2,1)} %get-tuple-element.16), channel_id=1, source_target_pairs={{0,8},{4,12},{8,0},{12,4},{16,24},{20,28},{24,16},{28,20},{1,9},{5... | collective-permute-start | bytes 798728 | tf_op jit(solution)/shard_map/ppermute | solution.py:397
  23.9 10.2 %collective-permute-start.2 = (s16[1040,128]{1,0:T(8,128)(2,1)}, s16[1040,128]{1,0:T(8,128)(2,1)S(1)}, u32[]{:S(2)}, u32[]{:S(2)}) collective-permute-start(s16[1040,128]{1,0:T(8,128)(2,1)} %get-tuple-element.17), channel_id=1, source_target_pairs={{0,12},{4,8},{8,4},{12,0},{16,28},{20,24},{24,20},{28,16},{1,13},{... | collective-permute-start | bytes 798728 | tf_op jit(solution)/shard_map/ppermute | solution.py:397
  24.1 10.0 %collective-permute-start.3 = (s16[1040,128]{1,0:T(8,128)(2,1)S(1)}, s16[1040,128]{1,0:T(8,128)(2,1)S(1)}, u32[]{:S(2)}, u32[]{:S(2)}) collective-permute-start(s16[1040,128]{1,0:T(8,128)(2,1)S(1)} %copy-done.8), channel_id=1, source_target_pairs={{0,16},{4,20},{8,24},{12,28},{16,0},{20,4},{24,8},{28,12},{1,17},{... | collective-permute-start | bytes 798728 | tf_op jit(solution)/shard_map/ppermute | solution.py:397
  25.8 23.3 %collective-permute-start.4 = (s16[1040,128]{1,0:T(8,128)(2,1)}, s16[1040,128]{1,0:T(8,128)(2,1)S(1)}, u32[]{:S(2)}, u32[]{:S(2)}) collective-permute-start(s16[1040,128]{1,0:T(8,128)(2,1)} %get-tuple-element.19), channel_id=1, source_target_pairs={{0,20},{4,16},{8,28},{12,24},{16,4},{20,0},{24,12},{28,8},{1,21},{... | collective-permute-start | bytes 798728 | tf_op jit(solution)/shard_map/ppermute | solution.py:397
  31.2 17.9 %copy-start.3 = (s16[1040,128]{1,0:T(8,128)(2,1)}, s16[1040,128]{1,0:T(8,128)(2,1)S(1)}, u32[]{:S(2)}) copy-start(s16[1040,128]{1,0:T(8,128)(2,1)S(1)} %collective-permute-done.refs_1_) | copy-start | bytes 798724
  31.2 17.9 %collective-permute-start.5 = (s16[1040,128]{1,0:T(8,128)(2,1)}, s16[1040,128]{1,0:T(8,128)(2,1)S(1)}, u32[]{:S(2)}, u32[]{:S(2)}) collective-permute-start(s16[1040,128]{1,0:T(8,128)(2,1)} %get-tuple-element.20), channel_id=1, source_target_pairs={{0,24},{4,28},{8,16},{12,20},{16,8},{20,12},{24,0},{28,4},{1,25},{... | collective-permute-start | bytes 798728 | tf_op jit(solution)/shard_map/ppermute | solution.py:397
  33.9 15.3 %copy-start.4 = (s16[1040,128]{1,0:T(8,128)(2,1)}, s16[1040,128]{1,0:T(8,128)(2,1)S(1)}, u32[]{:S(2)}) copy-start(s16[1040,128]{1,0:T(8,128)(2,1)S(1)} %collective-permute-done.1.refs_2_) | copy-start | bytes 798724
  33.9 15.3 %collective-permute-start.6 = (s16[1040,128]{1,0:T(8,128)(2,1)}, s16[1040,128]{1,0:T(8,128)(2,1)S(1)}, u32[]{:S(2)}, u32[]{:S(2)}) collective-permute-start(s16[1040,128]{1,0:T(8,128)(2,1)} %get-tuple-element.21), channel_id=1, source_target_pairs={{0,28},{4,24},{8,20},{12,16},{16,12},{20,8},{24,4},{28,0},{1,29},{... | collective-permute-start | bytes 798728 | tf_op jit(solution)/shard_map/ppermute | solution.py:397
  34.1 15.1 %copy-start.5 = (s16[1040,128]{1,0:T(8,128)(2,1)}, s16[1040,128]{1,0:T(8,128)(2,1)S(1)}, u32[]{:S(2)}) copy-start(s16[1040,128]{1,0:T(8,128)(2,1)S(1)} %collective-permute-done.2.refs_3_) | copy-start | bytes 798724
  34.1 15.1 %copy-start.6 = (s16[1040,128]{1,0:T(8,128)(2,1)}, s16[1040,128]{1,0:T(8,128)(2,1)S(1)}, u32[]{:S(2)}) copy-start(s16[1040,128]{1,0:T(8,128)(2,1)S(1)} %collective-permute-done.3.refs_4_) | copy-start | bytes 798724
  49.1 0.7 copy-start.7
  49.1 0.8 copy-start.9
  49.1 0.9 copy-start.10
  60.2 4.2 %copy-start.2 = (f32[4,256,128]{2,1,0:T(8,128)S(1)}, f32[4,256,128]{2,1,0:T(8,128)}, u32[]{:S(2)}) copy-start(f32[4,256,128]{2,1,0:T(8,128)} %get-tuple-element.24) | copy-start | bytes 1572868
  60.2 5.8 %copy-start.1 = (f32[4,256,128]{2,1,0:T(8,128)S(1)}, f32[4,256,128]{2,1,0:T(8,128)}, u32[]{:S(2)}) copy-start(f32[4,256,128]{2,1,0:T(8,128)} %get-tuple-element.25) | copy-start | bytes 1572868
  60.2 8.0 %copy-start = (f32[8,4,4]{0,2,1:T(4,128)S(1)}, f32[8,4,4]{0,2,1:T(4,128)}, u32[]{:S(2)}) copy-start(f32[8,4,4]{0,2,1:T(4,128)} %param.9) | copy-start | bytes 1540
  60.3 54.5 %all-to-all-start = ((f32[8,128,4,128]{3,2,1,0:T(4,128)}), f32[8,128,4,128]{3,2,1,0:T(4,128)S(1)}, u32[]{:S(2)}, u32[]{:S(2)}) async-start(f32[8,128,4,128]{3,2,1,0:T(4,128)} %bitcast.8), calls=%async_computation | async-start | bytes 4194304 | tf_op jit(solution)/shard_map/all_to_all | solution.py:402
  64.4 27.3 %collective-permute-start.7 = (f32[4,256,128]{2,1,0:T(8,128)S(1)}, f32[4,256,128]{2,1,0:T(8,128)}, u32[]{:S(2)}, u32[]{:S(2)}) collective-permute-start(f32[4,256,128]{2,1,0:T(8,128)S(1)} %copy-done.2), channel_id=1, source_target_pairs={{0,1},{1,2},{2,3},{3,0},{4,5},{5,6},{6,7},{7,4},{8,9},{9,10},{10,1... | collective-permute-start | bytes 1572872 | tf_op jit(solution)/shard_map/ppermute | solution.py:400
  66.0 25.7 %collective-permute-start.8 = (f32[4,256,128]{2,1,0:T(8,128)S(1)}, f32[4,256,128]{2,1,0:T(8,128)}, u32[]{:S(2)}, u32[]{:S(2)}) collective-permute-start(f32[4,256,128]{2,1,0:T(8,128)S(1)} %copy-done.1), channel_id=1, source_target_pairs={{1,0},{2,1},{3,2},{0,3},{5,4},{6,5},{7,6},{4,7},{9,8},{10,9},{11,1... | collective-permute-start | bytes 1572872 | tf_op jit(solution)/shard_map/ppermute | solution.py:401

commit v3 on v2

--- a/solution.py
+++ b/solution.py
@@ -22,6 +22,7 @@
 TINY = 2.0**-108
 FAINT = 2.0**-9
 SPARSE = 0.02
+TERMS = 16
 LOG2E = 1.4426950408889634
 LN2 = 0.6931471805599453
 
@@ -55,6 +56,23 @@
     return split_table(table) + (jnp.asarray(wide, jnp.float32),)
 
 
+def level_of(peak):
+    level = jnp.ceil(LEVELS * jnp.log2(jnp.maximum(peak, TINY))) + 1.0
+    return level, STEPS * jnp.exp2(level * (-1.0 / LEVELS))
+
+
+def code(value, scale):
+    return jnp.round(value * scale).astype(jnp.int32).astype(jnp.int16)
+
+
+def decode(whole, scale):
+    return whole.astype(jnp.int32).astype(jnp.float32) * scale
+
+
+def step_of(level):
+    return jnp.exp2(level * (1.0 / LEVELS)) * (1.0 / STEPS)
+
+
 def x_kernel(planes, target_ref, spec_ref, hi_ref, lo_ref, *refs):
     outs, (mixed_ref,) = refs[:-1], refs[-1:]
     half = spec_ref.shape[0] // 2
@@ -81,12 +99,10 @@
             parts = [mixed_ref[part, pl.ds(plane, rows, stride=planes)] for part in range(2)]
             peak = jnp.maximum(jnp.abs(parts[0]), jnp.abs(parts[1]))
             peak = jnp.max(peak, axis=0, keepdims=True)
-            level = jnp.ceil(LEVELS * jnp.log2(jnp.maximum(peak, TINY))) + 1.0
-            scale = STEPS * jnp.exp2(level * (-1.0 / LEVELS))
+            level, scale = level_of(peak)
             for part in range(2):
                 at = (plane * 2 + part) * rows
-                whole = jnp.round(parts[part] * scale).astype(jnp.int32)
-                out_ref[at : at + rows] = whole.astype(jnp.int16)
+                out_ref[at : at + rows] = code(parts[part], scale)
             levels = jnp.where(place == plane, jnp.broadcast_to(level, levels.shape), levels)
         at = planes * 2 * rows
         out_ref[at : at + PACK] = levels.astype(jnp.int32).astype(jnp.int16)
@@ -163,7 +179,7 @@
     def scale_of(source):
         level = in_ref[source, total - PACK : total].astype(jnp.int32).astype(jnp.float32)
         level = jnp.sum(jnp.where(place == plane, level, 0.0), axis=0, keepdims=True)
-        return jnp.exp2(level * (1.0 / LEVELS)) * (1.0 / STEPS)
+        return step_of(level)
 
     base = pl.multiple_of(plane * (2 * rows), 2 * rows)
     for block in range(per):
@@ -171,13 +187,14 @@
         scales = [jnp.broadcast_to(scale_of(source), (PACK, cols)) for source in sources]
 
         def load(t, part, chunk):
-            whole = in_ref[sources[t], pl.ds(base + part * rows + chunk, PACK)]
-            return whole.astype(jnp.int32).astype(jnp.float32) * scales[t]
-
-        for chunk in range(0, rows, PACK):
+            start = pl.multiple_of(base + part * rows + chunk, PACK)
+            return decode(in_ref[sources[t], pl.ds(start, PACK)], scales[t])
+
+        def turn(nth, carry):
+            chunk = nth * PACK
             re = [load(t, 0, chunk) for t in range(RADIX)]
             im = [load(t, 1, chunk) for t in range(RADIX)]
-            row = block * rows + chunk
+            row = pl.multiple_of(block * rows + chunk, PACK)
             even_re, even_im = re[0] + re[2], im[0] + im[2]
             diff_re, diff_im = re[0] - re[2], im[0] - im[2]
             odd_re, odd_im = re[1] + re[3], im[1] + im[3]
@@ -196,6 +213,9 @@
                     a, b = a * c - b * s, a * s + b * c
                 split(a, row, rank)
                 split(b, quarter + row, rank)
+            return carry
+
+        lax.fori_loop(0, rows // PACK, turn, 0, unroll=2)
     for pair in range(0, RADIX, 2):
         at = slice(pair * cols, (pair + 2) * cols)
         high = yhi_ref[:, at]
@@ -207,13 +227,18 @@
         out_ref[0, pair] = value[:, :cols]
         out_ref[0, pair + 1] = value[:, cols:]
 
-    @pl.when(plane == 0)
-    def _():
-        low_ref[...] = out_ref[0]
-
-    @pl.when(plane == planes - 1)
-    def _():
-        high_ref[...] = out_ref[0]
+    def edge(edge_ref):
+        peak = jnp.max(jnp.abs(out_ref[0, 0]), axis=0, keepdims=True)
+        for rank in range(1, RADIX):
+            peak = jnp.maximum(peak, jnp.max(jnp.abs(out_ref[0, rank]), axis=0, keepdims=True))
+        level, scale = level_of(peak)
+        for rank in range(RADIX):
+            edge_ref[rank * quarter : (rank + 1) * quarter] = code(out_ref[0, rank], scale)
+        level = jnp.broadcast_to(level, (PACK, cols)).astype(jnp.int32)
+        edge_ref[RADIX * quarter :] = level.astype(jnp.int16)
+
+    pl.when(plane == 0)(functools.partial(edge, low_ref))
+    pl.when(plane == planes - 1)(functools.partial(edge, high_ref))
 
     steps = quarter // SEGS
     count = slab_ref.shape[1] // (RADIX * steps)
@@ -228,6 +253,7 @@
     blocks = len(sent)
     quarter = hi.shape[0]
     field = (RADIX, quarter, cols)
+    edge = (RADIX * quarter + PACK, cols)
     slabs = (SEGS, RADIX * quarter // SEGS * planes, cols)
     return pl.pallas_call(
         z_kernel,
@@ -241,14 +267,14 @@
         ],
         out_specs=[
             pl.BlockSpec((1, *field), lambda p: (p, 0, 0, 0)),
-            pl.BlockSpec(field, lambda p: (0, 0, 0)),
-            pl.BlockSpec(field, lambda p: (0, 0, 0)),
+            pl.BlockSpec(edge, lambda p: (0, 0)),
+            pl.BlockSpec(edge, lambda p: (0, 0)),
             pl.BlockSpec(slabs, lambda p: (0, 0, 0)),
         ],
         out_shape=[
             jax.ShapeDtypeStruct((planes, *field), jnp.float32),
-            jax.ShapeDtypeStruct(field, jnp.float32),
-            jax.ShapeDtypeStruct(field, jnp.float32),
+            jax.ShapeDtypeStruct(edge, jnp.int16),
+            jax.ShapeDtypeStruct(edge, jnp.int16),
             jax.ShapeDtypeStruct(slabs, jnp.float32),
         ],
         scratch_shapes=[
@@ -266,8 +292,7 @@
     )(me, *sent, hi, lo, twiddle)
 
 
-def soft2(coeffs, value, careful):
-    power = ((coeffs[3] * value + coeffs[2]) * value + coeffs[1]) * value + coeffs[0]
+def grow(power, careful):
     grown = jnp.exp2(jnp.minimum(power, 126.0))
     soft = jnp.log2(1.0 + grown)
     if careful:
@@ -275,84 +300,209 @@
     return jnp.maximum(soft, power)
 
 
+def cubic(coeffs, value):
+    return ((coeffs[3] * value + coeffs[2]) * value + coeffs[1]) * value + coeffs[0]
+
+
+def halves(value):
+    high = value.astype(jnp.bfloat16).astype(jnp.float32)
+    return high, (value - high).astype(jnp.bfloat16).astype(jnp.float32)
+
+
 def render_kernel(cells, picked, coeffs_ref, index_ref, field_ref, *refs):
-    edges, (out_ref, light_ref) = refs[:-2], refs[-2:]
+    first = len(refs) == 11
+    if first:
+        out_ref, table_ref, *refs = refs
+    else:
+        done_ref, table_ref, *halo_refs, out_ref, edge_ref = refs[:6]
+        refs = refs[6:]
+        before_ref, after_ref = edge_ref.at[0], edge_ref.at[1]
+        out_ref[...] = done_ref[...]
+    kept_ref, light_ref, lhs_ref, state_ref, sem, *refs = refs
+    banks = (refs[0:2], refs[2:4])
+    loads = [pltpu.make_async_copy(field_ref, kept_ref, sem.at[0])]
+    if not first:
+        loads.append(pltpu.make_async_copy(table_ref, lhs_ref, sem.at[1]))
+    for load in loads:
+        load.start()
+    field_ref = kept_ref
     steps = field_ref.shape[2] // SEGS
     images = index_ref.shape[0]
     last = field_ref.shape[0] - 1
     shape = (SEGS, LANES)
-    if edges:
-        done_ref, before_ref, after_ref = edges
-        out_ref[...] = done_ref[...]
-    for plane in picked:
-        here = field_ref.at[plane]
+    tall = 2 * SEGS
+    wide = len(picked) * LANES
+
+    def rows_of(i):
+        return pl.ds(pl.multiple_of(i * SEGS, SEGS), SEGS)
+
+    def coeffs_of(m, j):
+        return [coeffs_ref[index_ref[m], j, n] * LOG2E for n in range(4)]
+
+    lane = lax.broadcasted_iota(jnp.int32, (tall, TERMS * tall), 1)
+    row = lax.broadcasted_iota(jnp.int32, (tall, TERMS * tall), 0)
+    term = jnp.where(lane % tall == row, lane // tall, -1)
+
+    def lay(m, carry):
+        for j in range(4):
+            splits = [halves(jnp.full((1, LANES), c, jnp.float32)) for c in coeffs_of(m, j)]
+            full = jnp.full((1, LANES), coeffs_of(m, j)[0], jnp.float32)
+            weights = [*splits[0], full - splits[0][0] - splits[0][1]]
+            for n in range(1, 4):
+                weights += [*splits[n], *splits[n]]
+            tile = jnp.zeros((tall, TERMS * tall), jnp.float32)
+            for at, weight in enumerate(weights):
+                spread = jnp.broadcast_to(weight[:, :1], tile.shape)
+                tile = jnp.where(term == at, spread, tile)
+            start = pl.multiple_of((m * 4 + j) * tall, tall)
+            lhs_ref[pl.ds(start, tall)] = tile.astype(jnp.bfloat16)
+        return carry
+
+    if first:
+        lax.fori_loop(0, images, lay, 0)
+        table_ref[...] = lhs_ref[...]
+    else:
+        for nth, halo_ref in enumerate(halo_refs):
+            level = halo_ref[RADIX * steps * SEGS :].astype(jnp.int32).astype(jnp.float32)
+            scale = step_of(level[0:1])
+            for rank in range(RADIX):
+                rows = slice(rank * steps * SEGS, (rank + 1) * steps * SEGS)
+                edge_ref[nth, rank] = decode(halo_ref[rows], scale)
+    for load in loads:
+        load.wait()
+    for side, plane in enumerate(picked):
         below = before_ref if plane == 0 else field_ref.at[plane - 1]
         above = after_ref if plane == last else field_ref.at[plane + 1]
 
         def light(i, carry):
-            rows = pl.ds(pl.multiple_of(i * SEGS, SEGS), SEGS)
             for rank in range(RADIX):
-                slope = 0.5 * (above[rank, rows] - below[rank, rows])
-                light_ref[rank, rows] = 1.0 + shade_gain * jnp.tanh(slope)
+                slope = 0.5 * (above[rank, rows_of(i)] - below[rank, rows_of(i)])
+                light_ref[side, rank, rows_of(i)] = 1.0 + shade_gain * jnp.tanh(slope)
             return carry
 
         lax.fori_loop(0, steps, light, 0, unroll=2)
 
-        def image(m, carry):
-            which = index_ref[m]
-            table = [
-                [jnp.full(shape, coeffs_ref[which, j, n] * LOG2E, jnp.float32) for n in range(4)]
-                for j in range(4)
-            ]
-
-            def step(careful, i, state):
-                clear, sums = state
-                rows = pl.ds(pl.multiple_of(i * SEGS, SEGS), SEGS)
+    one = jnp.ones((tall, wide), jnp.bfloat16)
+
+    def powers(i, bank):
+        for half, poly_ref in enumerate(bank):
+            value = jnp.concatenate(
+                [
+                    jnp.concatenate(
+                        [field_ref[plane, 2 * half + odd, rows_of(i)] for plane in picked], axis=1
+                    )
+                    for odd in range(2)
+                ],
+                axis=0,
+            )
+            terms = [one, one, one]
+            power = value
+            for _ in range(3):
+                high = power.astype(jnp.bfloat16)
+                low = (power - high.astype(jnp.float32)).astype(jnp.bfloat16)
+                terms += [high, high, low, low]
+                power = power * value
+            terms += [one] * (TERMS - len(terms))
+            poly_ref[...] = jnp.dot(
+                lhs_ref[...], jnp.concatenate(terms, axis=0), preferred_element_type=jnp.float32
+            )
+
+    def absorb(i, bank):
+        for m in range(images):
+            for side in range(len(picked)):
+                clear = state_ref[m, side, 3]
+                sums = [state_ref[m, side, j] for j in range(3)]
                 for rank in range(RADIX):
-                    value = here[rank, rows]
-                    depth = soft2(table[3], value, careful) * (-density / cells)
-                    left = clear * jnp.exp2(depth)
-                    weight = clear - left
-                    if careful:
-                        near = depth * (-LN2 - (0.5 * LN2 * LN2) * depth)
-                        weight = jnp.where(depth > -(2.0**-9), clear * near, weight)
+                    poly_ref = bank[rank // 2]
+
+                    def poly(j):
+                        at = (m * 4 + j) * tall + (rank % 2) * SEGS
+                        return poly_ref[at : at + SEGS, side * LANES : (side + 1) * LANES]
+
+                    left = clear * jnp.exp2(grow(poly(3), False) * (-density / cells))
+                    weight = (clear - left) * light_ref[side, rank, rows_of(i)]
                     clear = left
-                    weight = weight * light_ref[rank, rows]
-                    sums = [
-                        acc + weight * soft2(table[j], value, careful)
-                        for j, acc in enumerate(sums)
-                    ]
-                return clear, sums
-
-            def march(careful, unroll):
+                    sums = [acc + weight * grow(poly(j), False) for j, acc in enumerate(sums)]
+                state_ref[m, side, 3] = clear
+                for j in range(3):
+                    state_ref[m, side, j] = sums[j]
+
+    state_ref[:, :, 0:3] = jnp.zeros((images, len(picked), 3, *shape), jnp.float32)
+    state_ref[:, :, 3] = jnp.ones((images, len(picked), *shape), jnp.float32)
+    powers(0, banks[0])
+    powers(1, banks[1])
+
+    def pair(k, carry):
+        absorb(2 * k, banks[0])
+        absorb(2 * k + 1, banks[1])
+        powers(jnp.minimum(2 * k + 2, steps - 2), banks[0])
+        powers(jnp.minimum(2 * k + 3, steps - 1), banks[1])
+        return carry
+
+    lax.fori_loop(0, steps // 2, pair, 0)
+
+    seg = lax.broadcasted_iota(jnp.int32, shape, 0)
+
+    def finish(m, plane, clear, sums):
+        reach = jnp.where(seg == 0, 1.0, pltpu.roll(clear, 1, 0))
+        for shift in (1, 2, 4):
+            reach = reach * jnp.where(seg < shift, 1.0, pltpu.roll(reach, shift, 0))
+        totals = [jnp.sum(reach * acc, axis=0, keepdims=True) for acc in sums]
+        clear = (reach * clear)[SEGS - 1 :]
+        for j in range(3):
+            out_ref[m, j, plane : plane + 1] = totals[j] * LN2
+        out_ref[m, 3, plane : plane + 1] = clear
+        least = jnp.minimum(jnp.minimum(totals[0], totals[1]), totals[2])
+        taken = 1.0 - clear
+        return jnp.minimum(least - FAINT * taken, taken - SPARSE)
+
+    margins = []
+    for m in range(images):
+        for side, plane in enumerate(picked):
+            sums = [state_ref[m, side, j] for j in range(3)]
+            margins.append(finish(m, plane, state_ref[m, side, 3], sums))
+    while len(margins) > 1:
+        margins = [
+            jnp.minimum(a, b) for a, b in zip(margins[::2], margins[1::2])
+        ]
+
+    def image(m, carry):
+        for side, plane in enumerate(picked):
+            sums = [state_ref[m, side, j] for j in range(3)]
+            margin = jnp.min(finish(m, plane, state_ref[m, side, 3], sums))
+
+            @pl.when(jnp.logical_not(margin > 0.0))
+            def _():
+                table = [
+                    [jnp.full(shape, c, jnp.float32) for c in coeffs_of(m, j)] for j in range(4)
+                ]
+
+                def step(i, state):
+                    clear, sums = state
+                    for rank in range(RADIX):
+                        value = field_ref[plane, rank, rows_of(i)]
+                        depth = grow(cubic(table[3], value), True) * (-density / cells)
+                        left = clear * jnp.exp2(depth)
+                        near = clear * depth * (-LN2 - (0.5 * LN2 * LN2) * depth)
+                        weight = jnp.where(depth > -(2.0**-9), near, clear - left)
+                        weight = weight * light_ref[side, rank, rows_of(i)]
+                        clear = left
+                        sums = [
+                            acc + weight * grow(cubic(table[j], value), True)
+                            for j, acc in enumerate(sums)
+                        ]
+                    return clear, sums
+
                 zero = jnp.zeros(shape, jnp.float32)
                 clear, sums = lax.fori_loop(
-                    0,
-                    steps,
-                    functools.partial(step, careful),
-                    (jnp.ones(shape, jnp.float32), [zero, zero, zero]),
-                    unroll=unroll,
+                    0, steps, step, (jnp.ones(shape, jnp.float32), [zero, zero, zero])
                 )
-                reach = clear[0:1]
-                totals = [acc[0:1] for acc in sums]
-                for seg in range(1, SEGS):
-                    totals = [t + reach * acc[seg : seg + 1] for t, acc in zip(totals, sums)]
-                    reach = reach * clear[seg : seg + 1]
-                for j in range(3):
-                    out_ref[m, j, plane : plane + 1] = totals[j] * LN2
-                out_ref[m, 3, plane : plane + 1] = reach
-                least = jnp.minimum(jnp.minimum(totals[0], totals[1]), totals[2])
-                taken = 1.0 - reach
-                return jnp.min(jnp.minimum(least - FAINT * taken, taken - SPARSE))
-
-            margin = march(False, 2)
-
-            @pl.when(jnp.logical_not(margin > 0.0))
-            def _():
-                march(True, 1)
-
-            return carry
-
+                finish(m, plane, clear, sums)
+
+        return carry
+
+    @pl.when(jnp.logical_not(jnp.min(margins[0]) > 0.0))
+    def _():
         lax.fori_loop(0, images, image, 0)
 
 
@@ -362,12 +512,25 @@
     vmem = pl.BlockSpec(memory_space=pltpu.VMEM)
     smem = pl.BlockSpec(memory_space=pltpu.SMEM)
     points = images * len(picked) * cells * LANES
+    poly = (images * 4 * 2 * SEGS, len(picked) * LANES)
+    table = (poly[0], TERMS * 2 * SEGS)
+    picture = jax.ShapeDtypeStruct((images, 4, planes, LANES), jnp.float32)
+    any_space = pl.BlockSpec(memory_space=pl.ANY)
+    first = not edges
     return pl.pallas_call(
         functools.partial(render_kernel, cells, picked),
-        in_specs=[smem, smem, vmem] + [vmem] * len(edges),
-        out_specs=vmem,
-        out_shape=jax.ShapeDtypeStruct((images, 4, planes, LANES), jnp.float32),
-        scratch_shapes=[pltpu.VMEM(fields.shape[1:], jnp.float32)],
+        in_specs=[smem, smem, any_space] + ([] if first else [vmem, any_space, vmem, vmem]),
+        out_specs=[vmem, vmem] if first else vmem,
+        out_shape=[picture, jax.ShapeDtypeStruct(table, jnp.bfloat16)] if first else picture,
+        scratch_shapes=([] if first else [pltpu.VMEM((2, *fields.shape[1:]), jnp.float32)])
+        + [
+            pltpu.VMEM(fields.shape, jnp.float32),
+            pltpu.VMEM((len(picked), *fields.shape[1:]), jnp.float32),
+            pltpu.VMEM(table, jnp.bfloat16),
+            pltpu.VMEM((images, len(picked), 4, SEGS, LANES), jnp.float32),
+            pltpu.SemaphoreType.DMA((2,)),
+        ]
+        + [pltpu.VMEM(poly, jnp.float32)] * 4,
         cost_estimate=pl.CostEstimate(
             flops=64 * points, bytes_accessed=4 * 2**20, transcendentals=9 * points
         ),
@@ -404,9 +567,9 @@
     )
     scalar_field = slabs.transpose(1, 2, 0, 3).reshape(rows, planes, nx)
     inner = tuple(range(1, planes - 1))
-    picture = render(nz, inner, transfer_coeffs, transfer_index, fields)
+    picture, table = render(nz, inner, transfer_coeffs, transfer_index, fields)
     rendered = render(
-        nz, (0, planes - 1), transfer_coeffs, transfer_index, fields, picture, before, after
+        nz, (0, planes - 1), transfer_coeffs, transfer_index, fields, picture, table, before, after
     )
     return scalar_field, rendered
 
@@ -502,7 +665,7 @@
     def pick(spectrum, *rest):
         _, rows, planes, nx = spectrum.shape
         blocks = lax.axis_size("depth")
-        if nx == LANES * blocks and blocks == SEGS and planes > 2 and rows % PACK == 0:
+        if nx == LANES * blocks and blocks == SEGS and planes == 4 and rows % PACK == 0:
             return fast_body(spectrum, *rest)
         return body(spectrum, *rest)
 

time: 117 us -> 110 us (0.940)
  Pallas kernels: 77.7 us -> 69.8 us
    pallas_call x2, Pallas kernels: 45.8 us -> 37.6 us  [render(): pl.pallas_call(functools.partial(render_kernel, cells, picked), in_specs=...]
    unnamed x23 -> x27, local copies, waits for them, and re-layouts: 1.6 us -> 2.37 us
  transfers between devices with their start and end apart: 10 -> 10, of which waited for: 1 -> 1; matrix products, arithmetic and copies ran while one was open for 1% -> 1% of each run, Pallas kernels for 53% -> 49%
where the time goes in v3:
time: 110 us
  Pallas kernels  69.8 us (63%)
  starting transfers between devices  15.7 us (14%)
  waiting for transfers between devices  15.1 us (14%)
  local copies, waits for them, and re-layouts  8.24 us (7%)
    pallas_call x2, Pallas kernels, render(): pl.pallas_call(functools.partial(render_kernel, cells, picked), in_specs=...  37.6 us
    pallas_call x4, Pallas kernels, x_transform(): pl.pallas_call(functools.partial(x_kernel, planes), grid_spec=pltpu.Prefe...  21.9 us
    ppermute x7, waiting for transfers between devices, fast_body(): sent[step] = lax.ppermute(block, 'depth', swap) if step else block  15.1 us
    pallas_call x1, Pallas kernels, z_transform(): pl.pallas_call(z_kernel, grid=(planes,), in_specs=[pl.BlockSpec(memory_sp...  10.4 us
    ppermute x7, starting transfers between devices, fast_body(): sent[step] = lax.ppermute(block, 'depth', swap) if step else block  7.64 us
    all_to_all x1, starting transfers between devices, fast_body(): lax.all_to_all(slabs.reshape(blocks, rows, planes, LANES), 'depth', split...  4.14 us
    reshape x1, local copies, waits for them, and re-layouts, fast_body(): modes = spectrum.reshape(2 * rows * planes, nx)  3.95 us
    unnamed x27, local copies, waits for them, and re-layouts  2.37 us
  transfers between devices with their start and end apart: 10, of which 1 were waited for; matrix products, arithmetic and copies ran while one was open for 1% of the time, Pallas kernels for 49%

profile of v3, /device:TPU:0, one launch (start us, length us, event | category | flops | bytes accessed | tf_op | source)
XLA Modules:
  0.0 109.6 jit_solution(18330872483565732220)
XLA Ops:
  0.6 4.0 %reshape.13.spec_ref = bf16[1024,1024]{1,0:T(8,128)(2,1)} reshape(bf16[2,128,4,1024]{3,2,1,0:T(4,128)(2,1)} %param.8) | data formatting | bytes 4194304 | tf_op jit(solution)/shard_map/reshape | solution.py:554
  4.6 5.5 %x_transform.4 = (s16[1040,128]{1,0:T(8,128)(2,1)}, s16[1040,128]{1,0:T(8,128)(2,1)}) custom-call(s32[1]{0:T(128)} %bitcast.target_ref.me_ref, bf16[1024,1024]{1,0:T(8,128)(2,1)} %reshape.13.spec_ref, bf16[8,1024,256]{2,1,0:T(8,128)(2,1)} %constant.16.clone.hi_ref, bf16[8,1024,256]{2,1,0:T(8,128)(2,1)} %constant.17.clone.lo_ref), custom_call_target="tpu_custom_call" | custom-call | flops 2147483648 | bytes 4194304 | tf_op jit(solution)/shard_map/x_transform/pallas_call | solution.py:124
  10.1 0.5 collective-permute-start
  10.5 5.4 %x_transform.5 = (s16[1040,128]{1,0:T(8,128)(2,1)}, s16[1040,128]{1,0:T(8,128)(2,1)}) custom-call(s32[1]{0:T(128)} %bitcast.target_ref.me_ref, bf16[1024,1024]{1,0:T(8,128)(2,1)} %reshape.13.spec_ref, bf16[8,1024,256]{2,1,0:T(8,128)(2,1)} %constant.16.clone.hi_ref, bf16[8,1024,256]{2,1,0:T(8,128)(2,1)} %constant.17.clone.lo_ref), custom_call_target="tpu_custom_call" | custom-call | flops 2147483648 | bytes 4194304 | tf_op jit(solution)/shard_map/x_transform/pallas_call | solution.py:124
  16.0 2.5 %collective-permute-start.1 = (s16[1040,128]{1,0:T(8,128)(2,1)}, s16[1040,128]{1,0:T(8,128)(2,1)S(1)}, u32[]{:S(2)}, u32[]{:S(2)}) collective-permute-start(s16[1040,128]{1,0:T(8,128)(2,1)} %get-tuple-element.18), channel_id=1, source_target_pairs={{0,8},{4,12},{8,0},{12,4},{16,24},{20,28},{24,16},{28,20},{1,9},{5... | collective-permute-start | bytes 798728 | tf_op jit(solution)/shard_map/ppermute | solution.py:560
  18.5 5.5 %x_transform.6 = (s16[1040,128]{1,0:T(8,128)(2,1)}, s16[1040,128]{1,0:T(8,128)(2,1)}) custom-call(s32[1]{0:T(128)} %bitcast.target_ref.me_ref, bf16[1024,1024]{1,0:T(8,128)(2,1)} %reshape.13.spec_ref, bf16[8,1024,256]{2,1,0:T(8,128)(2,1)} %constant.16.clone.hi_ref, bf16[8,1024,256]{2,1,0:T(8,128)(2,1)} %constant.17.clone.lo_ref), custom_call_target="tpu_custom_call" | custom-call | flops 2147483648 | bytes 4194304 | tf_op jit(solution)/shard_map/x_transform/pallas_call | solution.py:124
  24.0 0.1 collective-permute-start.2
  24.1 1.7 %collective-permute-start.3 = (s16[1040,128]{1,0:T(8,128)(2,1)S(1)}, s16[1040,128]{1,0:T(8,128)(2,1)S(1)}, u32[]{:S(2)}, u32[]{:S(2)}) collective-permute-start(s16[1040,128]{1,0:T(8,128)(2,1)S(1)} %copy-done.6), channel_id=1, source_target_pairs={{0,16},{4,20},{8,24},{12,28},{16,0},{20,4},{24,8},{28,12},{1,17},{... | collective-permute-start | bytes 798728 | tf_op jit(solution)/shard_map/ppermute | solution.py:560
  25.8 0.0 collective-permute-start.4
  25.8 5.5 %x_transform.7 = (s16[1040,128]{1,0:T(8,128)(2,1)}, s16[1040,128]{1,0:T(8,128)(2,1)}) custom-call(s32[1]{0:T(128)} %bitcast.target_ref.me_ref, bf16[1024,1024]{1,0:T(8,128)(2,1)} %reshape.13.spec_ref, bf16[8,1024,256]{2,1,0:T(8,128)(2,1)} %constant.16.clone.hi_ref, bf16[8,1024,256]{2,1,0:T(8,128)(2,1)} %constant.17.clone.lo_ref), custom_call_target="tpu_custom_call" | custom-call | flops 2147483648 | bytes 4194304 | tf_op jit(solution)/shard_map/x_transform/pallas_call | solution.py:124
  31.3 2.6 %collective-permute-start.5 = (s16[1040,128]{1,0:T(8,128)(2,1)}, s16[1040,128]{1,0:T(8,128)(2,1)S(1)}, u32[]{:S(2)}, u32[]{:S(2)}) collective-permute-start(s16[1040,128]{1,0:T(8,128)(2,1)} %get-tuple-element.22), channel_id=1, source_target_pairs={{0,24},{4,28},{8,16},{12,20},{16,8},{20,12},{24,0},{28,4},{1,25},{... | collective-permute-start | bytes 798728 | tf_op jit(solution)/shard_map/ppermute | solution.py:560
  33.9 0.2 collective-permute-start.6
  34.1 0.0 collective-permute-done.3.refs_4_
  34.1 15.0 %collective-permute-done.4.refs_5_ = s16[1040,128]{1,0:T(8,128)(2,1)S(1)} collective-permute-done((s16[1040,128]{1,0:T(8,128)(2,1)}, s16[1040,128]{1,0:T(8,128)(2,1)S(1)}, u32[]{:S(2)}, u32[]{:S(2)}) %collective-permute-start.4) | collective-permute-done | bytes 266272 | tf_op jit(solution)/shard_map/ppermute | solution.py:560
  49.2 0.0 collective-permute-done.5.refs_6_
  49.2 0.6 copy-done.5
  49.9 0.1 copy-done.7
  50.0 0.1 copy-done.8
  50.1 10.4 %z_transform.1 = (f32[4,4,256,128]{3,2,1,0:T(8,128)}, s16[1040,128]{1,0:T(8,128)(2,1)}, s16[1040,128]{1,0:T(8,128)(2,1)}, f32[8,512,128]{2,1,0:T(8,128)}) custom-call(s32[1]{0:T(128)} %bitcast.target_ref.me_ref, s16[1040,128]{1,0:T(8,128)(2,1)} %get-tuple-element.16.refs_0_, s16[1040,128]{1,0:T(8,128)(2,1)} %copy-done.1, s16[1040,128]{1,0:T(8,128)(2,1)} %copy-done.2, ...), custom_call_target="tpu_custom_call" | custom-call | flops 1610612736 | bytes 6291456 | tf_op jit(solution)/shard_map/z_transform/pallas_call | solution.py:258
  60.5 0.0 copy-start
  60.5 4.1 %all-to-all-start = ((f32[8,128,4,128]{3,2,1,0:T(4,128)}), f32[8,128,4,128]{3,2,1,0:T(4,128)S(1)}, u32[]{:S(2)}, u32[]{:S(2)}) async-start(f32[8,128,4,128]{3,2,1,0:T(4,128)} %bitcast.8), calls=%async_computation | async-start | bytes 4194304 | tf_op jit(solution)/shard_map/all_to_all | solution.py:565
  64.6 1.6 %collective-permute-start.7 = (s16[1040,128]{1,0:T(8,128)(2,1)S(1)}, s16[1040,128]{1,0:T(8,128)(2,1)S(1)}, u32[]{:S(2)}, u32[]{:S(2)}) collective-permute-start(s16[1040,128]{1,0:T(8,128)(2,1)S(1)} %copy-done.10), channel_id=1, source_target_pairs={{0,1},{1,2},{2,3},{3,0},{4,5},{5,6},{6,7},{7,4},{8,9},{9,10},{10,1... | collective-permute-start | bytes 798728 | tf_op jit(solution)/shard_map/ppermute | solution.py:563
  66.3 2.2 %collective-permute-start.8 = (s16[1040,128]{1,0:T(8,128)(2,1)S(1)}, s16[1040,128]{1,0:T(8,128)(2,1)S(1)}, u32[]{:S(2)}, u32[]{:S(2)}) collective-permute-start(s16[1040,128]{1,0:T(8,128)(2,1)S(1)} %copy-done.9), channel_id=1, source_target_pairs={{1,0},{2,1},{3,2},{0,3},{5,4},{6,5},{7,6},{4,7},{9,8},{10,9},{11,1... | collective-permute-start | bytes 798728 | tf_op jit(solution)/shard_map/ppermute | solution.py:564
  68.5 0.7 copy.12.coeffs_ref
  69.2 18.8 %render.2 = (f32[8,4,4,128]{3,2,1,0:T(4,128)}, bf16[512,256]{1,0:T(8,128)(2,1)}) custom-call(f32[8,4,4]{2,1,0:T(4,128)} %copy.12.coeffs_ref, s32[8]{0:T(128)} %index_ref.3, f32[4,4,256,128]{3,2,1,0:T(8,128)} %get-tuple-element.25.field_ref), custom_call_target="tpu_custom_call" | custom-call | flops 134217728 | bytes 4194304 | tf_op jit(solution)/shard_map/render/pallas_call | solution.py:520
  88.0 0.0 collective-permute-done.7.refs_2_
  88.0 0.0 collective-permute-done.8.refs_3_
  88.1 0.7 copy-done.11
  88.7 0.1 copy-done.12
  88.9 18.8 %render.3 = f32[8,4,4,128]{3,2,1,0:T(4,128)} custom-call(f32[8,4,4]{2,1,0:T(4,128)} %copy.12.coeffs_ref, s32[8]{0:T(128)} %index_ref.3, f32[4,4,256,128]{3,2,1,0:T(8,128)} %get-tuple-element.25.field_ref, f32[8,4,4,128]{3,2,1,0:T(4,128)} %get-tuple-element.26.refs_0_, bf16[512,256]{1,0:T(8,128)(2,1)} %get-tuple-element.27.refs_1_, ...), custom_call_target="tpu_custom_call" | custom-call | flops 134217728 | bytes 4194304 | tf_op jit(solution)/shard_map/render/pallas_call | solution.py:520
  107.7 0.0 all-to-all-done
  107.7 1.9 %copy_bitcast_fusion = f32[128,4,1024]{2,1,0:T(4,128)} fusion(f32[8,128,4,128]{3,2,1,0:T(4,128)S(1)} %all-to-all-done), kind=kLoop, calls=%fused_computation | loop fusion | bytes 4194304 | tf_op jit(solution)/shard_map/reshape | solution.py:568
  (24 shorter events, 0.0 us)
Async XLA Ops:
  10.1 21.2 %collective-permute-start = (s16[1040,128]{1,0:T(8,128)(2,1)}, s16[1040,128]{1,0:T(8,128)(2,1)S(1)}, u32[]{:S(2)}, u32[]{:S(2)}) collective-permute-start(s16[1040,128]{1,0:T(8,128)(2,1)} %get-tuple-element.17), channel_id=1, source_target_pairs={{0,4},{4,0},{8,12},{12,8},{16,20},{20,16},{24,28},{28,24},{1,5},{5... | collective-permute-start | bytes 798728 | tf_op jit(solution)/shard_map/ppermute | solution.py:560
  16.0 8.1 %copy-start.6 = (s16[1040,128]{1,0:T(8,128)(2,1)S(1)}, s16[1040,128]{1,0:T(8,128)(2,1)}, u32[]{:S(2)}) copy-start(s16[1040,128]{1,0:T(8,128)(2,1)} %get-tuple-element.20) | copy-start | bytes 798724
  16.0 18.0 %collective-permute-start.1 = (s16[1040,128]{1,0:T(8,128)(2,1)}, s16[1040,128]{1,0:T(8,128)(2,1)S(1)}, u32[]{:S(2)}, u32[]{:S(2)}) collective-permute-start(s16[1040,128]{1,0:T(8,128)(2,1)} %get-tuple-element.18), channel_id=1, source_target_pairs={{0,8},{4,12},{8,0},{12,4},{16,24},{20,28},{24,16},{28,20},{1,9},{5... | collective-permute-start | bytes 798728 | tf_op jit(solution)/shard_map/ppermute | solution.py:560
  24.0 10.2 %collective-permute-start.2 = (s16[1040,128]{1,0:T(8,128)(2,1)}, s16[1040,128]{1,0:T(8,128)(2,1)S(1)}, u32[]{:S(2)}, u32[]{:S(2)}) collective-permute-start(s16[1040,128]{1,0:T(8,128)(2,1)} %get-tuple-element.19), channel_id=1, source_target_pairs={{0,12},{4,8},{8,4},{12,0},{16,28},{20,24},{24,20},{28,16},{1,13},{... | collective-permute-start | bytes 798728 | tf_op jit(solution)/shard_map/ppermute | solution.py:560
  24.1 10.0 %collective-permute-start.3 = (s16[1040,128]{1,0:T(8,128)(2,1)S(1)}, s16[1040,128]{1,0:T(8,128)(2,1)S(1)}, u32[]{:S(2)}, u32[]{:S(2)}) collective-permute-start(s16[1040,128]{1,0:T(8,128)(2,1)S(1)} %copy-done.6), channel_id=1, source_target_pairs={{0,16},{4,20},{8,24},{12,28},{16,0},{20,4},{24,8},{28,12},{1,17},{... | collective-permute-start | bytes 798728 | tf_op jit(solution)/shard_map/ppermute | solution.py:560
  25.8 23.4 %collective-permute-start.4 = (s16[1040,128]{1,0:T(8,128)(2,1)}, s16[1040,128]{1,0:T(8,128)(2,1)S(1)}, u32[]{:S(2)}, u32[]{:S(2)}) collective-permute-start(s16[1040,128]{1,0:T(8,128)(2,1)} %get-tuple-element.21), channel_id=1, source_target_pairs={{0,20},{4,16},{8,28},{12,24},{16,4},{20,0},{24,12},{28,8},{1,21},{... | collective-permute-start | bytes 798728 | tf_op jit(solution)/shard_map/ppermute | solution.py:560
  31.3 17.9 %copy-start.1 = (s16[1040,128]{1,0:T(8,128)(2,1)}, s16[1040,128]{1,0:T(8,128)(2,1)S(1)}, u32[]{:S(2)}) copy-start(s16[1040,128]{1,0:T(8,128)(2,1)S(1)} %collective-permute-done.refs_1_) | copy-start | bytes 798724
  31.3 17.9 %collective-permute-start.5 = (s16[1040,128]{1,0:T(8,128)(2,1)}, s16[1040,128]{1,0:T(8,128)(2,1)S(1)}, u32[]{:S(2)}, u32[]{:S(2)}) collective-permute-start(s16[1040,128]{1,0:T(8,128)(2,1)} %get-tuple-element.22), channel_id=1, source_target_pairs={{0,24},{4,28},{8,16},{12,20},{16,8},{20,12},{24,0},{28,4},{1,25},{... | collective-permute-start | bytes 798728 | tf_op jit(solution)/shard_map/ppermute | solution.py:560
  33.9 15.3 %copy-start.2 = (s16[1040,128]{1,0:T(8,128)(2,1)}, s16[1040,128]{1,0:T(8,128)(2,1)S(1)}, u32[]{:S(2)}) copy-start(s16[1040,128]{1,0:T(8,128)(2,1)S(1)} %collective-permute-done.1.refs_2_) | copy-start | bytes 798724
  33.9 15.2 %collective-permute-start.6 = (s16[1040,128]{1,0:T(8,128)(2,1)}, s16[1040,128]{1,0:T(8,128)(2,1)S(1)}, u32[]{:S(2)}, u32[]{:S(2)}) collective-permute-start(s16[1040,128]{1,0:T(8,128)(2,1)} %get-tuple-element.23), channel_id=1, source_target_pairs={{0,28},{4,24},{8,20},{12,16},{16,12},{20,8},{24,4},{28,0},{1,29},{... | collective-permute-start | bytes 798728 | tf_op jit(solution)/shard_map/ppermute | solution.py:560
  34.1 15.1 %copy-start.3 = (s16[1040,128]{1,0:T(8,128)(2,1)}, s16[1040,128]{1,0:T(8,128)(2,1)S(1)}, u32[]{:S(2)}) copy-start(s16[1040,128]{1,0:T(8,128)(2,1)S(1)} %collective-permute-done.2.refs_3_) | copy-start | bytes 798724
  34.1 15.1 %copy-start.4 = (s16[1040,128]{1,0:T(8,128)(2,1)}, s16[1040,128]{1,0:T(8,128)(2,1)S(1)}, u32[]{:S(2)}) copy-start(s16[1040,128]{1,0:T(8,128)(2,1)S(1)} %collective-permute-done.3.refs_4_) | copy-start | bytes 798724
  49.2 0.7 copy-start.5
  49.2 0.8 copy-start.7
  49.2 0.9 copy-start.8
  60.5 4.2 %copy-start.10 = (s16[1040,128]{1,0:T(8,128)(2,1)S(1)}, s16[1040,128]{1,0:T(8,128)(2,1)}, u32[]{:S(2)}) copy-start(s16[1040,128]{1,0:T(8,128)(2,1)} %get-tuple-element.28) | copy-start | bytes 798724
  60.5 5.8 %copy-start.9 = (s16[1040,128]{1,0:T(8,128)(2,1)S(1)}, s16[1040,128]{1,0:T(8,128)(2,1)}, u32[]{:S(2)}) copy-start(s16[1040,128]{1,0:T(8,128)(2,1)} %get-tuple-element.29) | copy-start | bytes 798724
  60.5 8.0 %copy-start = (f32[8,4,4]{0,2,1:T(4,128)S(1)}, f32[8,4,4]{0,2,1:T(4,128)}, u32[]{:S(2)}) copy-start(f32[8,4,4]{0,2,1:T(4,128)} %param.9) | copy-start | bytes 1540
  60.5 47.2 %all-to-all-start = ((f32[8,128,4,128]{3,2,1,0:T(4,128)}), f32[8,128,4,128]{3,2,1,0:T(4,128)S(1)}, u32[]{:S(2)}, u32[]{:S(2)}) async-start(f32[8,128,4,128]{3,2,1,0:T(4,128)} %bitcast.8), calls=%async_computation | async-start | bytes 4194304 | tf_op jit(solution)/shard_map/all_to_all | solution.py:565
  64.6 23.4 %collective-permute-start.7 = (s16[1040,128]{1,0:T(8,128)(2,1)S(1)}, s16[1040,128]{1,0:T(8,128)(2,1)S(1)}, u32[]{:S(2)}, u32[]{:S(2)}) collective-permute-start(s16[1040,128]{1,0:T(8,128)(2,1)S(1)} %copy-done.10), channel_id=1, source_target_pairs={{0,1},{1,2},{2,3},{3,0},{4,5},{5,6},{6,7},{7,4},{8,9},{9,10},{10,1... | collective-permute-start | bytes 798728 | tf_op jit(solution)/shard_map/ppermute | solution.py:563
  66.3 21.7 %collective-permute-start.8 = (s16[1040,128]{1,0:T(8,128)(2,1)S(1)}, s16[1040,128]{1,0:T(8,128)(2,1)S(1)}, u32[]{:S(2)}, u32[]{:S(2)}) collective-permute-start(s16[1040,128]{1,0:T(8,128)(2,1)S(1)} %copy-done.9), channel_id=1, source_target_pairs={{1,0},{2,1},{3,2},{0,3},{5,4},{6,5},{7,6},{4,7},{9,8},{10,9},{11,1... | collective-permute-start | bytes 798728 | tf_op jit(solution)/shard_map/ppermute | solution.py:564
  88.0 0.7 copy-start.11
  88.0 0.8 copy-start.12

commit v4 on v3

--- a/solution.py
+++ b/solution.py
@@ -23,6 +23,7 @@
 FAINT = 2.0**-9
 SPARSE = 0.02
 TERMS = 16
+VMEM_LIMIT = 24 * 2**20
 LOG2E = 1.4426950408889634
 LN2 = 0.6931471805599453
 
@@ -30,7 +31,7 @@
 def split_table(table):
     hi = table.astype(jnp.bfloat16)
     lo = (table - hi.astype(np.float64)).astype(jnp.bfloat16)
-    return jnp.asarray(hi), jnp.asarray(lo)
+    return hi, lo
 
 
 def x_tables(nx, blocks):
@@ -39,7 +40,8 @@
     cols = nx // blocks
     cos = (np.cos(angle) / np.sqrt(nx)).reshape(nx, blocks, cols)
     sin = (np.sin(angle) / np.sqrt(nx)).reshape(nx, blocks, cols)
-    return split_table(np.concatenate([cos, sin], axis=2).transpose(1, 0, 2))
+    hi, lo = split_table(np.concatenate([cos, sin], axis=2).transpose(1, 0, 2))
+    return jnp.asarray(np.concatenate([hi, lo], axis=2))
 
 
 def z_tables(nz):
@@ -53,7 +55,8 @@
     turn = 2.0 * np.pi * np.arange(1, RADIX)[:, None] * q[None, :] / nz
     twiddle = np.stack([np.cos(turn), np.sin(turn)], axis=1)
     wide = np.broadcast_to(twiddle[..., None], twiddle.shape + (LANES,))
-    return split_table(table) + (jnp.asarray(wide, jnp.float32),)
+    hi, lo = split_table(table)
+    return jnp.asarray(hi), jnp.asarray(lo), jnp.asarray(wide, jnp.float32)
 
 
 def level_of(peak):
@@ -73,19 +76,18 @@
     return jnp.exp2(level * (1.0 / LEVELS)) * (1.0 / STEPS)
 
 
-def x_kernel(planes, target_ref, spec_ref, hi_ref, lo_ref, *refs):
+def x_kernel(planes, target_ref, spec_ref, table_ref, *refs):
     outs, (mixed_ref,) = refs[:-1], refs[-1:]
-    half = spec_ref.shape[0] // 2
+    half = spec_ref.shape[1] // 2
     rows = half // planes
-    cols = hi_ref.shape[2] // 2
-    hi = hi_ref[0]
-    lo = lo_ref[0]
+    cols = table_ref.shape[2] // 4
+    table = table_ref[0]
 
     def product(part):
-        modes = spec_ref[part * half : (part + 1) * half]
-        return jnp.dot(modes, hi, preferred_element_type=jnp.float32) + jnp.dot(
-            modes, lo, preferred_element_type=jnp.float32
-        )
+        own = slice(part * half, (part + 1) * half)
+        modes = jnp.concatenate([spec_ref[at, own] for at in range(spec_ref.shape[0])], axis=1)
+        both = jnp.dot(modes, table, preferred_element_type=jnp.float32)
+        return both[:, : 2 * cols] + both[:, 2 * cols :]
 
     a = product(0)
     b = product(1)
@@ -111,10 +113,11 @@
         pl.when(pl.program_id(0) == which)(functools.partial(emit, out_ref))
 
 
-def x_transform(spec, me, pair, planes, hi, lo):
-    modes, nx = spec.shape
-    _, _, wide = hi.shape
-    cols = wide // 2
+def x_transform(spec, me, pair, planes, tables):
+    tiles, modes, lanes = spec.shape
+    nx = tiles * lanes
+    _, _, wide = tables.shape
+    cols = wide // 4
     count = len(pair)
     sent = (modes + PACK, cols)
 
@@ -127,8 +130,7 @@
             num_scalar_prefetch=1,
             grid=(count,),
             in_specs=[
-                pl.BlockSpec((modes, nx), lambda d, t: (0, 0)),
-                pl.BlockSpec((1, nx, wide), table),
+                pl.BlockSpec(spec.shape, lambda d, t: (0, 0, 0)),
                 pl.BlockSpec((1, nx, wide), table),
             ],
             out_specs=[pl.BlockSpec(sent, lambda d, t: (0, 0))] * count,
@@ -136,12 +138,13 @@
         ),
         out_shape=[jax.ShapeDtypeStruct(sent, jnp.int16)] * count,
         cost_estimate=pl.CostEstimate(
-            flops=2 * modes * nx * wide * 2 * count,
-            bytes_accessed=2 * modes * nx + 4 * nx * wide * count,
+            flops=2 * modes * nx * wide * count,
+            bytes_accessed=2 * modes * nx + 2 * nx * wide * count,
             transcendentals=0,
         ),
         name="x_transform",
-    )(me, spec, hi, lo)
+        compiler_params=pltpu.CompilerParams(vmem_limit_bytes=VMEM_LIMIT),
+    )(me, spec, tables)
 
 
 def z_kernel(me_ref, *refs):
@@ -289,6 +292,7 @@
             transcendentals=0,
         ),
         name="z_transform",
+        compiler_params=pltpu.CompilerParams(vmem_limit_bytes=VMEM_LIMIT),
     )(me, *sent, hi, lo, twiddle)
 
 
@@ -535,6 +539,7 @@
             flops=64 * points, bytes_accessed=4 * 2**20, transcendentals=9 * points
         ),
         name="render",
+        compiler_params=pltpu.CompilerParams(vmem_limit_bytes=VMEM_LIMIT),
     )(coeffs, index, fields, *edges)
 
 
@@ -548,13 +553,13 @@
     _, rows, planes, nx = spectrum.shape
     blocks = lax.axis_size("depth")
     nz = rows * blocks
-    xhi, xlo = x_tables(nx, blocks)
+    x_table = x_tables(nx, blocks)
     zhi, zlo, twiddle = z_tables(nz)
     me = lax.axis_index("depth")[None]
-    modes = spectrum.reshape(2 * rows * planes, nx)
+    modes = spectrum.reshape(2 * rows * planes, blocks, LANES).transpose(1, 0, 2)
     sent = [None] * blocks
     for pair in PAIRS:
-        made = x_transform(modes, me, pair, planes, xhi, xlo)
+        made = x_transform(modes, me, pair, planes, x_table)
         for step, block in zip(pair, made):
             swap = [(i, i ^ step) for i in range(blocks)]
             sent[step] = lax.ppermute(block, "depth", swap) if step else block

time: 110 us -> 97.9 us (0.89)
  Pallas kernels: 69.8 us -> 52.8 us
  waiting for transfers between devices: 15.1 us -> 17.7 us
  local copies, waits for them, and re-layouts: 8.24 us -> 10.1 us
    pallas_call x4, Pallas kernels: 21.9 us -> 11 us  [x_transform(): pl.pallas_call(functools.partial(x_kernel, planes), grid_spec=pltpu.Prefe...]
    pallas_call x2, Pallas kernels: 37.6 us -> 34.4 us  [render(): pl.pallas_call(functools.partial(render_kernel, cells, picked), in_specs=...]
    pallas_call x1, Pallas kernels: 10.4 us -> 7.37 us  [z_transform(): pl.pallas_call(z_kernel, grid=(planes,), in_specs=[pl.BlockSpec(memory_sp...]
    ppermute x7, waiting for transfers between devices: 15.1 us -> 17.7 us  [fast_body(): sent[step] = lax.ppermute(block, 'depth', swap) if step else block]
    reshape x1, local copies, waits for them, and re-layouts: 1.92 us -> 3.51 us  [fast_body(): scalar_field = slabs.transpose(1, 2, 0, 3).reshape(rows, planes, nx)]
    unnamed x27 -> x13, local copies, waits for them, and re-layouts: 2.37 us -> 3.54 us
    reshape x1 -> x2, local copies, waits for them, and re-layouts: 3.95 us -> 3.02 us  [fast_body(): spectrum.reshape(2 * rows * planes, blocks, LANES).transpose(1, 0, 2)]
  transfers between devices with their start and end apart: 10 -> 10, of which waited for: 1 -> 2; matrix products, arithmetic and copies ran while one was open for 1% -> 0% of each run, Pallas kernels for 49% -> 44%
where the time goes in v4:
time: 97.9 us; the launch traced here: 97.6 us
  Pallas kernels  52.8 us (54%)
  waiting for transfers between devices  17.7 us (18%)
  starting transfers between devices  16.1 us (16%)
  local copies, waits for them, and re-layouts  10.1 us (10%)
    pallas_call x2, Pallas kernels, render(): pl.pallas_call(functools.partial(render_kernel, cells, picked), in_specs=...  34.4 us
    ppermute x7, waiting for transfers between devices, fast_body(): sent[step] = lax.ppermute(block, 'depth', swap) if step else block  17.7 us
    pallas_call x4, Pallas kernels, x_transform(): pl.pallas_call(functools.partial(x_kernel, planes), grid_spec=pltpu.Prefe...  11 us
    ppermute x7, starting transfers between devices, fast_body(): sent[step] = lax.ppermute(block, 'depth', swap) if step else block  7.85 us
    pallas_call x1, Pallas kernels, z_transform(): pl.pallas_call(z_kernel, grid=(planes,), in_specs=[pl.BlockSpec(memory_sp...  7.37 us
    all_to_all x1, starting transfers between devices, fast_body(): lax.all_to_all(slabs.reshape(blocks, rows, planes, LANES), 'depth', split...  4.36 us
    unnamed x13, local copies, waits for them, and re-layouts  3.54 us
    reshape x1, local copies, waits for them, and re-layouts, fast_body(): scalar_field = slabs.transpose(1, 2, 0, 3).reshape(rows, planes, nx)  3.51 us
  transfers between devices with their start and end apart: 10, of which 2 were waited for; matrix products, arithmetic and copies ran while one was open for 0% of the time, Pallas kernels for 44%

profile of v4, /device:TPU:0, one launch (start us, length us, event | category | flops | bytes accessed | tf_op | source)
XLA Modules:
  0.0 97.6 jit_solution(6244201380025557738)
XLA Ops:
  0.6 2.7 %reshape.13 = bf16[1024,8,128]{2,1,0:T(8,128)(2,1)S(1)} reshape(bf16[2,128,4,1024]{3,2,1,0:T(4,128)(2,1)} %param.7) | data formatting | bytes 4194304 | tf_op jit(solution)/shard_map/reshape | solution.py:559
  3.4 0.3 copy.19
  3.7 0.0 copy-start
  3.7 3.4 %copy-done = bf16[8,1024,512]{2,1,0:T(8,128)(2,1)S(1)} copy-done((bf16[8,1024,512]{2,1,0:T(8,128)(2,1)S(1)}, bf16[8,1024,512]{2,1,0:T(8,128)(2,1)}, u32[]{:S(2)}) %copy-start) | copy-done | bytes 8388632
  7.1 2.8 %x_transform.4 = (s16[1040,128]{1,0:T(8,128)(2,1)S(1)}, s16[1040,128]{1,0:T(8,128)(2,1)S(1)}) custom-call(s32[1]{0:T(128)} %bitcast.target_ref.me_ref, bf16[8,1024,128]{2,1,0:T(8,128)(2,1)S(1)} %bitcast.11, bf16[8,1024,512]{2,1,0:T(8,128)(2,1)S(1)} %copy-done), custom_call_target="tpu_custom_call" | custom-call | flops 2147483648 | bytes 4194304 | tf_op jit(solution)/shard_map/x_transform/pallas_call | solution.py:127
  9.9 0.6 collective-permute-start
  10.4 2.8 %x_transform.5 = (s16[1040,128]{1,0:T(8,128)(2,1)S(1)}, s16[1040,128]{1,0:T(8,128)(2,1)S(1)}) custom-call(s32[1]{0:T(128)} %bitcast.target_ref.me_ref, bf16[8,1024,128]{2,1,0:T(8,128)(2,1)S(1)} %bitcast.12, bf16[8,1024,512]{2,1,0:T(8,128)(2,1)S(1)} %copy-done), custom_call_target="tpu_custom_call" | custom-call | flops 2147483648 | bytes 4194304 | tf_op jit(solution)/shard_map/x_transform/pallas_call | solution.py:127
  13.2 2.6 %collective-permute-start.1 = (s16[1040,128]{1,0:T(8,128)(2,1)S(1)}, s16[1040,128]{1,0:T(8,128)(2,1)S(1)}, u32[]{:S(2)}, u32[]{:S(2)}) collective-permute-start(s16[1040,128]{1,0:T(8,128)(2,1)S(1)} %get-tuple-element.18), channel_id=1, source_target_pairs={{0,8},{4,12},{8,0},{12,4},{16,24},{20,28},{24,16},{28,20},{1,9},{5... | collective-permute-start | bytes 798728 | tf_op jit(solution)/shard_map/ppermute | solution.py:565
  15.8 2.8 %x_transform.6 = (s16[1040,128]{1,0:T(8,128)(2,1)S(1)}, s16[1040,128]{1,0:T(8,128)(2,1)S(1)}) custom-call(s32[1]{0:T(128)} %bitcast.target_ref.me_ref, bf16[8,1024,128]{2,1,0:T(8,128)(2,1)S(1)} %bitcast.13, bf16[8,1024,512]{2,1,0:T(8,128)(2,1)S(1)} %copy-done), custom_call_target="tpu_custom_call" | custom-call | flops 2147483648 | bytes 4194304 | tf_op jit(solution)/shard_map/x_transform/pallas_call | solution.py:127
  18.5 0.2 collective-permute-start.2
  18.7 1.7 %collective-permute-start.3 = (s16[1040,128]{1,0:T(8,128)(2,1)S(1)}, s16[1040,128]{1,0:T(8,128)(2,1)S(1)}, u32[]{:S(2)}, u32[]{:S(2)}) collective-permute-start(s16[1040,128]{1,0:T(8,128)(2,1)S(1)} %get-tuple-element.20), channel_id=1, source_target_pairs={{0,16},{4,20},{8,24},{12,28},{16,0},{20,4},{24,8},{28,12},{1,17},{... | collective-permute-start | bytes 798728 | tf_op jit(solution)/shard_map/ppermute | solution.py:565
  20.4 0.0 collective-permute-start.4
  20.4 2.8 %x_transform.7 = (s16[1040,128]{1,0:T(8,128)(2,1)S(1)}, s16[1040,128]{1,0:T(8,128)(2,1)S(1)}) custom-call(s32[1]{0:T(128)} %bitcast.target_ref.me_ref, bf16[8,1024,128]{2,1,0:T(8,128)(2,1)S(1)} %bitcast.14, bf16[8,1024,512]{2,1,0:T(8,128)(2,1)S(1)} %copy-done), custom_call_target="tpu_custom_call" | custom-call | flops 2147483648 | bytes 4194304 | tf_op jit(solution)/shard_map/x_transform/pallas_call | solution.py:127
  23.2 0.0 collective-permute-done.refs_1_
  23.2 2.6 %collective-permute-start.5 = (s16[1040,128]{1,0:T(8,128)(2,1)S(1)}, s16[1040,128]{1,0:T(8,128)(2,1)S(1)}, u32[]{:S(2)}, u32[]{:S(2)}) collective-permute-start(s16[1040,128]{1,0:T(8,128)(2,1)S(1)} %get-tuple-element.22), channel_id=1, source_target_pairs={{0,24},{4,28},{8,16},{12,20},{16,8},{20,12},{24,0},{28,4},{1,25},{... | collective-permute-start | bytes 798728 | tf_op jit(solution)/shard_map/ppermute | solution.py:565
  25.9 0.0 collective-permute-done.1.refs_2_
  25.9 0.2 collective-permute-start.6
  26.0 2.2 %collective-permute-done.2.refs_3_ = s16[1040,128]{1,0:T(8,128)(2,1)S(1)} collective-permute-done((s16[1040,128]{1,0:T(8,128)(2,1)S(1)}, s16[1040,128]{1,0:T(8,128)(2,1)S(1)}, u32[]{:S(2)}, u32[]{:S(2)}) %collective-permute-start.2) | collective-permute-done | bytes 266272 | tf_op jit(solution)/shard_map/ppermute | solution.py:565
  28.3 0.0 collective-permute-done.3.refs_4_
  28.3 15.5 %collective-permute-done.4.refs_5_ = s16[1040,128]{1,0:T(8,128)(2,1)S(1)} collective-permute-done((s16[1040,128]{1,0:T(8,128)(2,1)S(1)}, s16[1040,128]{1,0:T(8,128)(2,1)S(1)}, u32[]{:S(2)}, u32[]{:S(2)}) %collective-permute-start.4) | collective-permute-done | bytes 266272 | tf_op jit(solution)/shard_map/ppermute | solution.py:565
  43.8 0.0 collective-permute-done.6.refs_7_
  43.8 7.4 %z_transform.1 = (f32[4,4,256,128]{3,2,1,0:T(8,128)S(1)}, s16[1040,128]{1,0:T(8,128)(2,1)S(1)}, s16[1040,128]{1,0:T(8,128)(2,1)S(1)}, f32[8,512,128]{2,1,0:T(8,128)}) custom-call(s32[1]{0:T(128)} %bitcast.target_ref.me_ref, s16[1040,128]{1,0:T(8,128)(2,1)S(1)} %get-tuple-element.16.refs_0_, s16[1040,128]{1,0:T(8,128)(2,1)S(1)} %collective-permute-done.refs_1_, ...), custom_call_target="tpu_custom_call" | custom-call | flops 1610612736 | bytes 6291456 | tf_op jit(solution)/shard_map/z_transform/pallas_call | solution.py:261
  51.2 0.0 copy-start.5
  51.2 0.0 copy-start.1
  51.2 4.4 %all-to-all-start = ((f32[8,128,4,128]{3,2,1,0:T(4,128)}), f32[8,128,4,128]{3,2,1,0:T(4,128)}, u32[]{:S(2)}, u32[]{:S(2)}) async-start(f32[8,128,4,128]{3,2,1,0:T(4,128)} %bitcast.2), calls=%async_computation | async-start | bytes 4194304 | tf_op jit(solution)/shard_map/all_to_all | solution.py:570
  55.6 1.9 %collective-permute-start.7 = (s16[1040,128]{1,0:T(8,128)(2,1)S(1)}, s16[1040,128]{1,0:T(8,128)(2,1)S(1)}, u32[]{:S(2)}, u32[]{:S(2)}) collective-permute-start(s16[1040,128]{1,0:T(8,128)(2,1)S(1)} %get-tuple-element.28), channel_id=1, source_target_pairs={{0,1},{1,2},{2,3},{3,0},{4,5},{5,6},{6,7},{7,4},{8,9},{9,10},{10,1... | collective-permute-start | bytes 798728 | tf_op jit(solution)/shard_map/ppermute | solution.py:568
  57.4 2.1 %collective-permute-start.8 = (s16[1040,128]{1,0:T(8,128)(2,1)S(1)}, s16[1040,128]{1,0:T(8,128)(2,1)S(1)}, u32[]{:S(2)}, u32[]{:S(2)}) collective-permute-start(s16[1040,128]{1,0:T(8,128)(2,1)S(1)} %get-tuple-element.29), channel_id=1, source_target_pairs={{1,0},{2,1},{3,2},{0,3},{5,4},{6,5},{7,6},{4,7},{9,8},{10,9},{11,1... | collective-permute-start | bytes 798728 | tf_op jit(solution)/shard_map/ppermute | solution.py:569
  59.5 0.1 copy.15.coeffs_ref
  59.6 17.1 %render.2 = (f32[8,4,4,128]{3,2,1,0:T(4,128)S(1)}, bf16[512,256]{1,0:T(8,128)(2,1)S(1)}) custom-call(f32[8,4,4]{2,1,0:T(4,128)S(1)} %copy.15.coeffs_ref, s32[8]{0:T(128)S(1)} %copy-done.1, f32[4,4,256,128]{3,2,1,0:T(8,128)S(1)} %get-tuple-element.25.field_ref), custom_call_target="tpu_custom_call" | custom-call | flops 134217728 | bytes 4194304 | tf_op jit(solution)/shard_map/render/pallas_call | solution.py:524
  76.8 17.3 %render.3 = f32[8,4,4,128]{3,2,1,0:T(4,128)} custom-call(f32[8,4,4]{2,1,0:T(4,128)S(1)} %copy.15.coeffs_ref, s32[8]{0:T(128)S(1)} %copy-done.1, f32[4,4,256,128]{3,2,1,0:T(8,128)S(1)} %get-tuple-element.25.field_ref, f32[8,4,4,128]{3,2,1,0:T(4,128)S(1)} %get-tuple-element.26.refs_0_, bf16[512,256]{1,0:T(8,128)(2,1)S(1)} %get-tuple-element.27.refs_1_, ...), custom_call_target="tpu_custom_call" | custom-call | flops 134217728 | bytes 4194304 | tf_op jit(solution)/shard_map/render/pallas_call | solution.py:524
  94.0 0.0 all-to-all-done
  94.0 3.5 %copy_bitcast_fusion = f32[128,4,1024]{2,1,0:T(4,128)} fusion(f32[8,128,4,128]{3,2,1,0:T(4,128)} %all-to-all-done), kind=kLoop, calls=%fused_computation | loop fusion | bytes 4194304 | tf_op jit(solution)/shard_map/reshape | solution.py:573
  (11 shorter events, 0.0 us)
Async XLA Ops:
  3.7 3.4 %copy-start = (bf16[8,1024,512]{2,1,0:T(8,128)(2,1)S(1)}, bf16[8,1024,512]{2,1,0:T(8,128)(2,1)}, u32[]{:S(2)}) copy-start(bf16[8,1024,512]{2,1,0:T(8,128)(2,1)} %constant.14.clone.table_ref) | copy-start | bytes 25165828
  9.9 13.4 %collective-permute-start = (s16[1040,128]{1,0:T(8,128)(2,1)S(1)}, s16[1040,128]{1,0:T(8,128)(2,1)S(1)}, u32[]{:S(2)}, u32[]{:S(2)}) collective-permute-start(s16[1040,128]{1,0:T(8,128)(2,1)S(1)} %get-tuple-element.17), channel_id=1, source_target_pairs={{0,4},{4,0},{8,12},{12,8},{16,20},{20,16},{24,28},{28,24},{1,5},{5... | collective-permute-start | bytes 798728 | tf_op jit(solution)/shard_map/ppermute | solution.py:565
  13.2 12.7 %collective-permute-start.1 = (s16[1040,128]{1,0:T(8,128)(2,1)S(1)}, s16[1040,128]{1,0:T(8,128)(2,1)S(1)}, u32[]{:S(2)}, u32[]{:S(2)}) collective-permute-start(s16[1040,128]{1,0:T(8,128)(2,1)S(1)} %get-tuple-element.18), channel_id=1, source_target_pairs={{0,8},{4,12},{8,0},{12,4},{16,24},{20,28},{24,16},{28,20},{1,9},{5... | collective-permute-start | bytes 798728 | tf_op jit(solution)/shard_map/ppermute | solution.py:565
  18.5 9.8 %collective-permute-start.2 = (s16[1040,128]{1,0:T(8,128)(2,1)S(1)}, s16[1040,128]{1,0:T(8,128)(2,1)S(1)}, u32[]{:S(2)}, u32[]{:S(2)}) collective-permute-start(s16[1040,128]{1,0:T(8,128)(2,1)S(1)} %get-tuple-element.19), channel_id=1, source_target_pairs={{0,12},{4,8},{8,4},{12,0},{16,28},{20,24},{24,20},{28,16},{1,13},{... | collective-permute-start | bytes 798728 | tf_op jit(solution)/shard_map/ppermute | solution.py:565
  18.7 9.6 %collective-permute-start.3 = (s16[1040,128]{1,0:T(8,128)(2,1)S(1)}, s16[1040,128]{1,0:T(8,128)(2,1)S(1)}, u32[]{:S(2)}, u32[]{:S(2)}) collective-permute-start(s16[1040,128]{1,0:T(8,128)(2,1)S(1)} %get-tuple-element.20), channel_id=1, source_target_pairs={{0,16},{4,20},{8,24},{12,28},{16,0},{20,4},{24,8},{28,12},{1,17},{... | collective-permute-start | bytes 798728 | tf_op jit(solution)/shard_map/ppermute | solution.py:565
  20.4 23.3 %copy-start.2 = (f32[3,2,256,128]{3,2,1,0:T(8,128)S(1)}, f32[3,2,256,128]{3,2,1,0:T(8,128)}, u32[]{:S(2)}) copy-start(f32[3,2,256,128]{3,2,1,0:T(8,128)} %constant.17.clone.refs_10_) | copy-start | bytes 2359300
  20.4 23.3 %copy-start.3 = (bf16[256,512]{1,0:T(8,128)(2,1)S(1)}, bf16[256,512]{1,0:T(8,128)(2,1)}, u32[]{:S(2)}) copy-start(bf16[256,512]{1,0:T(8,128)(2,1)} %constant.15.clone.refs_8_) | copy-start | bytes 786436
  20.4 23.4 %copy-start.4 = (bf16[256,512]{1,0:T(8,128)(2,1)S(1)}, bf16[256,512]{1,0:T(8,128)(2,1)}, u32[]{:S(2)}) copy-start(bf16[256,512]{1,0:T(8,128)(2,1)} %constant.16.clone.refs_9_) | copy-start | bytes 786436
  20.4 23.3 %collective-permute-start.4 = (s16[1040,128]{1,0:T(8,128)(2,1)S(1)}, s16[1040,128]{1,0:T(8,128)(2,1)S(1)}, u32[]{:S(2)}, u32[]{:S(2)}) collective-permute-start(s16[1040,128]{1,0:T(8,128)(2,1)S(1)} %get-tuple-element.21), channel_id=1, source_target_pairs={{0,20},{4,16},{8,28},{12,24},{16,4},{20,0},{24,12},{28,8},{1,21},{... | collective-permute-start | bytes 798728 | tf_op jit(solution)/shard_map/ppermute | solution.py:565
  23.2 20.5 %collective-permute-start.5 = (s16[1040,128]{1,0:T(8,128)(2,1)S(1)}, s16[1040,128]{1,0:T(8,128)(2,1)S(1)}, u32[]{:S(2)}, u32[]{:S(2)}) collective-permute-start(s16[1040,128]{1,0:T(8,128)(2,1)S(1)} %get-tuple-element.22), channel_id=1, source_target_pairs={{0,24},{4,28},{8,16},{12,20},{16,8},{20,12},{24,0},{28,4},{1,25},{... | collective-permute-start | bytes 798728 | tf_op jit(solution)/shard_map/ppermute | solution.py:565
  25.9 17.9 %collective-permute-start.6 = (s16[1040,128]{1,0:T(8,128)(2,1)S(1)}, s16[1040,128]{1,0:T(8,128)(2,1)S(1)}, u32[]{:S(2)}, u32[]{:S(2)}) collective-permute-start(s16[1040,128]{1,0:T(8,128)(2,1)S(1)} %get-tuple-element.23), channel_id=1, source_target_pairs={{0,28},{4,24},{8,20},{12,16},{16,12},{20,8},{24,4},{28,0},{1,29},{... | collective-permute-start | bytes 798728 | tf_op jit(solution)/shard_map/ppermute | solution.py:565
  51.2 8.3 %copy-start.5 = (f32[8,4,4]{0,2,1:T(4,128)S(1)}, f32[8,4,4]{0,2,1:T(4,128)}, u32[]{:S(2)}) copy-start(f32[8,4,4]{0,2,1:T(4,128)} %param.8) | copy-start | bytes 1540
  51.2 8.4 %copy-start.1 = (s32[8]{0:T(128)S(1)}, s32[8]{0:T(128)}, u32[]{:S(2)}) copy-start(s32[8]{0:T(128)} %index_ref.3) | copy-start | bytes 100
  51.2 42.8 %all-to-all-start = ((f32[8,128,4,128]{3,2,1,0:T(4,128)}), f32[8,128,4,128]{3,2,1,0:T(4,128)}, u32[]{:S(2)}, u32[]{:S(2)}) async-start(f32[8,128,4,128]{3,2,1,0:T(4,128)} %bitcast.2), calls=%async_computation | async-start | bytes 4194304 | tf_op jit(solution)/shard_map/all_to_all | solution.py:570
  55.6 21.2 %collective-permute-start.7 = (s16[1040,128]{1,0:T(8,128)(2,1)S(1)}, s16[1040,128]{1,0:T(8,128)(2,1)S(1)}, u32[]{:S(2)}, u32[]{:S(2)}) collective-permute-start(s16[1040,128]{1,0:T(8,128)(2,1)S(1)} %get-tuple-element.28), channel_id=1, source_target_pairs={{0,1},{1,2},{2,3},{3,0},{4,5},{5,6},{6,7},{7,4},{8,9},{9,10},{10,1... | collective-permute-start | bytes 798728 | tf_op jit(solution)/shard_map/ppermute | solution.py:568
  57.4 19.4 %collective-permute-start.8 = (s16[1040,128]{1,0:T(8,128)(2,1)S(1)}, s16[1040,128]{1,0:T(8,128)(2,1)S(1)}, u32[]{:S(2)}, u32[]{:S(2)}) collective-permute-start(s16[1040,128]{1,0:T(8,128)(2,1)S(1)} %get-tuple-element.29), channel_id=1, source_target_pairs={{1,0},{2,1},{3,2},{0,3},{5,4},{6,5},{7,6},{4,7},{9,8},{10,9},{11,1... | collective-permute-start | bytes 798728 | tf_op jit(solution)/shard_map/ppermute | solution.py:569

commit v5 on v4

--- a/solution.py
+++ b/solution.py
@@ -23,7 +23,8 @@
 FAINT = 2.0**-9
 SPARSE = 0.02
 TERMS = 16
-VMEM_LIMIT = 24 * 2**20
+VMEM_LIMIT = 14 * 2**20
+RENDER_LIMIT = 14 * 2**20
 LOG2E = 1.4426950408889634
 LN2 = 0.6931471805599453
 
@@ -41,7 +42,7 @@
     cos = (np.cos(angle) / np.sqrt(nx)).reshape(nx, blocks, cols)
     sin = (np.sin(angle) / np.sqrt(nx)).reshape(nx, blocks, cols)
     hi, lo = split_table(np.concatenate([cos, sin], axis=2).transpose(1, 0, 2))
-    return jnp.asarray(np.concatenate([hi, lo], axis=2))
+    return jnp.asarray(np.concatenate([hi, lo], axis=2)[: blocks // RADIX])
 
 
 def z_tables(nz):
@@ -76,12 +77,28 @@
     return jnp.exp2(level * (1.0 / LEVELS)) * (1.0 / STEPS)
 
 
-def x_kernel(planes, target_ref, spec_ref, table_ref, *refs):
+def x_kernel(planes, blocks, pair, target_ref, spec_ref, table_ref, *refs):
     outs, (mixed_ref,) = refs[:-1], refs[-1:]
     half = spec_ref.shape[1] // 2
     rows = half // planes
     cols = table_ref.shape[2] // 4
-    table = table_ref[0]
+    step = jnp.where(pl.program_id(0) == 0, pair[0], pair[1])
+    turns = jnp.bitwise_xor(target_ref[0], step) // (blocks // RADIX)
+    row = lax.broadcasted_iota(jnp.int32, (PACK, cols), 0)
+    phase = (row % RADIX * turns) % RADIX
+    cosine = jnp.where(phase == 0, 1.0, jnp.where(phase == 2, -1.0, 0.0)).astype(jnp.bfloat16)
+    sine = jnp.where(phase == 1, 1.0, jnp.where(phase == 3, -1.0, 0.0)).astype(jnp.bfloat16)
+
+    def turned(at):
+        parts = [
+            table_ref[0, at : at + PACK, part * cols : (part + 1) * cols] for part in range(4)
+        ]
+        made = []
+        for c, s in (parts[:2], parts[2:]):
+            made += [c * cosine - s * sine, c * sine + s * cosine]
+        return jnp.concatenate(made, axis=1)
+
+    table = jnp.concatenate([turned(at) for at in range(0, table_ref.shape[1], PACK)], axis=0)
 
     def product(part):
         own = slice(part * half, (part + 1) * half)
@@ -122,10 +139,10 @@
     sent = (modes + PACK, cols)
 
     def table(d, t):
-        return (jnp.bitwise_xor(t[0], jnp.where(d == 0, pair[0], pair[1])), 0, 0)
+        return (jnp.bitwise_xor(t[0], jnp.where(d == 0, pair[0], pair[1])) % (tiles // RADIX), 0, 0)
 
     return pl.pallas_call(
-        functools.partial(x_kernel, planes),
+        functools.partial(x_kernel, planes, tiles, pair),
         grid_spec=pltpu.PrefetchScalarGridSpec(
             num_scalar_prefetch=1,
             grid=(count,),
@@ -539,7 +556,7 @@
             flops=64 * points, bytes_accessed=4 * 2**20, transcendentals=9 * points
         ),
         name="render",
-        compiler_params=pltpu.CompilerParams(vmem_limit_bytes=VMEM_LIMIT),
+        compiler_params=pltpu.CompilerParams(vmem_limit_bytes=RENDER_LIMIT),
     )(coeffs, index, fields, *edges)
 
 

time: 97.9 us -> 95.9 us (0.980)
  local copies, waits for them, and re-layouts: 10.1 us -> 7.97 us
    unnamed x13, local copies, waits for them, and re-layouts: 3.54 us -> 1.43 us
  transfers between devices with their start and end apart: 10 -> 10, of which waited for: 2 -> 2; matrix products, arithmetic and copies ran while one was open for 0% -> 0% of each run, Pallas kernels for 44% -> 45%
where the time goes in v5:
time: 95.9 us; the launch traced here: 95.6 us
  Pallas kernels  53 us (55%)
  waiting for transfers between devices  17.7 us (18%)
  starting transfers between devices  16.1 us (17%)
  local copies, waits for them, and re-layouts  7.97 us (8%)
    pallas_call x2, Pallas kernels, render(): pl.pallas_call(functools.partial(render_kernel, cells, picked), in_specs=...  34.4 us
    ppermute x7, waiting for transfers between devices, fast_body(): sent[step] = lax.ppermute(block, 'depth', swap) if step else block  17.7 us
    pallas_call x4, Pallas kernels, x_transform(): pl.pallas_call(functools.partial(x_kernel, planes, tiles, pair), grid_spe...  11.2 us
    ppermute x7, starting transfers between devices, fast_body(): sent[step] = lax.ppermute(block, 'depth', swap) if step else block  7.82 us
    pallas_call x1, Pallas kernels, z_transform(): pl.pallas_call(z_kernel, grid=(planes,), in_specs=[pl.BlockSpec(memory_sp...  7.36 us
    all_to_all x1, starting transfers between devices, fast_body(): lax.all_to_all(slabs.reshape(blocks, rows, planes, LANES), 'depth', split...  4.36 us
    reshape x1, local copies, waits for them, and re-layouts, fast_body(): scalar_field = slabs.transpose(1, 2, 0, 3).reshape(rows, planes, nx)  3.51 us
    reshape x2, local copies, waits for them, and re-layouts, fast_body(): spectrum.reshape(2 * rows * planes, blocks, LANES).transpose(1, 0, 2)  3.02 us
  transfers between devices with their start and end apart: 10, of which 2 were waited for; matrix products, arithmetic and copies ran while one was open for 0% of the time, Pallas kernels for 45%

profile of v5, /device:TPU:0, one launch (start us, length us, event | category | flops | bytes accessed | tf_op | source)
XLA Modules:
  0.0 95.6 jit_solution(1419993479583007409)
XLA Ops:
  0.6 2.7 %reshape.13 = bf16[1024,8,128]{2,1,0:T(8,128)(2,1)S(1)} reshape(bf16[2,128,4,1024]{3,2,1,0:T(4,128)(2,1)} %param.7) | data formatting | bytes 4194304 | tf_op jit(solution)/shard_map/reshape | solution.py:576
  3.4 0.0 copy-start.1
  3.4 0.3 copy.19
  3.7 1.3 %copy-done.1 = bf16[2,1024,512]{2,1,0:T(8,128)(2,1)S(1)} copy-done((bf16[2,1024,512]{2,1,0:T(8,128)(2,1)S(1)}, bf16[2,1024,512]{2,1,0:T(8,128)(2,1)}, u32[]{:S(2)}) %copy-start.1) | copy-done | bytes 2097176
  5.0 2.8 %x_transform.4 = (s16[1040,128]{1,0:T(8,128)(2,1)S(1)}, s16[1040,128]{1,0:T(8,128)(2,1)S(1)}) custom-call(s32[1]{0:T(128)} %bitcast.target_ref.me_ref, bf16[8,1024,128]{2,1,0:T(8,128)(2,1)S(1)} %bitcast.11, bf16[2,1024,512]{2,1,0:T(8,128)(2,1)S(1)} %copy-done.1), custom_call_target="tpu_custom_call" | custom-call | flops 2147483648 | bytes 4194304 | tf_op jit(solution)/shard_map/x_transform/pallas_call | solution.py:144
  7.8 0.6 collective-permute-start
  8.4 2.8 %x_transform.5 = (s16[1040,128]{1,0:T(8,128)(2,1)S(1)}, s16[1040,128]{1,0:T(8,128)(2,1)S(1)}) custom-call(s32[1]{0:T(128)} %bitcast.target_ref.me_ref, bf16[8,1024,128]{2,1,0:T(8,128)(2,1)S(1)} %bitcast.12, bf16[2,1024,512]{2,1,0:T(8,128)(2,1)S(1)} %copy-done.1), custom_call_target="tpu_custom_call" | custom-call | flops 2147483648 | bytes 4194304 | tf_op jit(solution)/shard_map/x_transform/pallas_call | solution.py:144
  11.2 2.6 %collective-permute-start.1 = (s16[1040,128]{1,0:T(8,128)(2,1)S(1)}, s16[1040,128]{1,0:T(8,128)(2,1)S(1)}, u32[]{:S(2)}, u32[]{:S(2)}) collective-permute-start(s16[1040,128]{1,0:T(8,128)(2,1)S(1)} %get-tuple-element.18), channel_id=1, source_target_pairs={{0,8},{4,12},{8,0},{12,4},{16,24},{20,28},{24,16},{28,20},{1,9},{5... | collective-permute-start | bytes 798728 | tf_op jit(solution)/shard_map/ppermute | solution.py:582
  13.8 2.8 %x_transform.6 = (s16[1040,128]{1,0:T(8,128)(2,1)S(1)}, s16[1040,128]{1,0:T(8,128)(2,1)S(1)}) custom-call(s32[1]{0:T(128)} %bitcast.target_ref.me_ref, bf16[8,1024,128]{2,1,0:T(8,128)(2,1)S(1)} %bitcast.13, bf16[2,1024,512]{2,1,0:T(8,128)(2,1)S(1)} %copy-done.1), custom_call_target="tpu_custom_call" | custom-call | flops 2147483648 | bytes 4194304 | tf_op jit(solution)/shard_map/x_transform/pallas_call | solution.py:144
  16.6 0.2 collective-permute-start.2
  16.7 1.7 %collective-permute-start.3 = (s16[1040,128]{1,0:T(8,128)(2,1)S(1)}, s16[1040,128]{1,0:T(8,128)(2,1)S(1)}, u32[]{:S(2)}, u32[]{:S(2)}) collective-permute-start(s16[1040,128]{1,0:T(8,128)(2,1)S(1)} %get-tuple-element.20), channel_id=1, source_target_pairs={{0,16},{4,20},{8,24},{12,28},{16,0},{20,4},{24,8},{28,12},{1,17},{... | collective-permute-start | bytes 798728 | tf_op jit(solution)/shard_map/ppermute | solution.py:582
  18.5 0.0 collective-permute-start.4
  18.5 2.8 %x_transform.7 = (s16[1040,128]{1,0:T(8,128)(2,1)S(1)}, s16[1040,128]{1,0:T(8,128)(2,1)S(1)}) custom-call(s32[1]{0:T(128)} %bitcast.target_ref.me_ref, bf16[8,1024,128]{2,1,0:T(8,128)(2,1)S(1)} %bitcast.14, bf16[2,1024,512]{2,1,0:T(8,128)(2,1)S(1)} %copy-done.1), custom_call_target="tpu_custom_call" | custom-call | flops 2147483648 | bytes 4194304 | tf_op jit(solution)/shard_map/x_transform/pallas_call | solution.py:144
  21.3 0.0 collective-permute-done.refs_1_
  21.3 2.6 %collective-permute-start.5 = (s16[1040,128]{1,0:T(8,128)(2,1)S(1)}, s16[1040,128]{1,0:T(8,128)(2,1)S(1)}, u32[]{:S(2)}, u32[]{:S(2)}) collective-permute-start(s16[1040,128]{1,0:T(8,128)(2,1)S(1)} %get-tuple-element.22), channel_id=1, source_target_pairs={{0,24},{4,28},{8,16},{12,20},{16,8},{20,12},{24,0},{28,4},{1,25},{... | collective-permute-start | bytes 798728 | tf_op jit(solution)/shard_map/ppermute | solution.py:582
  24.0 0.0 collective-permute-done.1.refs_2_
  24.0 0.2 collective-permute-start.6
  24.1 2.1 %collective-permute-done.2.refs_3_ = s16[1040,128]{1,0:T(8,128)(2,1)S(1)} collective-permute-done((s16[1040,128]{1,0:T(8,128)(2,1)S(1)}, s16[1040,128]{1,0:T(8,128)(2,1)S(1)}, u32[]{:S(2)}, u32[]{:S(2)}) %collective-permute-start.2) | collective-permute-done | bytes 266272 | tf_op jit(solution)/shard_map/ppermute | solution.py:582
  26.2 0.0 collective-permute-done.3.refs_4_
  26.3 15.6 %collective-permute-done.4.refs_5_ = s16[1040,128]{1,0:T(8,128)(2,1)S(1)} collective-permute-done((s16[1040,128]{1,0:T(8,128)(2,1)S(1)}, s16[1040,128]{1,0:T(8,128)(2,1)S(1)}, u32[]{:S(2)}, u32[]{:S(2)}) %collective-permute-start.4) | collective-permute-done | bytes 266272 | tf_op jit(solution)/shard_map/ppermute | solution.py:582
  41.8 0.0 collective-permute-done.6.refs_7_
  41.9 7.4 %z_transform.1 = (f32[4,4,256,128]{3,2,1,0:T(8,128)S(1)}, s16[1040,128]{1,0:T(8,128)(2,1)S(1)}, s16[1040,128]{1,0:T(8,128)(2,1)S(1)}, f32[8,512,128]{2,1,0:T(8,128)}) custom-call(s32[1]{0:T(128)} %bitcast.target_ref.me_ref, s16[1040,128]{1,0:T(8,128)(2,1)S(1)} %get-tuple-element.16.refs_0_, s16[1040,128]{1,0:T(8,128)(2,1)S(1)} %collective-permute-done.refs_1_, ...), custom_call_target="tpu_custom_call" | custom-call | flops 1610612736 | bytes 6291456 | tf_op jit(solution)/shard_map/z_transform/pallas_call | solution.py:278
  49.2 0.0 copy-start.5
  49.2 0.0 copy-start
  49.2 4.4 %all-to-all-start = ((f32[8,128,4,128]{3,2,1,0:T(4,128)}), f32[8,128,4,128]{3,2,1,0:T(4,128)}, u32[]{:S(2)}, u32[]{:S(2)}) async-start(f32[8,128,4,128]{3,2,1,0:T(4,128)} %bitcast.2), calls=%async_computation | async-start | bytes 4194304 | tf_op jit(solution)/shard_map/all_to_all | solution.py:587
  53.6 1.9 %collective-permute-start.7 = (s16[1040,128]{1,0:T(8,128)(2,1)S(1)}, s16[1040,128]{1,0:T(8,128)(2,1)S(1)}, u32[]{:S(2)}, u32[]{:S(2)}) collective-permute-start(s16[1040,128]{1,0:T(8,128)(2,1)S(1)} %get-tuple-element.28), channel_id=1, source_target_pairs={{0,1},{1,2},{2,3},{3,0},{4,5},{5,6},{6,7},{7,4},{8,9},{9,10},{10,1... | collective-permute-start | bytes 798728 | tf_op jit(solution)/shard_map/ppermute | solution.py:585
  55.5 2.1 %collective-permute-start.8 = (s16[1040,128]{1,0:T(8,128)(2,1)S(1)}, s16[1040,128]{1,0:T(8,128)(2,1)S(1)}, u32[]{:S(2)}, u32[]{:S(2)}) collective-permute-start(s16[1040,128]{1,0:T(8,128)(2,1)S(1)} %get-tuple-element.29), channel_id=1, source_target_pairs={{1,0},{2,1},{3,2},{0,3},{5,4},{6,5},{7,6},{4,7},{9,8},{10,9},{11,1... | collective-permute-start | bytes 798728 | tf_op jit(solution)/shard_map/ppermute | solution.py:586
  57.6 0.1 copy.15.coeffs_ref
  57.7 17.1 %render.2 = (f32[8,4,4,128]{3,2,1,0:T(4,128)S(1)}, bf16[512,256]{1,0:T(8,128)(2,1)S(1)}) custom-call(f32[8,4,4]{2,1,0:T(4,128)S(1)} %copy.15.coeffs_ref, s32[8]{0:T(128)S(1)} %copy-done, f32[4,4,256,128]{3,2,1,0:T(8,128)S(1)} %get-tuple-element.25.field_ref), custom_call_target="tpu_custom_call" | custom-call | flops 134217728 | bytes 4194304 | tf_op jit(solution)/shard_map/render/pallas_call | solution.py:541
  74.8 0.0 collective-permute-done.7.refs_2_
  74.8 17.2 %render.3 = f32[8,4,4,128]{3,2,1,0:T(4,128)} custom-call(f32[8,4,4]{2,1,0:T(4,128)S(1)} %copy.15.coeffs_ref, s32[8]{0:T(128)S(1)} %copy-done, f32[4,4,256,128]{3,2,1,0:T(8,128)S(1)} %get-tuple-element.25.field_ref, f32[8,4,4,128]{3,2,1,0:T(4,128)S(1)} %get-tuple-element.26.refs_0_, bf16[512,256]{1,0:T(8,128)(2,1)S(1)} %get-tuple-element.27.refs_1_, ...), custom_call_target="tpu_custom_call" | custom-call | flops 134217728 | bytes 4194304 | tf_op jit(solution)/shard_map/render/pallas_call | solution.py:541
  92.1 3.5 %copy_bitcast_fusion = f32[128,4,1024]{2,1,0:T(4,128)} fusion(f32[8,128,4,128]{3,2,1,0:T(4,128)} %all-to-all-done), kind=kLoop, calls=%fused_computation | loop fusion | bytes 4194304 | tf_op jit(solution)/shard_map/reshape | solution.py:590
  (11 shorter events, 0.0 us)
Async XLA Ops:
  3.4 1.6 %copy-start.1 = (bf16[2,1024,512]{2,1,0:T(8,128)(2,1)S(1)}, bf16[2,1024,512]{2,1,0:T(8,128)(2,1)}, u32[]{:S(2)}) copy-start(bf16[2,1024,512]{2,1,0:T(8,128)(2,1)} %constant.14.clone.table_ref) | copy-start | bytes 6291460
  7.8 13.5 %collective-permute-start = (s16[1040,128]{1,0:T(8,128)(2,1)S(1)}, s16[1040,128]{1,0:T(8,128)(2,1)S(1)}, u32[]{:S(2)}, u32[]{:S(2)}) collective-permute-start(s16[1040,128]{1,0:T(8,128)(2,1)S(1)} %get-tuple-element.17), channel_id=1, source_target_pairs={{0,4},{4,0},{8,12},{12,8},{16,20},{20,16},{24,28},{28,24},{1,5},{5... | collective-permute-start | bytes 798728 | tf_op jit(solution)/shard_map/ppermute | solution.py:582
  11.2 12.8 %collective-permute-start.1 = (s16[1040,128]{1,0:T(8,128)(2,1)S(1)}, s16[1040,128]{1,0:T(8,128)(2,1)S(1)}, u32[]{:S(2)}, u32[]{:S(2)}) collective-permute-start(s16[1040,128]{1,0:T(8,128)(2,1)S(1)} %get-tuple-element.18), channel_id=1, source_target_pairs={{0,8},{4,12},{8,0},{12,4},{16,24},{20,28},{24,16},{28,20},{1,9},{5... | collective-permute-start | bytes 798728 | tf_op jit(solution)/shard_map/ppermute | solution.py:582
  16.6 9.7 %collective-permute-start.2 = (s16[1040,128]{1,0:T(8,128)(2,1)S(1)}, s16[1040,128]{1,0:T(8,128)(2,1)S(1)}, u32[]{:S(2)}, u32[]{:S(2)}) collective-permute-start(s16[1040,128]{1,0:T(8,128)(2,1)S(1)} %get-tuple-element.19), channel_id=1, source_target_pairs={{0,12},{4,8},{8,4},{12,0},{16,28},{20,24},{24,20},{28,16},{1,13},{... | collective-permute-start | bytes 798728 | tf_op jit(solution)/shard_map/ppermute | solution.py:582
  16.7 9.5 %collective-permute-start.3 = (s16[1040,128]{1,0:T(8,128)(2,1)S(1)}, s16[1040,128]{1,0:T(8,128)(2,1)S(1)}, u32[]{:S(2)}, u32[]{:S(2)}) collective-permute-start(s16[1040,128]{1,0:T(8,128)(2,1)S(1)} %get-tuple-element.20), channel_id=1, source_target_pairs={{0,16},{4,20},{8,24},{12,28},{16,0},{20,4},{24,8},{28,12},{1,17},{... | collective-permute-start | bytes 798728 | tf_op jit(solution)/shard_map/ppermute | solution.py:582
  18.5 23.3 %copy-start.2 = (f32[3,2,256,128]{3,2,1,0:T(8,128)S(1)}, f32[3,2,256,128]{3,2,1,0:T(8,128)}, u32[]{:S(2)}) copy-start(f32[3,2,256,128]{3,2,1,0:T(8,128)} %constant.17.clone.refs_10_) | copy-start | bytes 2359300
  18.5 23.4 %copy-start.3 = (bf16[256,512]{1,0:T(8,128)(2,1)S(1)}, bf16[256,512]{1,0:T(8,128)(2,1)}, u32[]{:S(2)}) copy-start(bf16[256,512]{1,0:T(8,128)(2,1)} %constant.15.clone.refs_8_) | copy-start | bytes 786436
  18.5 23.4 %copy-start.4 = (bf16[256,512]{1,0:T(8,128)(2,1)S(1)}, bf16[256,512]{1,0:T(8,128)(2,1)}, u32[]{:S(2)}) copy-start(bf16[256,512]{1,0:T(8,128)(2,1)} %constant.16.clone.refs_9_) | copy-start | bytes 786436
  18.5 23.3 %collective-permute-start.4 = (s16[1040,128]{1,0:T(8,128)(2,1)S(1)}, s16[1040,128]{1,0:T(8,128)(2,1)S(1)}, u32[]{:S(2)}, u32[]{:S(2)}) collective-permute-start(s16[1040,128]{1,0:T(8,128)(2,1)S(1)} %get-tuple-element.21), channel_id=1, source_target_pairs={{0,20},{4,16},{8,28},{12,24},{16,4},{20,0},{24,12},{28,8},{1,21},{... | collective-permute-start | bytes 798728 | tf_op jit(solution)/shard_map/ppermute | solution.py:582
  21.3 20.5 %collective-permute-start.5 = (s16[1040,128]{1,0:T(8,128)(2,1)S(1)}, s16[1040,128]{1,0:T(8,128)(2,1)S(1)}, u32[]{:S(2)}, u32[]{:S(2)}) collective-permute-start(s16[1040,128]{1,0:T(8,128)(2,1)S(1)} %get-tuple-element.22), channel_id=1, source_target_pairs={{0,24},{4,28},{8,16},{12,20},{16,8},{20,12},{24,0},{28,4},{1,25},{... | collective-permute-start | bytes 798728 | tf_op jit(solution)/shard_map/ppermute | solution.py:582
  24.0 17.9 %collective-permute-start.6 = (s16[1040,128]{1,0:T(8,128)(2,1)S(1)}, s16[1040,128]{1,0:T(8,128)(2,1)S(1)}, u32[]{:S(2)}, u32[]{:S(2)}) collective-permute-start(s16[1040,128]{1,0:T(8,128)(2,1)S(1)} %get-tuple-element.23), channel_id=1, source_target_pairs={{0,28},{4,24},{8,20},{12,16},{16,12},{20,8},{24,4},{28,0},{1,29},{... | collective-permute-start | bytes 798728 | tf_op jit(solution)/shard_map/ppermute | solution.py:582
  49.2 8.3 %copy-start.5 = (f32[8,4,4]{0,2,1:T(4,128)S(1)}, f32[8,4,4]{0,2,1:T(4,128)}, u32[]{:S(2)}) copy-start(f32[8,4,4]{0,2,1:T(4,128)} %param.8) | copy-start | bytes 1540
  49.2 8.4 %copy-start = (s32[8]{0:T(128)S(1)}, s32[8]{0:T(128)}, u32[]{:S(2)}) copy-start(s32[8]{0:T(128)} %index_ref.3) | copy-start | bytes 100
  49.2 42.8 %all-to-all-start = ((f32[8,128,4,128]{3,2,1,0:T(4,128)}), f32[8,128,4,128]{3,2,1,0:T(4,128)}, u32[]{:S(2)}, u32[]{:S(2)}) async-start(f32[8,128,4,128]{3,2,1,0:T(4,128)} %bitcast.2), calls=%async_computation | async-start | bytes 4194304 | tf_op jit(solution)/shard_map/all_to_all | solution.py:587
  53.6 21.2 %collective-permute-start.7 = (s16[1040,128]{1,0:T(8,128)(2,1)S(1)}, s16[1040,128]{1,0:T(8,128)(2,1)S(1)}, u32[]{:S(2)}, u32[]{:S(2)}) collective-permute-start(s16[1040,128]{1,0:T(8,128)(2,1)S(1)} %get-tuple-element.28), channel_id=1, source_target_pairs={{0,1},{1,2},{2,3},{3,0},{4,5},{5,6},{6,7},{7,4},{8,9},{9,10},{10,1... | collective-permute-start | bytes 798728 | tf_op jit(solution)/shard_map/ppermute | solution.py:585
  55.5 19.3 %collective-permute-start.8 = (s16[1040,128]{1,0:T(8,128)(2,1)S(1)}, s16[1040,128]{1,0:T(8,128)(2,1)S(1)}, u32[]{:S(2)}, u32[]{:S(2)}) collective-permute-start(s16[1040,128]{1,0:T(8,128)(2,1)S(1)} %get-tuple-element.29), channel_id=1, source_target_pairs={{1,0},{2,1},{3,2},{0,3},{5,4},{6,5},{7,6},{4,7},{9,8},{10,9},{11,1... | collective-permute-start | bytes 798728 | tf_op jit(solution)/shard_map/ppermute | solution.py:586

commit v6 on v5

--- a/solution.py
+++ b/solution.py
@@ -16,7 +16,7 @@
 SEGS = 8
 RADIX = 4
 PACK = 16
-PAIRS = ((6, 7), (2, 4), (3, 5), (1, 0))
+PAIRS = ((6, 7), (2, 3), (4, 5), (1, 0))
 LEVELS = 16.0
 STEPS = 32766.0
 TINY = 2.0**-108
@@ -147,7 +147,7 @@
             num_scalar_prefetch=1,
             grid=(count,),
             in_specs=[
-                pl.BlockSpec(spec.shape, lambda d, t: (0, 0, 0)),
+                pl.BlockSpec(memory_space=pltpu.VMEM),
                 pl.BlockSpec((1, nx, wide), table),
             ],
             out_specs=[pl.BlockSpec(sent, lambda d, t: (0, 0))] * count,
@@ -331,7 +331,7 @@
 
 
 def render_kernel(cells, picked, coeffs_ref, index_ref, field_ref, *refs):
-    first = len(refs) == 11
+    first = len(refs) == 10
     if first:
         out_ref, table_ref, *refs = refs
     else:
@@ -339,14 +339,11 @@
         refs = refs[6:]
         before_ref, after_ref = edge_ref.at[0], edge_ref.at[1]
         out_ref[...] = done_ref[...]
-    kept_ref, light_ref, lhs_ref, state_ref, sem, *refs = refs
+    light_ref, lhs_ref, state_ref, sem, *refs = refs
     banks = (refs[0:2], refs[2:4])
-    loads = [pltpu.make_async_copy(field_ref, kept_ref, sem.at[0])]
-    if not first:
-        loads.append(pltpu.make_async_copy(table_ref, lhs_ref, sem.at[1]))
+    loads = [] if first else [pltpu.make_async_copy(table_ref, lhs_ref, sem.at[0])]
     for load in loads:
         load.start()
-    field_ref = kept_ref
     steps = field_ref.shape[2] // SEGS
     images = index_ref.shape[0]
     last = field_ref.shape[0] - 1
@@ -540,16 +537,15 @@
     first = not edges
     return pl.pallas_call(
         functools.partial(render_kernel, cells, picked),
-        in_specs=[smem, smem, any_space] + ([] if first else [vmem, any_space, vmem, vmem]),
+        in_specs=[smem, smem, vmem] + ([] if first else [vmem, any_space, vmem, vmem]),
         out_specs=[vmem, vmem] if first else vmem,
         out_shape=[picture, jax.ShapeDtypeStruct(table, jnp.bfloat16)] if first else picture,
         scratch_shapes=([] if first else [pltpu.VMEM((2, *fields.shape[1:]), jnp.float32)])
         + [
-            pltpu.VMEM(fields.shape, jnp.float32),
             pltpu.VMEM((len(picked), *fields.shape[1:]), jnp.float32),
             pltpu.VMEM(table, jnp.bfloat16),
             pltpu.VMEM((images, len(picked), 4, SEGS, LANES), jnp.float32),
-            pltpu.SemaphoreType.DMA((2,)),
+            pltpu.SemaphoreType.DMA((1,)),
         ]
         + [pltpu.VMEM(poly, jnp.float32)] * 4,
         cost_estimate=pl.CostEstimate(

time: 95.9 us -> 95.6 us (level)
  no operation moved by 1% of the time
where the time goes in v6:
time: 95.6 us; the launch traced here: 95.3 us
  Pallas kernels  52.7 us (55%)
  waiting for transfers between devices  17.7 us (19%)
  starting transfers between devices  16.2 us (17%)
  local copies, waits for them, and re-layouts  7.97 us (8%)
    pallas_call x2, Pallas kernels, render(): pl.pallas_call(functools.partial(render_kernel, cells, picked), in_specs=...  34.1 us
    ppermute x7, waiting for transfers between devices, fast_body(): sent[step] = lax.ppermute(block, 'depth', swap) if step else block  17.7 us
    pallas_call x4, Pallas kernels, x_transform(): pl.pallas_call(functools.partial(x_kernel, planes, tiles, pair), grid_spe...  11.2 us
    ppermute x7, starting transfers between devices, fast_body(): sent[step] = lax.ppermute(block, 'depth', swap) if step else block  7.85 us
    pallas_call x1, Pallas kernels, z_transform(): pl.pallas_call(z_kernel, grid=(planes,), in_specs=[pl.BlockSpec(memory_sp...  7.36 us
    all_to_all x1, starting transfers between devices, fast_body(): lax.all_to_all(slabs.reshape(blocks, rows, planes, LANES), 'depth', split...  4.36 us
    reshape x1, local copies, waits for them, and re-layouts, fast_body(): scalar_field = slabs.transpose(1, 2, 0, 3).reshape(rows, planes, nx)  3.51 us
    reshape x2, local copies, waits for them, and re-layouts, fast_body(): spectrum.reshape(2 * rows * planes, blocks, LANES).transpose(1, 0, 2)  3.02 us
  transfers between devices with their start and end apart: 10, of which 2 were waited for; matrix products, arithmetic and copies ran while one was open for 0% of the time, Pallas kernels for 45%

profile of v6, /device:TPU:0, one launch (start us, length us, event | category | flops | bytes accessed | tf_op | source)
XLA Modules:
  0.0 95.3 jit_solution(11933237401723981898)
XLA Ops:
  0.6 2.7 %reshape.13 = bf16[1024,8,128]{2,1,0:T(8,128)(2,1)S(1)} reshape(bf16[2,128,4,1024]{3,2,1,0:T(4,128)(2,1)} %param.7) | data formatting | bytes 4194304 | tf_op jit(solution)/shard_map/reshape | solution.py:572
  3.4 0.0 copy-start.1
  3.4 0.3 copy.19
  3.7 1.3 %copy-done.1 = bf16[2,1024,512]{2,1,0:T(8,128)(2,1)S(1)} copy-done((bf16[2,1024,512]{2,1,0:T(8,128)(2,1)S(1)}, bf16[2,1024,512]{2,1,0:T(8,128)(2,1)}, u32[]{:S(2)}) %copy-start.1) | copy-done | bytes 2097176
  5.0 2.8 %x_transform.4 = (s16[1040,128]{1,0:T(8,128)(2,1)S(1)}, s16[1040,128]{1,0:T(8,128)(2,1)S(1)}) custom-call(s32[1]{0:T(128)} %bitcast.target_ref.me_ref, bf16[8,1024,128]{2,1,0:T(8,128)(2,1)S(1)} %bitcast.11, bf16[2,1024,512]{2,1,0:T(8,128)(2,1)S(1)} %copy-done.1), custom_call_target="tpu_custom_call" | custom-call | flops 2147483648 | bytes 4194304 | tf_op jit(solution)/shard_map/x_transform/pallas_call | solution.py:144
  7.8 0.6 collective-permute-start
  8.4 2.8 %x_transform.5 = (s16[1040,128]{1,0:T(8,128)(2,1)S(1)}, s16[1040,128]{1,0:T(8,128)(2,1)S(1)}) custom-call(s32[1]{0:T(128)} %bitcast.target_ref.me_ref, bf16[8,1024,128]{2,1,0:T(8,128)(2,1)S(1)} %bitcast.12, bf16[2,1024,512]{2,1,0:T(8,128)(2,1)S(1)} %copy-done.1), custom_call_target="tpu_custom_call" | custom-call | flops 2147483648 | bytes 4194304 | tf_op jit(solution)/shard_map/x_transform/pallas_call | solution.py:144
  11.2 2.6 %collective-permute-start.1 = (s16[1040,128]{1,0:T(8,128)(2,1)S(1)}, s16[1040,128]{1,0:T(8,128)(2,1)S(1)}, u32[]{:S(2)}, u32[]{:S(2)}) collective-permute-start(s16[1040,128]{1,0:T(8,128)(2,1)S(1)} %get-tuple-element.18), channel_id=1, source_target_pairs={{0,8},{4,12},{8,0},{12,4},{16,24},{20,28},{24,16},{28,20},{1,9},{5... | collective-permute-start | bytes 798728 | tf_op jit(solution)/shard_map/ppermute | solution.py:578
  13.8 0.1 collective-permute-start.2
  13.9 2.8 %x_transform.6 = (s16[1040,128]{1,0:T(8,128)(2,1)S(1)}, s16[1040,128]{1,0:T(8,128)(2,1)S(1)}) custom-call(s32[1]{0:T(128)} %bitcast.target_ref.me_ref, bf16[8,1024,128]{2,1,0:T(8,128)(2,1)S(1)} %bitcast.13, bf16[2,1024,512]{2,1,0:T(8,128)(2,1)S(1)} %copy-done.1), custom_call_target="tpu_custom_call" | custom-call | flops 2147483648 | bytes 4194304 | tf_op jit(solution)/shard_map/x_transform/pallas_call | solution.py:144
  16.7 1.8 %collective-permute-start.3 = (s16[1040,128]{1,0:T(8,128)(2,1)S(1)}, s16[1040,128]{1,0:T(8,128)(2,1)S(1)}, u32[]{:S(2)}, u32[]{:S(2)}) collective-permute-start(s16[1040,128]{1,0:T(8,128)(2,1)S(1)} %get-tuple-element.20), channel_id=1, source_target_pairs={{0,16},{4,20},{8,24},{12,28},{16,0},{20,4},{24,8},{28,12},{1,17},{... | collective-permute-start | bytes 798728 | tf_op jit(solution)/shard_map/ppermute | solution.py:578
  18.5 0.0 collective-permute-start.4
  18.5 2.8 %x_transform.7 = (s16[1040,128]{1,0:T(8,128)(2,1)S(1)}, s16[1040,128]{1,0:T(8,128)(2,1)S(1)}) custom-call(s32[1]{0:T(128)} %bitcast.target_ref.me_ref, bf16[8,1024,128]{2,1,0:T(8,128)(2,1)S(1)} %bitcast.14, bf16[2,1024,512]{2,1,0:T(8,128)(2,1)S(1)} %copy-done.1), custom_call_target="tpu_custom_call" | custom-call | flops 2147483648 | bytes 4194304 | tf_op jit(solution)/shard_map/x_transform/pallas_call | solution.py:144
  21.3 0.0 collective-permute-done.refs_1_
  21.3 2.6 %collective-permute-start.5 = (s16[1040,128]{1,0:T(8,128)(2,1)S(1)}, s16[1040,128]{1,0:T(8,128)(2,1)S(1)}, u32[]{:S(2)}, u32[]{:S(2)}) collective-permute-start(s16[1040,128]{1,0:T(8,128)(2,1)S(1)} %get-tuple-element.22), channel_id=1, source_target_pairs={{0,24},{4,28},{8,16},{12,20},{16,8},{20,12},{24,0},{28,4},{1,25},{... | collective-permute-start | bytes 798728 | tf_op jit(solution)/shard_map/ppermute | solution.py:578
  24.0 0.0 collective-permute-done.1.refs_2_
  24.0 0.1 collective-permute-start.6
  24.1 2.1 %collective-permute-done.2.refs_3_ = s16[1040,128]{1,0:T(8,128)(2,1)S(1)} collective-permute-done((s16[1040,128]{1,0:T(8,128)(2,1)S(1)}, s16[1040,128]{1,0:T(8,128)(2,1)S(1)}, u32[]{:S(2)}, u32[]{:S(2)}) %collective-permute-start.2) | collective-permute-done | bytes 266272 | tf_op jit(solution)/shard_map/ppermute | solution.py:578
  26.3 15.5 %collective-permute-done.4.refs_5_ = s16[1040,128]{1,0:T(8,128)(2,1)S(1)} collective-permute-done((s16[1040,128]{1,0:T(8,128)(2,1)S(1)}, s16[1040,128]{1,0:T(8,128)(2,1)S(1)}, u32[]{:S(2)}, u32[]{:S(2)}) %collective-permute-start.4) | collective-permute-done | bytes 266272 | tf_op jit(solution)/shard_map/ppermute | solution.py:578
  41.8 0.0 collective-permute-done.6.refs_7_
  41.8 7.4 %z_transform.1 = (f32[4,4,256,128]{3,2,1,0:T(8,128)S(1)}, s16[1040,128]{1,0:T(8,128)(2,1)S(1)}, s16[1040,128]{1,0:T(8,128)(2,1)S(1)}, f32[8,512,128]{2,1,0:T(8,128)}) custom-call(s32[1]{0:T(128)} %bitcast.target_ref.me_ref, s16[1040,128]{1,0:T(8,128)(2,1)S(1)} %get-tuple-element.16.refs_0_, s16[1040,128]{1,0:T(8,128)(2,1)S(1)} %collective-permute-done.refs_1_, ...), custom_call_target="tpu_custom_call" | custom-call | flops 1610612736 | bytes 6291456 | tf_op jit(solution)/shard_map/z_transform/pallas_call | solution.py:278
  49.2 0.0 copy-start.5
  49.2 0.0 copy-start
  49.2 4.4 %all-to-all-start = ((f32[8,128,4,128]{3,2,1,0:T(4,128)}), f32[8,128,4,128]{3,2,1,0:T(4,128)}, u32[]{:S(2)}, u32[]{:S(2)}) async-start(f32[8,128,4,128]{3,2,1,0:T(4,128)} %bitcast.2), calls=%async_computation | async-start | bytes 4194304 | tf_op jit(solution)/shard_map/all_to_all | solution.py:583
  53.6 1.9 %collective-permute-start.7 = (s16[1040,128]{1,0:T(8,128)(2,1)S(1)}, s16[1040,128]{1,0:T(8,128)(2,1)S(1)}, u32[]{:S(2)}, u32[]{:S(2)}) collective-permute-start(s16[1040,128]{1,0:T(8,128)(2,1)S(1)} %get-tuple-element.28), channel_id=1, source_target_pairs={{0,1},{1,2},{2,3},{3,0},{4,5},{5,6},{6,7},{7,4},{8,9},{9,10},{10,1... | collective-permute-start | bytes 798728 | tf_op jit(solution)/shard_map/ppermute | solution.py:581
  55.5 2.1 %collective-permute-start.8 = (s16[1040,128]{1,0:T(8,128)(2,1)S(1)}, s16[1040,128]{1,0:T(8,128)(2,1)S(1)}, u32[]{:S(2)}, u32[]{:S(2)}) collective-permute-start(s16[1040,128]{1,0:T(8,128)(2,1)S(1)} %get-tuple-element.29), channel_id=1, source_target_pairs={{1,0},{2,1},{3,2},{0,3},{5,4},{6,5},{7,6},{4,7},{9,8},{10,9},{11,1... | collective-permute-start | bytes 798728 | tf_op jit(solution)/shard_map/ppermute | solution.py:582
  57.6 0.1 copy.15.coeffs_ref
  57.7 17.0 %render.2 = (f32[8,4,4,128]{3,2,1,0:T(4,128)S(1)}, bf16[512,256]{1,0:T(8,128)(2,1)S(1)}) custom-call(f32[8,4,4]{2,1,0:T(4,128)S(1)} %copy.15.coeffs_ref, s32[8]{0:T(128)S(1)} %copy-done, f32[4,4,256,128]{3,2,1,0:T(8,128)S(1)} %get-tuple-element.25.field_ref), custom_call_target="tpu_custom_call" | custom-call | flops 134217728 | bytes 4194304 | tf_op jit(solution)/shard_map/render/pallas_call | solution.py:538
  74.7 0.0 collective-permute-done.7.refs_2_
  74.7 0.0 collective-permute-done.8.refs_3_
  74.7 17.1 %render.3 = f32[8,4,4,128]{3,2,1,0:T(4,128)} custom-call(f32[8,4,4]{2,1,0:T(4,128)S(1)} %copy.15.coeffs_ref, s32[8]{0:T(128)S(1)} %copy-done, f32[4,4,256,128]{3,2,1,0:T(8,128)S(1)} %get-tuple-element.25.field_ref, f32[8,4,4,128]{3,2,1,0:T(4,128)S(1)} %get-tuple-element.26.refs_0_, bf16[512,256]{1,0:T(8,128)(2,1)S(1)} %get-tuple-element.27.refs_1_, ...), custom_call_target="tpu_custom_call" | custom-call | flops 134217728 | bytes 4194304 | tf_op jit(solution)/shard_map/render/pallas_call | solution.py:538
  91.8 3.5 %copy_bitcast_fusion = f32[128,4,1024]{2,1,0:T(4,128)} fusion(f32[8,128,4,128]{3,2,1,0:T(4,128)} %all-to-all-done), kind=kLoop, calls=%fused_computation | loop fusion | bytes 4194304 | tf_op jit(solution)/shard_map/reshape | solution.py:586
  (11 shorter events, 0.0 us)
Async XLA Ops:
  3.4 1.6 %copy-start.1 = (bf16[2,1024,512]{2,1,0:T(8,128)(2,1)S(1)}, bf16[2,1024,512]{2,1,0:T(8,128)(2,1)}, u32[]{:S(2)}) copy-start(bf16[2,1024,512]{2,1,0:T(8,128)(2,1)} %constant.14.clone.table_ref) | copy-start | bytes 6291460
  7.8 13.5 %collective-permute-start = (s16[1040,128]{1,0:T(8,128)(2,1)S(1)}, s16[1040,128]{1,0:T(8,128)(2,1)S(1)}, u32[]{:S(2)}, u32[]{:S(2)}) collective-permute-start(s16[1040,128]{1,0:T(8,128)(2,1)S(1)} %get-tuple-element.17), channel_id=1, source_target_pairs={{0,4},{4,0},{8,12},{12,8},{16,20},{20,16},{24,28},{28,24},{1,5},{5... | collective-permute-start | bytes 798728 | tf_op jit(solution)/shard_map/ppermute | solution.py:578
  11.2 12.8 %collective-permute-start.1 = (s16[1040,128]{1,0:T(8,128)(2,1)S(1)}, s16[1040,128]{1,0:T(8,128)(2,1)S(1)}, u32[]{:S(2)}, u32[]{:S(2)}) collective-permute-start(s16[1040,128]{1,0:T(8,128)(2,1)S(1)} %get-tuple-element.18), channel_id=1, source_target_pairs={{0,8},{4,12},{8,0},{12,4},{16,24},{20,28},{24,16},{28,20},{1,9},{5... | collective-permute-start | bytes 798728 | tf_op jit(solution)/shard_map/ppermute | solution.py:578
  13.8 12.5 %collective-permute-start.2 = (s16[1040,128]{1,0:T(8,128)(2,1)S(1)}, s16[1040,128]{1,0:T(8,128)(2,1)S(1)}, u32[]{:S(2)}, u32[]{:S(2)}) collective-permute-start(s16[1040,128]{1,0:T(8,128)(2,1)S(1)} %get-tuple-element.19), channel_id=1, source_target_pairs={{0,12},{4,8},{8,4},{12,0},{16,28},{20,24},{24,20},{28,16},{1,13},{... | collective-permute-start | bytes 798728 | tf_op jit(solution)/shard_map/ppermute | solution.py:578
  16.7 9.5 %collective-permute-start.3 = (s16[1040,128]{1,0:T(8,128)(2,1)S(1)}, s16[1040,128]{1,0:T(8,128)(2,1)S(1)}, u32[]{:S(2)}, u32[]{:S(2)}) collective-permute-start(s16[1040,128]{1,0:T(8,128)(2,1)S(1)} %get-tuple-element.20), channel_id=1, source_target_pairs={{0,16},{4,20},{8,24},{12,28},{16,0},{20,4},{24,8},{28,12},{1,17},{... | collective-permute-start | bytes 798728 | tf_op jit(solution)/shard_map/ppermute | solution.py:578
  18.5 23.3 %copy-start.2 = (f32[3,2,256,128]{3,2,1,0:T(8,128)S(1)}, f32[3,2,256,128]{3,2,1,0:T(8,128)}, u32[]{:S(2)}) copy-start(f32[3,2,256,128]{3,2,1,0:T(8,128)} %constant.17.clone.refs_10_) | copy-start | bytes 2359300
  18.5 23.3 %copy-start.3 = (bf16[256,512]{1,0:T(8,128)(2,1)S(1)}, bf16[256,512]{1,0:T(8,128)(2,1)}, u32[]{:S(2)}) copy-start(bf16[256,512]{1,0:T(8,128)(2,1)} %constant.15.clone.refs_8_) | copy-start | bytes 786436
  18.5 23.3 %copy-start.4 = (bf16[256,512]{1,0:T(8,128)(2,1)S(1)}, bf16[256,512]{1,0:T(8,128)(2,1)}, u32[]{:S(2)}) copy-start(bf16[256,512]{1,0:T(8,128)(2,1)} %constant.16.clone.refs_9_) | copy-start | bytes 786436
  18.5 23.3 %collective-permute-start.4 = (s16[1040,128]{1,0:T(8,128)(2,1)S(1)}, s16[1040,128]{1,0:T(8,128)(2,1)S(1)}, u32[]{:S(2)}, u32[]{:S(2)}) collective-permute-start(s16[1040,128]{1,0:T(8,128)(2,1)S(1)} %get-tuple-element.21), channel_id=1, source_target_pairs={{0,20},{4,16},{8,28},{12,24},{16,4},{20,0},{24,12},{28,8},{1,21},{... | collective-permute-start | bytes 798728 | tf_op jit(solution)/shard_map/ppermute | solution.py:578
  21.3 20.4 %collective-permute-start.5 = (s16[1040,128]{1,0:T(8,128)(2,1)S(1)}, s16[1040,128]{1,0:T(8,128)(2,1)S(1)}, u32[]{:S(2)}, u32[]{:S(2)}) collective-permute-start(s16[1040,128]{1,0:T(8,128)(2,1)S(1)} %get-tuple-element.22), channel_id=1, source_target_pairs={{0,24},{4,28},{8,16},{12,20},{16,8},{20,12},{24,0},{28,4},{1,25},{... | collective-permute-start | bytes 798728 | tf_op jit(solution)/shard_map/ppermute | solution.py:578
  24.0 17.8 %collective-permute-start.6 = (s16[1040,128]{1,0:T(8,128)(2,1)S(1)}, s16[1040,128]{1,0:T(8,128)(2,1)S(1)}, u32[]{:S(2)}, u32[]{:S(2)}) collective-permute-start(s16[1040,128]{1,0:T(8,128)(2,1)S(1)} %get-tuple-element.23), channel_id=1, source_target_pairs={{0,28},{4,24},{8,20},{12,16},{16,12},{20,8},{24,4},{28,0},{1,29},{... | collective-permute-start | bytes 798728 | tf_op jit(solution)/shard_map/ppermute | solution.py:578
  49.2 8.4 %copy-start.5 = (f32[8,4,4]{0,2,1:T(4,128)S(1)}, f32[8,4,4]{0,2,1:T(4,128)}, u32[]{:S(2)}) copy-start(f32[8,4,4]{0,2,1:T(4,128)} %param.8) | copy-start | bytes 1540
  49.2 8.5 %copy-start = (s32[8]{0:T(128)S(1)}, s32[8]{0:T(128)}, u32[]{:S(2)}) copy-start(s32[8]{0:T(128)} %index_ref.3) | copy-start | bytes 100
  49.2 42.6 %all-to-all-start = ((f32[8,128,4,128]{3,2,1,0:T(4,128)}), f32[8,128,4,128]{3,2,1,0:T(4,128)}, u32[]{:S(2)}, u32[]{:S(2)}) async-start(f32[8,128,4,128]{3,2,1,0:T(4,128)} %bitcast.2), calls=%async_computation | async-start | bytes 4194304 | tf_op jit(solution)/shard_map/all_to_all | solution.py:583
  53.6 21.1 %collective-permute-start.7 = (s16[1040,128]{1,0:T(8,128)(2,1)S(1)}, s16[1040,128]{1,0:T(8,128)(2,1)S(1)}, u32[]{:S(2)}, u32[]{:S(2)}) collective-permute-start(s16[1040,128]{1,0:T(8,128)(2,1)S(1)} %get-tuple-element.28), channel_id=1, source_target_pairs={{0,1},{1,2},{2,3},{3,0},{4,5},{5,6},{6,7},{7,4},{8,9},{9,10},{10,1... | collective-permute-start | bytes 798728 | tf_op jit(solution)/shard_map/ppermute | solution.py:581
  55.5 19.2 %collective-permute-start.8 = (s16[1040,128]{1,0:T(8,128)(2,1)S(1)}, s16[1040,128]{1,0:T(8,128)(2,1)S(1)}, u32[]{:S(2)}, u32[]{:S(2)}) collective-permute-start(s16[1040,128]{1,0:T(8,128)(2,1)S(1)} %get-tuple-element.29), channel_id=1, source_target_pairs={{1,0},{2,1},{3,2},{0,3},{5,4},{6,5},{7,6},{4,7},{9,8},{10,9},{11,1... | collective-permute-start | bytes 798728 | tf_op jit(solution)/shard_map/ppermute | solution.py:582
